TPU v7x, 128 devices: a whole 4x4x4 slice. The times are simulated.
128 devices in a mesh: group: 4 (over x), bulk: 32 (over z, y, core).
Axes of the slice: x: 4, y: 4, z: 4, core: 2. Of those that a mesh axis runs over, the one named last changes fastest.
Arguments:
- rhs: float32 [512, 64, 128], P(('group', 'bulk')), may hold values from -90 to 90, as said below
- diag_tiles: float32 [512, 128, 128], P(('group', 'bulk')), may hold values from -0.06 to 0.06
- offdiag_blocks: float32 [512, 11, 128, 128], P(('group', 'bulk')), may hold values from -0.026 to 0.026
- coupling: float32 [256, 4, 128, 128], P(('group', 'bulk')), may hold values from -0.05 to 0.05, as said below
- col_index: int32 [512, 11], replicated, may hold values from 0 to 511, as said below
- load: int32 [512], replicated, may hold values from 3 to 11
- new_slot: int32 [512], replicated, may hold values from 0 to 511, as said below
Outputs:
- solution_out: float32 [512, 64, 128], P(('group', 'bulk'))
- residual_out: float32 [512, 64, 128], P(('group', 'bulk'))
Inputs may be any that keep to these rules, and one draw needn't show every extreme that they name: `rhs`: made of random entries times scales of the rows and of the columns. `coupling`: entry [d * 2 + k, h] is the transpose of entry [(h * 32 + d % 32) * 2 + k, d // 32]. `col_index`: for each part g and each tile position t, the column t of the 128 block rows of part g is a permutation of that part's slots g * 128 to (g + 1) * 128 - 1. Of the 44 entries of the 4 block rows of one device (slots d * 4 to (d + 1) * 4 - 1), at most 2 name slots of any one device, and exactly 2 name slots of some device. `new_slot`: A permutation. On every device exactly one block row moves, from a slot k with 2 <= k % 4; it stays in its part, goes from owner b to owner b XOR m, where m (1 to 31) is one number for the whole part, and takes the slot that the moving row of that device leaves.
All inputs are finite; a program needn't handle non-finite values.
Results may differ from a plain program's by a relative error of at most 0.0003.
Values sent between devices are 32-bit elements; how exact they have to be, the bound alone decides.
A program may use at most 64 MiB of HBM per device.

v0:
```python
import jax
import jax.numpy as jnp
from jax import lax
from jax.sharding import PartitionSpec as P

highest = lax.Precision.HIGHEST
diagonal_shift = 4.0


def from_partner(value, axis, bit):
    mask = 2**bit
    pairs = [(source, source ^ mask) for source in range(lax.axis_size(axis))]
    return lax.ppermute(value, axis, pairs)


def chol_apply(matrix, right):
    factor = jnp.linalg.cholesky(matrix)
    middle = lax.linalg.triangular_solve(factor, right, left_side=True, lower=True)
    return lax.linalg.triangular_solve(factor, middle, left_side=True, lower=True, transpose_a=True)


def global_gram(left, right):
    partial_gram = jnp.einsum("snt,smt->nm", left, right, precision=highest)
    total = lax.psum(partial_gram, ("group", "bulk"))
    return 0.5 * (total + total.T)


def operate(vectors, diag, masked, column_ids, coupling):
    row_count = vectors.shape[0]
    boundary_rows = coupling.shape[0]
    part_count = coupling.shape[1]
    group_rows = row_count * lax.axis_size("bulk")
    border = lax.all_gather(vectors[:boundary_rows], "group", axis=0, tiled=True)
    final_output = diagonal_shift * vectors + jnp.einsum(
        "rnj,rij->rni", vectors, diag, precision=highest
    )
    returned = jnp.einsum("rni,rkij->rknj", vectors, masked, precision=highest)
    flat_terms = returned.reshape((-1,) + vectors.shape[1:])
    panel = lax.all_gather(vectors, "bulk", axis=0, tiled=True)
    buffer = jax.ops.segment_sum(flat_terms, column_ids.reshape(-1), num_segments=group_rows)
    owed = lax.psum_scatter(buffer, "bulk", scatter_dimension=0, tiled=True)
    picked = panel[column_ids]
    final_output = (
        final_output + jnp.einsum("rknj,rkij->rni", picked, masked, precision=highest) + owed
    )
    border = border.reshape((part_count, boundary_rows) + vectors.shape[1:])
    crossed = jnp.einsum("khij,hknj->kni", coupling, border, precision=highest)
    return final_output.at[:boundary_rows].add(crossed)


def advance(state, diag, masked, column_ids, coupling, last_step):
    solution, resid, direction, gram_rr = state
    image = operate(direction, diag, masked, column_ids, coupling)
    gram_pq = global_gram(direction, image)
    alpha = chol_apply(gram_pq, gram_rr)
    solution = solution + jnp.einsum("mn,smt->snt", alpha, direction, precision=highest)
    resid = resid - jnp.einsum("mn,smt->snt", alpha, image, precision=highest)
    if not last_step:
        gram_new = global_gram(resid, resid)
        beta = chol_apply(gram_rr, gram_new)
        direction = resid + jnp.einsum("mn,smt->snt", beta, direction, precision=highest)
        gram_rr = gram_new
    return (solution, resid, direction, gram_rr)


def local(rhs, diag_tiles, offdiag_blocks, coupling, col_index, load, new_slot):
    row_count = rhs.shape[0]
    off_count = offdiag_blocks.shape[1]
    bulk_count = lax.axis_size("bulk")
    group_rows = row_count * bulk_count
    my_group = lax.axis_index("group")
    my_bulk = lax.axis_index("bulk")
    first_slot = (my_group * bulk_count + my_bulk) * row_count
    group_base = my_group * group_rows
    own_slots = first_slot + jnp.arange(row_count, dtype=jnp.int32)
    tile_ids = jnp.arange(off_count, dtype=jnp.int32)
    old_columns = col_index[own_slots] - group_base
    old_mask = (tile_ids[None, :] < load[own_slots][:, None]).astype(jnp.float32)
    old_masked = offdiag_blocks * old_mask[:, :, None, None]
    own_new = new_slot[own_slots]
    leaving = jnp.argmax((own_new != own_slots).astype(jnp.int32))
    target = own_new[leaving]
    target_bulk = target // row_count % bulk_count
    xor_mask = jnp.bitwise_xor(target_bulk, my_bulk)
    start_state = (jnp.zeros_like(rhs), rhs, rhs, global_gram(rhs, rhs))
    state = advance(start_state, diag_tiles, old_masked, old_columns, coupling, False)
    solution, resid, direction, gram_rr = state
    pieces = [
        offdiag_blocks[leaving],
        diag_tiles[leaving],
        solution[leaving],
        resid[leaving],
        direction[leaving],
    ]
    flat = jnp.concatenate([piece.reshape(-1) for piece in pieces])
    for bit_pos in range(bulk_count.bit_length() - 1):
        partner = from_partner(flat, "bulk", bit_pos)
        chosen = jnp.bitwise_and(jnp.right_shift(xor_mask, bit_pos), 1) == 1
        flat = jnp.where(chosen, partner, flat)
    outputs = []
    offset = 0
    for piece in pieces:
        outputs.append(flat[offset : offset + piece.size].reshape(piece.shape))
        offset = offset + piece.size
    moved_off = offdiag_blocks.at[leaving].set(outputs[0])
    moved_diag = diag_tiles.at[leaving].set(outputs[1])
    solution = solution.at[leaving].set(outputs[2])
    resid = resid.at[leaving].set(outputs[3])
    direction = direction.at[leaving].set(outputs[4])
    inverse = (
        jnp.zeros_like(new_slot).at[new_slot].set(jnp.arange(new_slot.shape[0], dtype=jnp.int32))
    )
    old_rows = inverse[own_slots]
    new_columns = new_slot[col_index[old_rows]] - group_base
    new_mask = (tile_ids[None, :] < load[old_rows][:, None]).astype(jnp.float32)
    new_masked = moved_off * new_mask[:, :, None, None]
    state = advance(
        (solution, resid, direction, gram_rr), moved_diag, new_masked, new_columns, coupling, True
    )
    return (state[0], state[1])


def solution(mesh):
    return jax.shard_map(
        local,
        mesh=mesh,
        in_specs=(
            P(("group", "bulk"), None, None),
            P(("group", "bulk"), None, None),
            P(("group", "bulk"), None, None, None),
            P(("group", "bulk"), None, None, None),
            P(),
            P(),
            P(),
        ),
        out_specs=(P(("group", "bulk"), None, None), P(("group", "bulk"), None, None)),
        check_vma=False,
    )
```

profile of v0, /device:TPU:1, one launch (start us, length us, event | category | flops | bytes accessed | tf_op | source)
XLA Modules:
  0.0 662.4 jit_solution(1041182074401895514)
XLA Ops:
  7.3 1.9 copy.86
  9.9 1.6 copy.40
  12.1 2.6 scatter_custom_fusion.1
  15.9 1.5 gather_fusion
  18.7 2.2 gather_fusion.5
  25.3 3.2 fusion.4
  28.5 2.5 broadcast.320.clone
  31.0 8.0 %scatter_fusion = f32[128,64,128]{2,1,0:T(8,128)} fusion(f32[128,64,128]{2,1,0:T(8,128)} %broadcast.320.clone, s32[44]{0:T(128)} %reshape.516, f32[44,64,128]{2,1,0:T(8,128)} %bitcast.222), kind=kCustom, calls=%fused_computation.9 | custom fusion | flops 360448 | bytes 4325552 | tf_op jit(solution)/shard_map/scatter-add | solution.py:40
  40.2 1.3 fusion.68
  45.5 13.0 %all_gather.13 = f32[8,64,128]{2,1,0:T(8,128)} all-gather(f32[2,64,128]{2,1,0:T(8,128)} %slice.208), channel_id=1, replica_groups=mesh['group'=4,'bulk'=32] {'group'}, dimensions={0}, use_global_device_ids=true | all-gather | bytes 327680 | tf_op jit(solution)/shard_map/all_gather | solution.py:33
  60.9 1.5 bitcast_dynamic-update-slice_fusion
  62.4 4.0 gather_fusion.1
  66.4 5.4 fusion.12
  71.8 71.6 %reduce-scatter.3.cloned.1.call-done = f32[4,64,128]{2,1,0:T(8,128)} async-done(((f32[128,64,128]{2,1,0:T(8,128)}), f32[4,64,128]{2,1,0:T(8,128)}) %reduce-scatter.3.cloned.1.call-update) | async-done | bytes 131088 | tf_op jit(solution)/shard_map/reduce_scatter | solution.py:41
  143.4 1.7 fusion.21
  145.1 1.6 fusion.29
  148.3 66.3 %all-reduce = (f32[64,64]{1,0:T(8,128)}, f32[64,64]{1,0:T(8,128)}) all-reduce(f32[64,64]{1,0:T(8,128)} %convolution_bitcast_fusion.11, f32[64,64]{1,0:T(8,128)} %convolution_bitcast_fusion.12), channel_id=1, replica_groups=mesh['group'=4,'bulk'=32] {'group','bulk'}, use_global_device_ids=true, to_apply=%region_5.7 | all-reduce | flops 8192 | bytes 65536 | tf_op jit(solution)/shard_map/psum | solution.py:24
  214.6 1.4 copy.45
  216.0 1.4 fusion.56
  217.4 1.4 copy.48
  218.9 1.5 copy.43
  220.3 1.4 fusion.61
  221.7 1.4 copy.44
  223.2 1.4 fusion.60
  224.5 7.2 %cholesky.59 = f32[64,64]{1,0:T(8,128)} custom-call(f32[64,64]{1,0:T(8,128)} %fusion.60), custom_call_target="Cholesky" | custom-call | tf_op jit(solution)/shard_map/jit(cholesky)/cholesky | solution.py:17
  233.2 2.1 fusion.36
  235.3 6.3 custom-call.13
  243.6 1.8 fusion.25
  246.3 1.4 fusion.55
  247.7 7.2 %cholesky.70 = f32[64,64]{1,0:T(8,128)} custom-call(f32[64,64]{1,0:T(8,128)} %fusion.55), custom_call_target="Cholesky" | custom-call | tf_op jit(solution)/shard_map/jit(cholesky)/cholesky | solution.py:17
  256.4 2.1 fusion.37
  258.5 6.3 custom-call.15
  264.8 1.8 convolution_bitcast_fusion.9
  266.6 63.0 %psum.30 = f32[64,64]{1,0:T(8,128)} all-reduce(f32[64,64]{1,0:T(8,128)} %convolution_bitcast_fusion.9), channel_id=1, replica_groups=mesh['group'=4,'bulk'=32] {'group','bulk'}, use_global_device_ids=true, to_apply=%region_8.12 | all-reduce | flops 4096 | bytes 32768 | tf_op jit(solution)/shard_map/psum | solution.py:24
  329.6 1.4 copy.49
  334.3 1.4 bitcast_dynamic-update-slice_fusion.3
  335.7 1.4 bitcast_dynamic-update-slice_fusion.2
  341.3 2.2 broadcast_select_fusion
  344.8 20.3 %collective-permute-done.1 = f32[221184]{0:T(1024)} collective-permute-done((f32[221184]{0:T(1024)}, f32[221184]{0:T(1024)}, u32[]{:S(2)}, u32[]{:S(2)}) %collective-permute-start.1) | collective-permute-done | bytes 884768 | tf_op jit(solution)/shard_map/ppermute | solution.py:13
  365.0 2.2 broadcast_select_fusion.1
  367.3 2.9 collective-permute-start.2
  370.2 19.2 %collective-permute-done.2 = f32[221184]{0:T(1024)} collective-permute-done((f32[221184]{0:T(1024)}, f32[221184]{0:T(1024)}, u32[]{:S(2)}, u32[]{:S(2)}) %collective-permute-start.2) | collective-permute-done | bytes 884768 | tf_op jit(solution)/shard_map/ppermute | solution.py:13
  389.4 2.2 broadcast_select_fusion.2
  392.7 18.7 %collective-permute-done.3 = f32[221184]{0:T(1024)} collective-permute-done((f32[221184]{0:T(1024)}, f32[221184]{0:T(1024)}, u32[]{:S(2)}, u32[]{:S(2)}) %collective-permute-start.3) | collective-permute-done | bytes 884768 | tf_op jit(solution)/shard_map/ppermute | solution.py:13
  411.4 2.2 broadcast_select_fusion.3
  413.6 2.3 collective-permute-start.4
  416.7 17.4 %collective-permute-done.4 = f32[221184]{0:T(1024)} collective-permute-done((f32[221184]{0:T(1024)}, f32[221184]{0:T(1024)}, u32[]{:S(2)}, u32[]{:S(2)}) %collective-permute-start.4) | collective-permute-done | bytes 884768 | tf_op jit(solution)/shard_map/ppermute | solution.py:13
  436.3 2.0 fusion.40
  441.4 1.4 and_reduce_fusion
  445.5 3.2 fusion
  448.6 2.5 broadcast.320
  451.1 7.8 %scatter_fusion.1 = f32[128,64,128]{2,1,0:T(8,128)} fusion(f32[128,64,128]{2,1,0:T(8,128)} %broadcast.320, s32[44]{0:T(128)S(1)} %broadcast_subtract_fusion.1, f32[44,64,128]{2,1,0:T(8,128)} %bitcast.223), kind=kCustom, calls=%fused_computation.11 | custom fusion | flops 360448 | bytes 4325552 | tf_op jit(solution)/shard_map/scatter-add | solution.py:40
  459.2 10.1 %all_gather.15 = f32[8,64,128]{2,1,0:T(8,128)} all-gather(f32[2,64,128]{2,1,0:T(8,128)S(1)} %slice.243), channel_id=1, replica_groups=mesh['group'=4,'bulk'=32] {'group'}, dimensions={0}, use_global_device_ids=true | all-gather | bytes 327680 | tf_op jit(solution)/shard_map/all_gather | solution.py:33
  469.3 2.1 fusion.35
  471.4 15.3 %all-gather.5.cloned.1.call-done = f32[128,64,128]{2,1,0:T(8,128)} async-done(((f32[4,64,128]{2,1,0:T(8,128)}), f32[128,64,128]{2,1,0:T(8,128)}) %all-gather.5.cloned.1.call-update) | async-done | bytes 4194320 | tf_op jit(solution)/shard_map/all_gather | solution.py:39
  486.8 4.0 gather_fusion.7
  490.8 5.4 fusion.15
  496.2 73.8 %reduce-scatter.5.cloned.1.call-done = f32[4,64,128]{2,1,0:T(8,128)} async-done(((f32[128,64,128]{2,1,0:T(8,128)}), f32[4,64,128]{2,1,0:T(8,128)}) %reduce-scatter.5.cloned.1.call-update) | async-done | bytes 131088 | tf_op jit(solution)/shard_map/reduce_scatter | solution.py:41
  570.0 1.7 fusion.19
  571.7 1.6 fusion.27
  573.6 66.0 %psum.31 = f32[64,64]{1,0:T(8,128)S(1)} all-reduce(f32[64,64]{1,0:T(8,128)S(1)} %convolution_bitcast_fusion.7), channel_id=1, replica_groups=mesh['group'=4,'bulk'=32] {'group','bulk'}, use_global_device_ids=true, to_apply=%region_13.17 | all-reduce | flops 4096 | bytes 32768 | tf_op jit(solution)/shard_map/psum | solution.py:24
  639.8 5.8 cholesky.81
  647.0 4.9 custom-call.17
  653.1 1.8 fusion.22
  (102 shorter events, 41.5 us)
Async XLA Ops:
  7.2 137.9 %copy-start = (f32[2,4,128,128]{3,2,1,0:T(8,128)S(1)}, f32[2,4,128,128]{3,2,1,0:T(8,128)}, u32[]{:S(2)}) copy-start(f32[2,4,128,128]{3,2,1,0:T(8,128)} %param.29) | copy-start | bytes 1572868
  7.2 18.1 %copy-start.3 = (f32[4,64,128]{2,1,0:T(8,128)S(1)}, f32[4,64,128]{2,1,0:T(8,128)}, u32[]{:S(2)}) copy-start(f32[4,64,128]{2,1,0:T(8,128)} %param.26) | copy-start | bytes 393220
  7.2 16.2 %copy-start.2 = (s32[512]{0:T(512)S(1)}, s32[512]{0:T(512)}, u32[]{:S(2)}) copy-start(s32[512]{0:T(512)} %param.31) | copy-start | bytes 6148
  7.2 4.3 copy-start.1
  7.2 55.2 %all-gather.3.cloned.1.call-start = ((), (), s32[]{:S(2)}) async-start(), calls=%async_computation.2 | async-start | bytes 4325376 | tf_op jit(solution)/shard_map/all_gather | solution.py:39
  7.3 1.9 copy-start.11
  9.9 133.6 %reduce-scatter.3.cloned.1.call-start = ((), (), s32[]{:S(2)}) async-start(), calls=%async_computation.3 | async-start | bytes 4325376 | tf_op jit(solution)/shard_map/reduce_scatter | solution.py:41
  39.0 447.8 %all-gather.5.cloned.1.call-start = ((), (), s32[]{:S(2)}) async-start(), calls=%async_computation.4 | async-start | bytes 4325376 | tf_op jit(solution)/shard_map/all_gather | solution.py:39
  71.8 266.4 %copy-start.13 = (s32[4]{0:T(128)S(1)}, s32[4]{0:T(128)}, u32[]{:S(2)}) copy-start(s32[4]{0:T(128)} %gather_fusion.3) | copy-start | bytes 52
  146.7 0.7 copy-start.7
  334.2 2.8 copy-start.4
  337.6 3.7 collective-permute-start
  343.5 21.5 %collective-permute-start.1 = (f32[221184]{0:T(1024)}, f32[221184]{0:T(1024)}, u32[]{:S(2)}, u32[]{:S(2)}) collective-permute-start(f32[221184]{0:T(1024)} %broadcast_select_fusion), channel_id=1, source_target_pairs={{0,2},{1,3},{2,0},{3,1},{4,6},{5,7},{6,4},{7,5},{8,10},{9,11},{10,... | collective-permute-start | bytes 2654216 | tf_op jit(solution)/shard_map/ppermute | solution.py:13
  367.2 48.7 %copy-start.14 = (s32[3]{0:T(128)S(1)}, s32[3]{0:T(128)}, u32[]{:S(2)}) copy-start(s32[3]{0:T(128)} %constant.237.clone.1) | copy-start | bytes 40
  367.3 49.5 %copy-start.8 = (f32[64,4,128]{2,0,1:T(8,128)S(1)}, f32[64,4,128]{2,0,1:T(8,128)}, u32[]{:S(2)}) copy-start(f32[64,4,128]{2,0,1:T(8,128)} %fusion.73) | copy-start | bytes 393220
  367.3 22.2 %collective-permute-start.2 = (f32[221184]{0:T(1024)}, f32[221184]{0:T(1024)}, u32[]{:S(2)}, u32[]{:S(2)}) collective-permute-start(f32[221184]{0:T(1024)} %broadcast_select_fusion.1), channel_id=1, source_target_pairs={{0,4},{1,5},{2,6},{3,7},{4,0},{5,1},{6,2},{7,3},{8,12},{9,13},{10,... | collective-permute-start | bytes 2654216 | tf_op jit(solution)/shard_map/ppermute | solution.py:13
  391.6 19.8 %collective-permute-start.3 = (f32[221184]{0:T(1024)}, f32[221184]{0:T(1024)}, u32[]{:S(2)}, u32[]{:S(2)}) collective-permute-start(f32[221184]{0:T(1024)} %broadcast_select_fusion.2), channel_id=1, source_target_pairs={{0,8},{1,9},{2,10},{3,11},{4,12},{5,13},{6,14},{7,15},{8,0},{9,1},... | collective-permute-start | bytes 2654216 | tf_op jit(solution)/shard_map/ppermute | solution.py:13
  392.7 47.8 %copy-start.12 = (s32[4,11,1]{1,0,2:T(4,128)S(1)}, s32[4,11,1]{1,0,2:T(4,128)}, u32[]{:S(2)}) copy-start(s32[4,11,1]{1,0,2:T(4,128)} %get-tuple-element.98) | copy-start | bytes 532
  413.6 20.5 %collective-permute-start.4 = (f32[221184]{0:T(1024)}, f32[221184]{0:T(1024)}, u32[]{:S(2)}, u32[]{:S(2)}) collective-permute-start(f32[221184]{0:T(1024)} %broadcast_select_fusion.3), channel_id=1, source_target_pairs={{0,16},{1,17},{2,18},{3,19},{4,20},{5,21},{6,22},{7,23},{8,24},{9,... | collective-permute-start | bytes 2654216 | tf_op jit(solution)/shard_map/ppermute | solution.py:13
  435.4 0.9 copy-start.6
  438.3 0.7 copy-start.9
  439.0 131.0 %reduce-scatter.5.cloned.1.call-start = ((), (), s32[]{:S(2)}) async-start(), calls=%async_computation.5 | async-start | bytes 4325376 | tf_op jit(solution)/shard_map/reduce_scatter | solution.py:41
  440.5 4.9 copy-start.5
  496.2 158.8 %copy-start.10 = (f32[4,64,128]{2,1,0:T(8,128)S(1)}, f32[4,64,128]{2,1,0:T(8,128)}, u32[]{:S(2)}) copy-start(f32[4,64,128]{2,1,0:T(8,128)} %copy-done.9) | copy-start | bytes 393220
Sparse Core Ops, SparseCore 0:
  10.3 49.7 all-gather.2
  63.7 79.6 reduce-scatter.2
  439.1 47.6 all-gather.4
  490.3 79.7 reduce-scatter.4
where the time goes:
time: 666 us; the launch traced here: 662 us
  waiting for transfers between devices  236 us (35%)
  blocking collectives  218 us (33%)
  other arithmetic  90.7 us (14%)
  local copies, waits for them, and re-layouts  50.3 us (8%)
  matrix products  39.5 us (6%)
  between operations  18.6 us (3%)
  starting transfers between devices  8.55 us (1%)
    psum x3, blocking collectives, global_gram(): total = lax.psum(partial_gram, ('group', 'bulk'))  195 us
    reduce_scatter x2, waiting for transfers between devices, operate(): owed = lax.psum_scatter(buffer, 'bulk', scatter_dimension=0, tiled=True)  145 us
    ppermute x5, waiting for transfers between devices, from_partner(): return lax.ppermute(value, axis, pairs)  75.6 us
    another operation x9, other arithmetic, chol_apply(): factor = jnp.linalg.cholesky(matrix)  23.9 us
    all_gather x2, blocking collectives, operate(): lax.all_gather(vectors[:boundary_rows], 'group', axis=0, tiled=True)  23.1 us
    another operation x6, other arithmetic, chol_apply(): lax.linalg.triangular_solve(factor, middle, left_side=True, lower=True, t...  22.2 us
    scatter-add x2, other arithmetic, operate(): jax.ops.segment_sum(flat_terms, column_ids.reshape(-1), num_segments=grou...  15.8 us
    all_gather x2, waiting for transfers between devices, operate(): panel = lax.all_gather(vectors, 'bulk', axis=0, tiled=True)  15.3 us
  transfers between devices with their start and end apart: 9, of which 7 were waited for; matrix products, arithmetic and copies ran while one was open for 12% of the time, Pallas kernels for 0%

commit v1 on v0

v1 whole, which is shorter than its diff:
```python
import jax
import jax.numpy as jnp
from jax import lax
from jax.sharding import PartitionSpec as P

highest = lax.Precision.HIGHEST
diagonal_shift = 4.0


def chol_apply(matrix, right):
    factor = jnp.linalg.cholesky(matrix)
    middle = lax.linalg.triangular_solve(factor, right, left_side=True, lower=True)
    return lax.linalg.triangular_solve(factor, middle, left_side=True, lower=True, transpose_a=True)


def gram(left, right):
    return jnp.einsum("snt,smt->nm", left, right, precision=highest)


def sym(m):
    return 0.5 * (m + m.T)


def mm(a, b):
    return jnp.dot(a, b, precision=highest)


def off_part(vectors, diag, masked, column_ids, coupling):
    boundary_rows = coupling.shape[0]
    part_count = coupling.shape[1]
    border = lax.all_gather(vectors[:boundary_rows], "group", axis=0, tiled=True)
    own = jnp.einsum("rnj,rij->rni", vectors, diag, precision=highest)
    returned = jnp.einsum("rni,rkij->rknj", vectors, masked, precision=highest)
    panel = lax.all_gather(vectors, "bulk", axis=0, tiled=True)
    picked = panel[column_ids]
    own = own + jnp.einsum("rknj,rkij->rni", picked, masked, precision=highest)
    border = border.reshape((part_count, boundary_rows) + vectors.shape[1:])
    crossed = jnp.einsum("khij,hknj->kni", coupling, border, precision=highest)
    return own.at[:boundary_rows].add(crossed), returned.reshape((-1,) + vectors.shape[1:]), panel


def coefficients(n0, n1, n2, n3):
    n = n0.shape[0]
    eye = jnp.eye(n, dtype=n0.dtype)
    n0, n1, n2, n3 = sym(n0), sym(n1), sym(n2), sym(n3)
    delta = chol_apply(diagonal_shift * n0 + n1, n1)
    alpha = (eye - delta) / diagonal_shift
    b = -alpha
    cross = mm(delta.T, mm(n1, b))
    gram_new = sym(mm(delta.T, mm(n0, delta)) + cross + cross.T + mm(b.T, mm(n2, b)))
    beta = chol_apply(n0, gram_new)
    a = delta + beta
    c1 = mm(a.T, mm(n1, b))
    c2 = mm(a.T, mm(n2, b))
    pp = mm(a.T, mm(n0, a)) + c1 + c1.T + mm(b.T, mm(n2, b))
    pep = mm(a.T, mm(n1, a)) + c2 + c2.T + mm(b.T, mm(n3, b))
    alpha2 = chol_apply(sym(diagonal_shift * pp + pep), gram_new)
    ba = mm(b, alpha2)
    aa = mm(a, alpha2)
    sol = (alpha + aa, ba)
    res = (delta - diagonal_shift * aa, b - diagonal_shift * ba - aa, -ba)
    return sol, res


def local(rhs, diag_tiles, offdiag_blocks, coupling, col_index, load, new_slot):
    row_count = rhs.shape[0]
    off_count = offdiag_blocks.shape[1]
    bulk_count = lax.axis_size("bulk")
    group_rows = row_count * bulk_count
    group_base = lax.axis_index("group") * group_rows
    first = lax.axis_index("bulk") * row_count
    cols = lax.dynamic_slice_in_dim(col_index, group_base, group_rows) - group_base
    moved = lax.dynamic_slice_in_dim(new_slot, group_base, group_rows) - group_base
    loads = lax.dynamic_slice_in_dim(load, group_base + first, row_count)
    my_cols = lax.dynamic_slice_in_dim(cols, first, row_count)
    my_new = lax.dynamic_slice_in_dim(moved, first, row_count)
    tile_ids = jnp.arange(off_count, dtype=jnp.int32)
    mask = (tile_ids[None, :] < loads[:, None]).astype(jnp.float32)
    masked = offdiag_blocks * mask[:, :, None, None]
    u0 = rhs
    own, returned, panel0 = off_part(u0, diag_tiles, masked, my_cols, coupling)
    buffer = jax.ops.segment_sum(returned, my_cols.reshape(-1), num_segments=group_rows)
    u1 = own + lax.psum_scatter(buffer, "bulk", scatter_dimension=0, tiled=True)
    own, returned, panel1 = off_part(u1, diag_tiles, masked, my_cols, coupling)
    ids = jnp.concatenate([moved[my_cols.reshape(-1)], my_new])
    buffer = jax.ops.segment_sum(
        jnp.concatenate([returned, own]), ids, num_segments=group_rows
    )
    u2 = lax.psum_scatter(buffer, "bulk", scatter_dimension=0, tiled=True)
    inverse = jnp.zeros_like(moved).at[moved].set(jnp.arange(group_rows, dtype=jnp.int32))
    mine = lax.dynamic_slice_in_dim(inverse, first, row_count)
    v0, v1 = panel0[mine], panel1[mine]
    grams = jnp.stack([gram(v0, v0), gram(v0, v1), gram(v1, v1), gram(v1, u2)])
    grams = lax.psum(grams, ("group", "bulk"))
    sol, res = coefficients(grams[0], grams[1], grams[2], grams[3])
    basis = jnp.concatenate([v0, v1, u2], axis=1)
    zero = jnp.zeros_like(sol[0])
    weights = jnp.concatenate(
        [jnp.concatenate(sol + (zero,), axis=0), jnp.concatenate(res, axis=0)], axis=1
    )
    out = jnp.einsum("mn,smt->snt", weights, basis, precision=highest)
    n = rhs.shape[1]
    return out[:, :n], out[:, n:]


def solution(mesh):
    return jax.shard_map(
        local,
        mesh=mesh,
        in_specs=(
            P(("group", "bulk"), None, None),
            P(("group", "bulk"), None, None),
            P(("group", "bulk"), None, None, None),
            P(("group", "bulk"), None, None, None),
            P(),
            P(),
            P(),
        ),
        out_specs=(P(("group", "bulk"), None, None), P(("group", "bulk"), None, None)),
        check_vma=False,
    )
```

time: 666 us -> 496 us (0.74)
  blocking collectives: 218 us -> 23.2 us
  waiting for transfers between devices: 236 us -> 343 us
  other arithmetic: 90.7 us -> 55.1 us
  local copies, waits for them, and re-layouts: 50.3 us -> 28.1 us
  matrix products: 39.5 us -> 30.5 us
  starting transfers between devices: 8.55 us -> 0.2 us
    psum x3 -> x0, blocking collectives: 195 us -> none  [global_gram(): total = lax.psum(partial_gram, ('group', 'bulk'))]
    psum x0 -> x1, waiting for transfers between devices: none -> 146 us  [local(): grams = lax.psum(grams, ('group', 'bulk'))]
    ppermute x5 -> x0, waiting for transfers between devices: 75.6 us -> none  [from_partner(): return lax.ppermute(value, axis, pairs)]
    all_gather x2, waiting for transfers between devices: 15.3 us -> 52.9 us  [off_part(): panel = lax.all_gather(vectors, 'bulk', axis=0, tiled=True)]
    unnamed x38 -> x21, local copies, waits for them, and re-layouts: 11.6 us -> 0.95 us
    select_n x10 -> x4, other arithmetic: 12 us -> 1.62 us  [the longest x1 0.78 us: off_part(): picked = panel[column_ids]]
    ppermute x5 -> x0, starting transfers between devices: 8.17 us -> none  [from_partner(): return lax.ppermute(value, axis, pairs)]
    dot_general x17 -> x29, matrix products: 34.2 us -> 29.1 us  [the longest x2 9.75 us: off_part(): own = own + jnp.einsum('rknj,rkij->rni', picked, masked, precision=highest)]
  transfers between devices with their start and end apart: 9 -> 5, of which waited for: 7 -> 5; matrix products, arithmetic and copies ran while one was open for 12% -> 9% of each run, Pallas kernels for 0% -> 0%
where the time goes in v1:
time: 496 us; the launch traced here: 495 us
  waiting for transfers between devices  343 us (69%)
  other arithmetic  55.1 us (11%)
  matrix products  30.5 us (6%)
  local copies, waits for them, and re-layouts  28.1 us (6%)
  blocking collectives  23.2 us (5%)
  between operations  14.3 us (3%)
    psum x1, waiting for transfers between devices, local(): grams = lax.psum(grams, ('group', 'bulk'))  146 us
    reduce_scatter x1, waiting for transfers between devices, local(): u2 = lax.psum_scatter(buffer, 'bulk', scatter_dimension=0, tiled=True)  72.1 us
    reduce_scatter x1, waiting for transfers between devices, local(): u1 = own + lax.psum_scatter(buffer, 'bulk', scatter_dimension=0, tiled=True)  71 us
    all_gather x2, waiting for transfers between devices, off_part(): panel = lax.all_gather(vectors, 'bulk', axis=0, tiled=True)  52.9 us
    all_gather x2, blocking collectives, off_part(): lax.all_gather(vectors[:boundary_rows], 'group', axis=0, tiled=True)  23.2 us
    another operation x9, other arithmetic, chol_apply(): factor = jnp.linalg.cholesky(matrix)  19.6 us
    another operation x6, other arithmetic, chol_apply(): lax.linalg.triangular_solve(factor, middle, left_side=True, lower=True, t...  16.6 us
  transfers between devices with their start and end apart: 5, of which 5 were waited for; matrix products, arithmetic and copies ran while one was open for 9% of the time, Pallas kernels for 0%

profile of v1, /device:TPU:1, one launch (start us, length us, event | category | flops | bytes accessed | tf_op | source)
XLA Modules:
  0.0 494.6 jit_solution(10182201475086260046)
XLA Ops:
  7.2 0.7 all-gather.3.cloned.1.call-update
  8.0 0.8 compare_select_fusion
  8.9 0.8 dynamic_slice.22
  9.8 3.8 fusion.4
  13.5 2.5 broadcast.140.clone
  16.0 6.9 %scatter_fusion = f32[128,64,128]{2,1,0:T(8,128)} fusion(f32[128,64,128]{2,1,0:T(8,128)} %broadcast.140.clone, s32[44]{0:T(128)S(1)} %reshape.206, f32[44,64,128]{2,1,0:T(8,128)S(1)} %bitcast.248), kind=kCustom, calls=%fused_computation.6 | custom fusion | flops 360448 | bytes 4325552 | tf_op jit(solution)/shard_map/scatter-add | solution.py:82
  23.0 0.8 copy-done.4
  23.8 0.6 slice.81
  24.5 0.7 copy.72
  25.1 0.8 reshape.166
  25.9 12.6 %all_gather.13 = f32[8,64,128]{2,1,0:T(8,128)} all-gather(f32[2,64,128]{2,1,0:T(8,128)} %slice.81), channel_id=1, replica_groups=mesh['group'=4,'bulk'=32] {'group'}, dimensions={0}, use_global_device_ids=true | all-gather | bytes 327680 | tf_op jit(solution)/shard_map/all_gather | solution.py:31
  38.5 21.5 %all-gather.3.cloned.1.call-done = f32[128,64,128]{2,1,0:T(8,128)} async-done(((f32[4,64,128]{2,1,0:T(8,128)}), f32[128,64,128]{2,1,0:T(8,128)}) %all-gather.3.cloned.1.call-update) | async-done | bytes 4194320 | tf_op jit(solution)/shard_map/all_gather | solution.py:34
  60.1 4.0 gather_fusion.1
  64.1 4.8 fusion.12
  68.9 1.3 convolution_add_fusion.1
  70.2 2.1 fusion.21
  72.4 71.0 %reduce-scatter.3.cloned.1.call-done = f32[4,64,128]{2,1,0:T(8,128)} async-done(((f32[128,64,128]{2,1,0:T(8,128)}), f32[4,64,128]{2,1,0:T(8,128)}) %reduce-scatter.3.cloned.1.call-update) | async-done | bytes 131088 | tf_op jit(solution)/shard_map/reduce_scatter | solution.py:83
  143.4 1.6 add.181
  145.2 0.8 compare_select_fusion.3
  146.0 0.8 gather_fusion.3
  146.9 0.8 slice.102
  147.7 10.6 %all_gather.15 = f32[8,64,128]{2,1,0:T(8,128)} all-gather(f32[2,64,128]{2,1,0:T(8,128)S(1)} %slice.102), channel_id=1, replica_groups=mesh['group'=4,'bulk'=32] {'group'}, dimensions={0}, use_global_device_ids=true | all-gather | bytes 327680 | tf_op jit(solution)/shard_map/all_gather | solution.py:31
  158.3 4.1 fusion.2
  162.4 31.4 %all-gather.5.cloned.1.call-done = f32[128,64,128]{2,1,0:T(8,128)} async-done(((f32[4,64,128]{2,1,0:T(8,128)}), f32[128,64,128]{2,1,0:T(8,128)}) %all-gather.5.cloned.1.call-update) | async-done | bytes 4194320 | tf_op jit(solution)/shard_map/all_gather | solution.py:34
  193.8 3.9 gather_fusion.4
  197.7 4.9 fusion.15
  202.7 0.6 convolution_add_fusion
  203.3 0.7 fusion.19
  204.1 2.5 broadcast.140
  206.6 6.9 %scatter_fusion.1 = f32[128,64,128]{2,1,0:T(8,128)} fusion(f32[128,64,128]{2,1,0:T(8,128)} %broadcast.140, s32[48]{0:T(128)S(1)} %pad_add_fusion, f32[48,64,128]{2,1,0:T(8,128)S(1)} %pad_maximum_fusion), kind=kCustom, calls=%fused_computation.7 | custom fusion | flops 393216 | bytes 4718784 | tf_op jit(solution)/shard_map/scatter-add | solution.py:86
  213.6 1.2 scatter_custom_fusion
  214.9 2.7 gather_fusion
  217.6 0.3 convolution_bitcast_fusion.6
  217.9 2.7 gather_fusion.2
  220.7 0.3 convolution_bitcast_fusion.4
  220.9 0.3 convolution_bitcast_fusion.5
  221.2 72.1 %reduce-scatter.5.cloned.1.call-done = f32[4,64,128]{2,1,0:T(8,128)} async-done(((f32[128,64,128]{2,1,0:T(8,128)}), f32[4,64,128]{2,1,0:T(8,128)}) %reduce-scatter.5.cloned.1.call-update) | async-done | bytes 131088 | tf_op jit(solution)/shard_map/reduce_scatter | solution.py:89
  293.3 1.2 convolution_bitcast_fusion.3
  294.5 0.7 pad_maximum_fusion.1
  295.2 146.3 %all-reduce.2.cloned.1.call-done = f32[4,64,64]{2,1,0:T(8,128)} async-done(((f32[4,64,64]{2,1,0:T(8,128)}), f32[4,64,64]{2,1,0:T(8,128)}) %all-reduce.2.cloned.1.call-update) | async-done | bytes 65552 | tf_op jit(solution)/shard_map/psum | solution.py:94
  441.5 0.8 slice_bitcast_fusion.2
  442.5 0.8 multiply_add_fusion
  443.6 5.9 %cholesky.59 = f32[64,64]{1,0:T(8,128)S(1)} custom-call(f32[64,64]{1,0:T(8,128)S(1)} %copy.82), custom_call_target="Cholesky" | custom-call | tf_op jit(solution)/shard_map/jit(cholesky)/cholesky | solution.py:11
  449.5 0.6 compare_reduce_fusion.2
  450.1 0.7 fusion.41
  450.8 4.9 custom-call.13
  455.7 0.3 fusion.74
  455.9 0.2 fusion.76
  456.7 5.9 %cholesky.70 = f32[64,64]{1,0:T(8,128)S(1)} custom-call(f32[64,64]{1,0:T(8,128)S(1)} %copy.85), custom_call_target="Cholesky" | custom-call | tf_op jit(solution)/shard_map/jit(cholesky)/cholesky | solution.py:11
  462.6 0.6 compare_reduce_fusion.1
  463.2 0.7 fusion.42
  463.9 4.9 custom-call.15
  468.8 1.0 fusion.67
  470.8 0.2 convolution_add_fusion.2
  471.8 1.0 fusion.45
  473.9 5.8 %cholesky.81 = f32[64,64]{1,0:T(8,128)S(1)} custom-call(f32[64,64]{1,0:T(8,128)S(1)} %fusion.51), custom_call_target="Cholesky" | custom-call | tf_op jit(solution)/shard_map/jit(cholesky)/cholesky | solution.py:11
  479.8 0.6 compare_reduce_fusion
  480.4 0.7 fusion.43
  481.1 4.9 custom-call.17
  486.0 0.2 fusion.47
  486.4 0.2 fusion.92
  486.7 0.2 fusion.81
  486.9 0.4 convolution_bitcast_fusion
  487.4 0.7 fusion.103
  (80 shorter events, 4.9 us)
Async XLA Ops:
  7.2 63.1 %copy-start = (f32[2,4,128,128]{3,2,1,0:T(8,128)S(1)}, f32[2,4,128,128]{3,2,1,0:T(8,128)}, u32[]{:S(2)}) copy-start(f32[2,4,128,128]{3,2,1,0:T(8,128)} %param.19) | copy-start | bytes 1572868
  7.2 52.9 %all-gather.3.cloned.1.call-start = ((), (), s32[]{:S(2)}) async-start(), calls=%async_computation.2 | async-start | bytes 4325376 | tf_op jit(solution)/shard_map/all_gather | solution.py:34
  7.9 135.5 %reduce-scatter.3.cloned.1.call-start = ((), (), s32[]{:S(2)}) async-start(), calls=%async_computation.3 | async-start | bytes 4325376 | tf_op jit(solution)/shard_map/reduce_scatter | solution.py:83
  22.9 0.9 copy-start.4
  22.9 41.2 %copy-start.1 = (f32[4,11,128,128]{3,2,1,0:T(8,128)S(1)}, f32[4,11,128,128]{3,2,1,0:T(8,128)}, u32[]{:S(2)}) copy-start(f32[4,11,128,128]{3,2,1,0:T(8,128)} %param.18) | copy-start | bytes 8650756
  22.9 170.8 %all-gather.5.cloned.1.call-start = ((), (), s32[]{:S(2)}) async-start(), calls=%async_computation.4 | async-start | bytes 4325376 | tf_op jit(solution)/shard_map/all_gather | solution.py:34
  64.1 4.8 copy-start.7
  64.1 6.1 %copy-start.6 = (f32[8,64,128]{2,1,0:T(8,128)S(1)}, f32[8,64,128]{2,1,0:T(8,128)}, u32[]{:S(2)}) copy-start(f32[8,64,128]{2,1,0:T(8,128)} %all_gather.13) | copy-start | bytes 786436
  145.1 148.3 %reduce-scatter.5.cloned.1.call-start = ((), (), s32[]{:S(2)}) async-start(), calls=%async_computation.5 | async-start | bytes 4325376 | tf_op jit(solution)/shard_map/reduce_scatter | solution.py:89
  197.7 4.9 copy-start.3
  197.7 4.9 %copy-start.8 = (f32[4,128,128]{2,1,0:T(8,128)S(1)}, f32[4,128,128]{2,1,0:T(8,128)}, u32[]{:S(2)}) copy-start(f32[4,128,128]{2,1,0:T(8,128)} %param.17) | copy-start | bytes 786436
  197.7 5.6 %copy-start.5 = (f32[8,64,128]{2,1,0:T(8,128)S(1)}, f32[8,64,128]{2,1,0:T(8,128)}, u32[]{:S(2)}) copy-start(f32[8,64,128]{2,1,0:T(8,128)} %all_gather.15) | copy-start | bytes 786436
  197.7 6.2 %copy-start.2 = (f32[4,11,128,64]{2,3,1,0:T(8,128)S(1)}, f32[4,11,128,64]{2,3,1,0:T(8,128)}, u32[]{:S(2)}) copy-start(f32[4,11,128,64]{2,3,1,0:T(8,128)} %fusion.2) | copy-start | bytes 4325380
  213.5 228.0 %all-reduce.2.cloned.1.call-start = ((), (), s32[]{:S(2)}) async-start(), calls=%async_computation.6 | async-start | bytes 262144 | tf_op jit(solution)/shard_map/psum | solution.py:94
  294.5 192.4 %copy-start.9 = (f32[4,64,128]{2,1,0:T(8,128)S(1)}, f32[4,64,128]{2,1,0:T(8,128)}, u32[]{:S(2)}) copy-start(f32[4,64,128]{2,1,0:T(8,128)} %reduce-scatter.5.cloned.1.call-done) | copy-start | bytes 393220
Sparse Core Ops, SparseCore 0:
  10.2 49.7 all-gather.2
  63.7 79.6 reduce-scatter.2
  146.2 47.5 all-gather.4
  213.7 79.6 reduce-scatter.4
  298.5 142.9 all-reduce.1

commit v2 on v1

v2 whole, which is shorter than its diff:
```python
import functools

import jax
import jax.numpy as jnp
from jax import lax
from jax.experimental import pallas as pl
from jax.experimental.pallas import tpu as pltpu
from jax.sharding import PartitionSpec as P

highest = lax.Precision.HIGHEST
shift = 4.0
f32 = jnp.float32
bf16 = jnp.bfloat16
RING = 4
MESH = pl.DeviceIdType.MESH


class Net:
    def __init__(self, send, recv):
        self.g = lax.axis_index("group")
        b = lax.axis_index("bulk")
        self.c = lax.rem(b, 2)
        self.y = lax.rem(b // 2, RING)
        self.z = b // (2 * RING)
        self.send, self.recv = send, recv
        self.count = 0
        self.pending = []

    def device(self, dx=0, dy=0, dz=0, partner=False):
        c = 1 - self.c if partner else self.c
        y = lax.rem(self.y + dy, RING)
        z = lax.rem(self.z + dz, RING)
        return (lax.rem(self.g + dx, RING), (z * RING + y) * 2 + c)

    def copy(self, src, dst, device):
        i = self.count
        self.count += 1
        d = pltpu.make_async_remote_copy(
            src_ref=src,
            dst_ref=dst,
            send_sem=self.send.at[i],
            recv_sem=self.recv.at[i],
            device_id=device,
            device_id_type=MESH,
        )
        d.start()
        self.pending.append(d)
        return d

    def drain(self):
        for d in self.pending:
            d.wait_send()


def plus(a, k):
    return lax.rem(a + k, RING)


def greet(net, devices):
    barrier = pltpu.get_barrier_semaphore()
    for d in devices:
        pl.semaphore_signal(barrier, inc=1, device_id=d, device_id_type=MESH)
    pl.semaphore_wait(barrier, len(devices))


def gather_steps(net, j, u, panel, local_sem):
    c, y, z = net.c, net.y, net.z
    f0, s0 = (y, z) if j == 0 else (z, y)

    def unit(fi, si):
        return panel.at[c, j, si, fi] if j == 0 else panel.at[c, j, fi, si]

    def column(si):
        return panel.at[c, j, si] if j == 0 else panel.at[c, j, :, si]

    def to(df, ds):
        return net.device(dy=df, dz=ds) if j == 0 else net.device(dy=ds, dz=df)

    partner = net.device(partner=True)
    mine = unit(f0, s0)
    own = pltpu.make_async_copy(u.at[j], mine, local_sem)
    own.start()
    up = net.copy(u.at[j], mine, to(1, 0))
    down = net.copy(u.at[j], mine, to(3, 0))
    ups = [net.copy(u.at[j], mine, to(0, 1))]
    downs = [net.copy(u.at[j], mine, to(0, 3))]
    lo, hi = pl.ds(0, 2), pl.ds(2, 2)

    def pass_on(piece):
        ups.append(net.copy(piece, piece, to(0, 1)))
        downs.append(net.copy(piece, piece, to(0, 3)))

    yield
    up.wait_recv()
    piece = unit(plus(f0, 3), s0)
    up2 = net.copy(piece.at[lo], piece.at[lo], to(1, 0))
    pass_on(piece)
    yield
    down.wait_recv()
    piece = unit(plus(f0, 1), s0)
    down2 = net.copy(piece.at[hi], piece.at[hi], to(3, 0))
    pass_on(piece)
    order = [f0, plus(f0, 3), plus(f0, 1), plus(f0, 2)]
    ups2, downs2 = [], []
    for p in range(4):
        if p == 1:
            yield
            up2.wait_recv()
            down2.wait_recv()
            pass_on(unit(plus(f0, 2), s0))
            own.wait()
            exchanged = [net.copy(column(s0), column(s0), partner)]
        yield
        ups[p].wait_recv()
        piece = unit(order[p], plus(s0, 3))
        ups2.append(net.copy(piece.at[lo], piece.at[lo], to(0, 1)))
        yield
        downs[p].wait_recv()
        piece = unit(order[p], plus(s0, 1))
        downs2.append(net.copy(piece.at[hi], piece.at[hi], to(0, 3)))
    for k in (3, 1):
        exchanged.append(net.copy(column(plus(s0, k)), column(plus(s0, k)), partner))
    for d in ups2 + downs2:
        yield
        d.wait_recv()
    exchanged.append(net.copy(column(plus(s0, 2)), column(plus(s0, 2)), partner))
    for d in exchanged:
        yield
        d.wait_recv()


def scatter_steps(net, j, buf, owed, r, t0, t1, t2, t3, t4):
    c, y, z = net.c, net.y, net.z
    f0, s0 = (y, z) if j == 0 else (z, y)

    def column(ref, si):
        return ref.at[j, si] if j == 0 else ref.at[j, :, si]

    def to(df, ds):
        return net.device(dy=df, dz=ds) if j == 0 else net.device(dy=ds, dz=df)

    partner = net.device(partner=True)
    lo, hi = pl.ds(0, 2), pl.ds(2, 2)
    first = {}
    for k in (2, 1, 3, 0):
        si = plus(s0, k)
        src = buf.at[1 - c]
        first[k] = net.copy(column(src, si), column(t0, si), partner)
    cols = {k: column(r, plus(s0, k)) for k in range(4)}

    def start(k):
        si = plus(s0, k)
        a, b = column(buf.at[c], si), column(t0, si)
        for fi in range(RING):
            cols[k][fi] = a[fi] + b[fi]

    yield
    first[2].wait_recv()
    start(2)
    up = net.copy(cols[2].at[:, lo], t1.at[j, 0], to(0, 1))
    down = net.copy(cols[2].at[:, hi], t1.at[j, 1], to(0, 3))
    yield
    first[1].wait_recv()
    start(1)
    yield
    first[3].wait_recv()
    start(3)
    yield
    up.wait_recv()
    for fi in range(RING):
        cols[1][fi, lo] = cols[1][fi, lo] + t1[j, 0, fi]
    up2 = net.copy(cols[1], t2.at[j, 0], to(0, 1))
    yield
    down.wait_recv()
    for fi in range(RING):
        cols[3][fi, hi] = cols[3][fi, hi] + t1[j, 1, fi]
    down2 = net.copy(cols[3], t2.at[j, 1], to(0, 3))
    yield
    first[0].wait_recv()
    start(0)
    yield
    up2.wait_recv()
    down2.wait_recv()
    mine = cols[0]

    def add(k):
        fi = plus(f0, k)
        mine[fi] = mine[fi] + (t2[j, 0, fi] + t2[j, 1, fi])

    add(2)
    far = mine.at[plus(f0, 2)]
    up3 = net.copy(far.at[lo], t3.at[j, 0], to(1, 0))
    down3 = net.copy(far.at[hi], t3.at[j, 1], to(3, 0))
    add(1)
    add(3)
    add(0)
    yield
    up3.wait_recv()
    fi = plus(f0, 1)
    mine[fi, lo] = mine[fi, lo] + t3[j, 0]
    up4 = net.copy(mine.at[fi], t4.at[j, 0], to(1, 0))
    yield
    down3.wait_recv()
    fi = plus(f0, 3)
    mine[fi, hi] = mine[fi, hi] + t3[j, 1]
    down4 = net.copy(mine.at[fi], t4.at[j, 1], to(3, 0))
    yield
    up4.wait_recv()
    down4.wait_recv()
    owed[j] = mine[f0] + (t4[j, 0] + t4[j, 1])


def border_steps(net, u, border, local_sem):
    src = u.at[:, pl.ds(0, 2)]
    own = pltpu.make_async_copy(src, border.at[net.g], local_sem)
    own.start()
    sent = [net.copy(src, border.at[net.g], net.device(dx=k)) for k in (1, 3, 2)]
    yield
    own.wait()
    for d in sent:
        d.wait_recv()


def reduce_steps(net, m, out, acc, slots, halves):
    c = net.c
    rows = acc.shape[1]
    partner = net.device(partner=True)
    d = net.copy(m.at[pl.ds((1 - c) * rows, rows)], halves, partner)
    yield
    d.wait_recv()
    acc[0] = m[pl.ds(c * rows, rows)] + halves[...]
    for t in range(3):
        sent = []
        for k in (1, 3, 2):
            step = [0, 0, 0]
            step[t] = k * (1 - c)
            step[(t + 1) % 3] = step[(t + 1) % 3] + k * c
            sent.append(
                net.copy(acc.at[t], slots.at[t, k - 1], net.device(step[0], step[1], step[2]))
            )
        yield
        for d in sent:
            d.wait_recv()
        acc[t + 1] = (acc[t] + slots[t, 0]) + (slots[t, 1] + slots[t, 2])
    out[pl.ds(c * rows, rows)] = acc[3]
    d = net.copy(acc.at[3], out.at[pl.ds(c * rows, rows)], partner)
    yield
    d.wait_recv()


def run(steps):
    steps = list(steps)
    while steps:
        left = []
        for s in steps:
            try:
                next(s)
                left.append(s)
            except StopIteration:
                pass
        steps = left


def exchange_kernel(gather, scatter, reduce, *refs):
    refs = list(refs)
    u = refs.pop(0) if gather else None
    buf = refs.pop(0) if scatter else None
    m = refs.pop(0) if reduce else None
    panel = refs.pop(0) if gather else None
    border = refs.pop(0) if gather else None
    owed = refs.pop(0) if scatter else None
    total = refs.pop(0) if reduce else None
    parts = [refs.pop(0) for _ in range(6)] if scatter else None
    work = [refs.pop(0) for _ in range(3)] if reduce else None
    send, recv, local_sems = refs
    net = Net(send, recv)
    devices = [net.device(partner=True)]
    devices += [net.device(dy=k) for k in (1, 3)] + [net.device(dz=k) for k in (1, 3)]
    if gather or reduce:
        devices += [net.device(dx=k) for k in (1, 2, 3)]
    if reduce:
        devices += [net.device(dy=2), net.device(dz=2)]
    greet(net, devices)
    steps = []
    if reduce:
        steps.append(reduce_steps(net, m, total, *work))
    if scatter:
        steps += [scatter_steps(net, j, buf, owed, *parts) for j in range(2)]
    if gather:
        steps += [gather_steps(net, j, u, panel, local_sems.at[j]) for j in range(2)]
        steps.append(border_steps(net, u, border, local_sems.at[2]))
    run(steps)
    net.drain()


def exchange(u, buf, m, ident):
    gather, scatter, reduce = u is not None, buf is not None, m is not None
    n, w = (u if gather else buf).shape[-2:]
    ins = [a for a in (u, buf, m) if a is not None]
    outs, scratch = [], []
    copies = 0
    if gather:
        outs.append(jax.ShapeDtypeStruct((2, 2, RING, RING, 4, n, w), f32))
        outs.append(jax.ShapeDtypeStruct((RING, 2, 2, n, w), f32))
        copies += 2 * 24 + 3
    if scatter:
        outs.append(jax.ShapeDtypeStruct((2, 4, n, w), f32))
        scratch += [
            pltpu.VMEM((2, RING, RING, 4, n, w), f32),
            pltpu.VMEM((2, RING, RING, 4, n, w), f32),
            pltpu.VMEM((2, 2, RING, 2, n, w), f32),
            pltpu.VMEM((2, 2, RING, 4, n, w), f32),
            pltpu.VMEM((2, 2, 2, n, w), f32),
            pltpu.VMEM((2, 2, 4, n, w), f32),
        ]
        copies += 2 * 12
    if reduce:
        half = (m.shape[0] // 2, m.shape[1])
        outs.append(jax.ShapeDtypeStruct(m.shape, f32))
        scratch += [pltpu.VMEM((4,) + half, f32), pltpu.VMEM((3, 3) + half, f32), pltpu.VMEM(half, f32)]
        copies += 11
    scratch += [pltpu.SemaphoreType.DMA((copies,))] * 2 + [pltpu.SemaphoreType.DMA((3,))]
    vm = pl.BlockSpec(memory_space=pltpu.VMEM)
    return pl.pallas_call(
        functools.partial(exchange_kernel, gather, scatter, reduce),
        out_shape=outs,
        in_specs=[vm] * len(ins),
        out_specs=[vm] * len(outs),
        scratch_shapes=scratch,
        compiler_params=pltpu.CompilerParams(
            collective_id=ident, has_side_effects=True, vmem_limit_bytes=40 << 20
        ),
        name=f"exchange{ident}",
    )(*ins)


def split(a):
    top = a.astype(bf16)
    return top, (a - top.astype(f32)).astype(bf16)


def dot3(a, b, dims):
    dot = functools.partial(
        lax.dot_general, dimension_numbers=(dims, ((), ())), preferred_element_type=f32
    )
    return dot(a[0], b[0]) + (dot(a[0], b[1]) + dot(a[1], b[0]))


ROWS = ((1,), (1,))
COLS = ((1,), (0,))


def joined(ref, *idx):
    return jnp.concatenate([ref[idx[0], 0, idx[1]], ref[idx[0], 1, idx[1]]], axis=0)


def place(slot):
    return lax.rem(slot // 4, 2), (slot // 8) * 4 + lax.rem(slot, 4)


def fetch_tables(col_hbm, cols, sem):
    first = (lax.axis_index("group") * 32 + lax.axis_index("bulk")) * 4
    d = pltpu.make_async_copy(col_hbm.at[pl.ds(first, 4)], cols, sem)
    d.start()
    d.wait()
    return first


def returned_products(u, off, cols, load, first, base, buf, target):
    def zero(i, _):
        buf[0, 0, i] = jnp.zeros(buf.shape[3:], f32)
        buf[0, 1, i] = jnp.zeros(buf.shape[3:], f32)
        buf[1, 0, i] = jnp.zeros(buf.shape[3:], f32)
        buf[1, 1, i] = jnp.zeros(buf.shape[3:], f32)
        return 0

    lax.fori_loop(0, buf.shape[2], zero, 0)
    n = u.shape[2]

    def row(s, _):
        v = split(jnp.concatenate([u[0, s], u[1, s]], axis=0))
        for t in range(off.shape[1]):
            live = (t < load[first + s]).astype(f32)
            p = dot3(v, split(off[s, t]), COLS) * live
            c, i = place(target(cols[s, t]) - base)
            buf[c, 0, i] = buf[c, 0, i] + p[:n]
            buf[c, 1, i] = buf[c, 1, i] + p[n:]
        return 0

    lax.fori_loop(0, off.shape[0], row, 0)


def returned_kernel(col_hbm, load, u, off, buf, cols, sem):
    first = fetch_tables(col_hbm, cols, sem)
    base = lax.axis_index("group") * 128
    returned_products(u, off, cols, load, first, base, buf, lambda a: a)


def own_products(s, panel, border, u, diag, coup, off, cols, load, first, base):
    v = split(jnp.concatenate([u[0, s], u[1, s]], axis=0))
    rest = dot3(v, split(diag[s]), ROWS)
    tiles = jnp.zeros_like(rest)
    for t in range(off.shape[1]):
        live = (t < load[first + s]).astype(f32)
        c, i = place(cols[s, t] - base)
        tiles = tiles + dot3(split(joined(panel, c, i)), split(off[s, t]), ROWS) * live
    return tiles, rest


def crossed(s, border, coup):
    out = None
    for h in range(coup.shape[1]):
        v = split(jnp.concatenate([border[h, 0, s], border[h, 1, s]], axis=0))
        p = dot3(v, split(coup[s, h]), ROWS)
        out = p if out is None else out + p
    return out


def gram(a, b):
    return lax.dot_general(a, b, (ROWS, ((), ())), precision=highest, preferred_element_type=f32)


def first_kernel(col_hbm, load, panel, border, owed, u, diag, coup, off, u1, g, cols, cross, sem):
    first = fetch_tables(col_hbm, cols, sem)
    base = lax.axis_index("group") * 128
    n = u.shape[2]
    cross[...] = jnp.zeros_like(cross)
    for s in range(coup.shape[0]):
        cross[s] = crossed(s, border, coup)
    g[...] = jnp.zeros_like(g)

    def row(s, _):
        tiles, rest = own_products(s, panel, border, u, diag, coup, off, cols, load, first, base)
        w = tiles + rest + cross[s] + jnp.concatenate([owed[0, s], owed[1, s]], axis=0)
        u1[0, s] = w[:n]
        u1[1, s] = w[n:]
        x = jnp.concatenate([u[0, s], u[1, s], w], axis=0)
        g[...] += gram(x, x)
        return 0

    lax.fori_loop(0, off.shape[0], row, 0)


def second_kernel(col_hbm, load, moved, panel, border, u, diag, coup, off, buf, g, cols, cross, sem):
    first = fetch_tables(col_hbm, cols, sem)
    base = lax.axis_index("group") * 128
    n = u.shape[2]
    returned_products(u, off, cols, load, first, base, buf, lambda a: moved[a])
    cross[...] = jnp.zeros_like(cross)
    for s in range(coup.shape[0]):
        cross[s] = crossed(s, border, coup)

    def row(s, total):
        tiles, rest = own_products(s, panel, border, u, diag, coup, off, cols, load, first, base)
        rest = rest + cross[s]
        w = tiles + rest
        c, i = place(moved[first + s] - base)
        buf[c, 0, i] = buf[c, 0, i] + w[:n]
        buf[c, 1, i] = buf[c, 1, i] + w[n:]
        return total + gram(jnp.concatenate([u[0, s], u[1, s]], axis=0), w + tiles)

    total = lax.fori_loop(0, off.shape[0], row, jnp.zeros((2 * n, 2 * n), f32))
    g[...] = jnp.concatenate([total[:n], total[n:]], axis=1)


def last_kernel(moved, p0, p1, owed, weights, sol, res):
    first = (lax.axis_index("group") * 32 + lax.axis_index("bulk")) * 4
    base = lax.axis_index("group") * 128
    half = sol.shape[1]
    for s in range(sol.shape[0]):
        c, i = place(moved[first + s] - base)
        x = jnp.concatenate([joined(p0, c, i), joined(p1, c, i), owed[0, s], owed[1, s]], axis=0)
        out = lax.dot_general(
            weights[...], x, (COLS, ((), ())), precision=highest, preferred_element_type=f32
        )
        sol[s] = out[:half]
        res[s] = out[half:]


def chol_apply(matrix, right):
    factor = jnp.linalg.cholesky(matrix)
    middle = lax.linalg.triangular_solve(factor, right, left_side=True, lower=True)
    return lax.linalg.triangular_solve(factor, middle, left_side=True, lower=True, transpose_a=True)


def sym(m):
    return 0.5 * (m + m.T)


def mm(a, b):
    return jnp.dot(a, b, precision=highest)


def coefficients(n0, n1, n2, n3):
    n = n0.shape[0]
    eye = jnp.eye(n, dtype=n0.dtype)
    n0, n1, n2, n3 = sym(n0), sym(n1), sym(n2), sym(n3)
    delta = chol_apply(shift * n0 + n1, n1)
    alpha = (eye - delta) / shift
    b = -alpha
    cross = mm(delta.T, mm(n1, b))
    gram_new = sym(mm(delta.T, mm(n0, delta)) + cross + cross.T + mm(b.T, mm(n2, b)))
    beta = chol_apply(n0, gram_new)
    a = delta + beta
    c1 = mm(a.T, mm(n1, b))
    c2 = mm(a.T, mm(n2, b))
    pp = mm(a.T, mm(n0, a)) + c1 + c1.T + mm(b.T, mm(n2, b))
    pep = mm(a.T, mm(n1, a)) + c2 + c2.T + mm(b.T, mm(n3, b))
    alpha2 = chol_apply(sym(shift * pp + pep), gram_new)
    ba = mm(b, alpha2)
    aa = mm(a, alpha2)
    sol = (alpha + aa, ba, jnp.zeros_like(ba))
    res = (delta - shift * aa, b - shift * ba - aa, -ba)
    return jnp.concatenate(
        [jnp.concatenate(sol, axis=0), jnp.concatenate(res, axis=0)], axis=1
    ).T


def local(rhs, diag, off, coup, col_index, load, new_slot):
    rows, n2, w = rhs.shape
    n = n2 // 2
    offs = off.shape[1]
    vm = pl.BlockSpec(memory_space=pltpu.VMEM)
    sm = pl.BlockSpec(memory_space=pltpu.SMEM)
    anys = pl.BlockSpec(memory_space=pl.ANY)
    params = pltpu.CompilerParams(vmem_limit_bytes=40 << 20)
    tables = [pltpu.SMEM((rows, offs), jnp.int32)]
    cross = [pltpu.VMEM((rows, n2, w), f32)]
    sem = [pltpu.SemaphoreType.DMA(())]
    panel_shape = (2, 2, RING, RING, 4, n, w)
    flat = (2, 2, RING * RING * 4, n, w)
    row_shape = jax.ShapeDtypeStruct((2, rows, n, w), f32)
    u0 = rhs.reshape(rows, 2, n, w).transpose(1, 0, 2, 3)

    buf = pl.pallas_call(
        returned_kernel,
        out_shape=jax.ShapeDtypeStruct(flat, f32),
        in_specs=[anys, sm, vm, vm],
        out_specs=vm,
        scratch_shapes=tables + sem,
        compiler_params=params,
        name="returned",
    )(col_index, load, u0, off)
    p0, border0, owed = exchange(u0, buf.reshape(panel_shape), None, 0)
    u1, g01 = pl.pallas_call(
        first_kernel,
        out_shape=[row_shape, jax.ShapeDtypeStruct((2 * n2, 2 * n2), f32)],
        in_specs=[anys, sm] + [vm] * 7,
        out_specs=[vm, vm],
        scratch_shapes=tables + cross + sem,
        compiler_params=params,
        name="first",
    )(col_index, load, p0.reshape(flat), border0, owed, u0, diag, coup, off)
    p1, border1, g01 = exchange(u1, None, g01, 1)
    buf, g3 = pl.pallas_call(
        second_kernel,
        out_shape=[
            jax.ShapeDtypeStruct(flat, f32),
            jax.ShapeDtypeStruct((n, 2 * n2), f32),
        ],
        in_specs=[anys, sm, sm] + [vm] * 6,
        out_specs=[vm, vm],
        scratch_shapes=tables + cross + sem,
        compiler_params=params,
        name="second",
    )(col_index, load, new_slot, p1.reshape(flat), border1, u1, diag, coup, off)
    owed, g3 = exchange(None, buf.reshape(panel_shape), g3, 2)
    n3 = jnp.concatenate([g3[:, :n2], g3[:, n2:]], axis=0)
    weights = coefficients(g01[:n2, :n2], g01[:n2, n2:], g01[n2:, n2:], n3)
    sol, res = pl.pallas_call(
        last_kernel,
        out_shape=[jax.ShapeDtypeStruct(rhs.shape, f32)] * 2,
        in_specs=[sm] + [vm] * 4,
        out_specs=[vm, vm],
        compiler_params=params,
        name="last",
    )(new_slot, p0.reshape(flat), p1.reshape(flat), owed, weights)
    return sol, res


def solution(mesh):
    return jax.shard_map(
        local,
        mesh=mesh,
        in_specs=(
            P(("group", "bulk"), None, None),
            P(("group", "bulk"), None, None),
            P(("group", "bulk"), None, None, None),
            P(("group", "bulk"), None, None, None),
            P(),
            P(),
            P(),
        ),
        out_specs=(P(("group", "bulk"), None, None), P(("group", "bulk"), None, None)),
        check_vma=False,
    )
```

time: 496 us -> 171 us (0.34)
  waiting for transfers between devices: 343 us -> 0 us
  Pallas kernels: 0 us -> 118 us
  matrix products: 30.5 us -> 4.67 us
  blocking collectives: 23.2 us -> 0 us
  other arithmetic: 55.1 us -> 36.5 us
  local copies, waits for them, and re-layouts: 28.1 us -> 9.99 us
  between operations: 14.3 us -> 1.07 us
    psum x1 -> x0, waiting for transfers between devices: 146 us -> none  [local(): grams = lax.psum(grams, ('group', 'bulk'))]
    reduce_scatter x2 -> x0, waiting for transfers between devices: 143 us -> none  [the longest x1 72.1 us: local(): u2 = lax.psum_scatter(buffer, 'bulk', scatter_dimension=0, tiled=True)]
    pallas_call x0 -> x7, Pallas kernels: none -> 118 us  [the longest x3 98 us: exchange(): pl.pallas_call(functools.partial(exchange_kernel, gather, scatter, reduce...]
    all_gather x2 -> x0, waiting for transfers between devices: 52.9 us -> none  [off_part(): panel = lax.all_gather(vectors, 'bulk', axis=0, tiled=True)]
    dot_general x13 -> x0, matrix products: 24.6 us -> none  [the longest x2 9.75 us: off_part(): own = own + jnp.einsum('rknj,rkij->rni', picked, masked, precision=highest)]
    all_gather x2 -> x0, blocking collectives: 23.2 us -> none  [off_part(): lax.all_gather(vectors[:boundary_rows], 'group', axis=0, tiled=True)]
    gather x5 -> x0, local copies, waits for them, and re-layouts: 14.2 us -> none  [the longest x2 7.94 us: off_part(): picked = panel[column_ids]]
    scatter-add x2 -> x0, other arithmetic: 13.8 us -> none  [the longest x1 6.93 us: local(): jax.ops.segment_sum(jnp.concatenate([returned, own]), ids, num_segments=g...]
  transfers between devices with their start and end apart: 5 -> 0, of which waited for: 5 -> 0; matrix products, arithmetic and copies ran while one was open for 9% -> 0% of each run, Pallas kernels for 0% -> 0%
where the time goes in v2:
time: 171 us; the launch traced here: 170 us
  Pallas kernels  118 us (69%)
  other arithmetic  36.5 us (21%)
  local copies, waits for them, and re-layouts  9.99 us (6%)
  matrix products  4.67 us (3%)
    pallas_call x3, Pallas kernels, exchange(): pl.pallas_call(functools.partial(exchange_kernel, gather, scatter, reduce...  98 us
    another operation x9, other arithmetic, chol_apply(): factor = jnp.linalg.cholesky(matrix)  19.6 us
    another operation x6, other arithmetic, chol_apply(): lax.linalg.triangular_solve(factor, middle, left_side=True, lower=True, t...  16.6 us
    pallas_call x1, Pallas kernels, local(): pl.pallas_call(second_kernel, out_shape=[jax.ShapeDtypeStruct(flat, f32),...  8.55 us
    unnamed x23, local copies, waits for them, and re-layouts  7.78 us
    pallas_call x1, Pallas kernels, local(): pl.pallas_call(first_kernel, out_shape=[row_shape, jax.ShapeDtypeStruct((...  6.4 us

profile of v2, /device:TPU:1, one launch (start us, length us, event | category | flops | bytes accessed | tf_op | source)
XLA Modules:
  0.0 170.3 jit_solution(5164287853501890568)
XLA Ops:
  0.6 0.9 copy.58
  1.5 0.9 copy.33.col_hbm
  2.5 1.8 %copy-done = f32[4,11,128,128]{3,2,1,0:T(8,128)S(1)} copy-done((f32[4,11,128,128]{3,2,1,0:T(8,128)S(1)}, f32[4,11,128,128]{3,2,1,0:T(8,128)}, u32[]{:S(2)}) %copy-start) | copy-done | bytes 2883608
  4.3 0.7 copy-done.8
  5.0 3.2 %returned.1 = f32[2,2,64,32,128]{4,3,2,1,0:T(8,128)S(1)} custom-call(s32[512,11]{1,0:T(8,128)S(1)} %copy.33.col_hbm, s32[512]{0:T(512)S(1)} %copy-done.8, f32[2,4,32,128]{3,2,1,0:T(8,128)S(1)} %bitcast.168, f32[4,11,128,128]{3,2,1,0:T(8,128)S(1)} %copy-done), custom_call_target="tpu_custom_call" | custom-call | tf_op jit(solution)/shard_map/returned/pallas_call | solution.py:535
  8.2 41.5 %exchange0.1 = (f32[2,2,4,4,4,32,128]{6,5,4,3,2,1,0:T(8,128)S(1)}, f32[4,2,2,32,128]{4,3,2,1,0:T(8,128)S(1)}, f32[2,4,32,128]{3,2,1,0:T(8,128)S(1)}) custom-call(f32[2,4,32,128]{3,2,1,0:T(8,128)S(1)} %bitcast.169, f32[2,2,4,4,4,32,128]{6,5,4,3,2,1,0:T(8,128)S(1)} %bitcast.166), custom_call_target="tpu_custom_call" | custom-call | tf_op jit(solution)/shard_map/exchange0/pallas_call | solution.py:324
  49.8 6.4 %first.1 = (f32[2,4,32,128]{3,2,1,0:T(8,128)S(1)}, f32[128,128]{1,0:T(8,128)S(1)}) custom-call(s32[512,11]{1,0:T(8,128)S(1)} %copy.33.col_hbm, s32[512]{0:T(512)S(1)} %copy-done.9, f32[2,2,64,32,128]{4,3,2,1,0:T(8,128)S(1)} %bitcast.162, f32[4,2,2,32,128]{4,3,2,1,0:T(8,128)S(1)} %get-tuple-element.18.border, f32[2,4,32,128]{3,2,1,0:T(8,128)S(1)} %get-tuple-element.19.owed, ...), custom_call_target="tpu_custom_call" | custom-call | tf_op jit(solution)/shard_map/first/pallas_call | solution.py:545
  56.2 27.4 %exchange1.1 = (f32[2,2,4,4,4,32,128]{6,5,4,3,2,1,0:T(8,128)S(1)}, f32[4,2,2,32,128]{4,3,2,1,0:T(8,128)S(1)}, f32[128,128]{1,0:T(8,128)S(1)}) custom-call(f32[2,4,32,128]{3,2,1,0:T(8,128)S(1)} %get-tuple-element.20.refs_0_.u, f32[128,128]{1,0:T(8,128)S(1)} %get-tuple-element.21.refs_1_), custom_call_target="tpu_custom_call" | custom-call | tf_op jit(solution)/shard_map/exchange1/pallas_call | solution.py:324
  83.6 8.6 %second.1 = (f32[2,2,64,32,128]{4,3,2,1,0:T(8,128)S(1)}, f32[32,128]{1,0:T(8,128)S(1)}) custom-call(s32[512,11]{1,0:T(8,128)S(1)} %copy.33.col_hbm, s32[512]{0:T(512)S(1)} %copy-done.9, s32[512]{0:T(512)S(1)} %copy-done.10, f32[2,2,64,32,128]{4,3,2,1,0:T(8,128)S(1)} %bitcast.164, f32[4,2,2,32,128]{4,3,2,1,0:T(8,128)S(1)} %get-tuple-element.23.border, ...), custom_call_target="tpu_custom_call" | custom-call | tf_op jit(solution)/shard_map/second/pallas_call | solution.py:555
  92.2 29.1 %exchange2.1 = (f32[2,4,32,128]{3,2,1,0:T(8,128)S(1)}, f32[32,128]{1,0:T(8,128)S(1)}) custom-call(f32[2,2,4,4,4,32,128]{6,5,4,3,2,1,0:T(8,128)S(1)} %bitcast.167, f32[32,128]{1,0:T(8,128)S(1)} %get-tuple-element.25.refs_1_), custom_call_target="tpu_custom_call" | custom-call | tf_op jit(solution)/shard_map/exchange2/pallas_call | solution.py:324
  121.3 0.1 fusion.57
  121.4 0.1 copy.36
  121.5 0.1 copy.37
  121.6 0.1 multiply_add_fusion
  121.7 0.1 copy.39
  121.7 0.1 copy.38
  121.8 5.8 %cholesky.59 = f32[64,64]{1,0:T(8,128)S(1)} custom-call(f32[64,64]{1,0:T(8,128)S(1)} %get-tuple-element.42), custom_call_target="Cholesky" | custom-call | tf_op jit(solution)/shard_map/jit(cholesky)/cholesky | solution.py:481
  127.7 0.6 compare_reduce_fusion.2
  128.4 0.7 fusion
  129.0 4.9 %custom-call.13 = f32[1,64,64]{1,2,0:T(8,128)S(1)} custom-call(f32[1,64,64]{2,1,0:T(8,128)S(1)} %fusion), custom_call_target="InvertDiagBlocksLowerTriangular" | custom-call | tf_op jit(solution)/shard_map/triangular_solve/custom-call.2 | solution.py:483
  133.9 0.2 fusion.33
  134.2 0.2 fusion.35
  134.4 0.1 copy.42
  134.5 0.3 fusion.26
  134.8 0.2 fusion.51
  135.0 0.2 fusion.54
  135.2 0.2 fusion.61
  135.4 0.1 copy.41
  135.5 0.2 fusion.59
  135.7 0.2 fusion.60
  135.9 0.1 copy.43
  136.0 0.1 copy.40
  136.2 0.1 copy.51
  136.2 0.2 fusion.16
  136.5 0.2 fusion.48
  136.7 5.8 %cholesky.70 = f32[64,64]{1,0:T(8,128)S(1)} custom-call(f32[64,64]{1,0:T(8,128)S(1)} %get-tuple-element.41), custom_call_target="Cholesky" | custom-call | tf_op jit(solution)/shard_map/jit(cholesky)/cholesky | solution.py:481
  142.5 0.6 compare_reduce_fusion.1
  143.2 0.7 fusion.1
  143.9 4.9 %custom-call.15 = f32[1,64,64]{1,2,0:T(8,128)S(1)} custom-call(f32[1,64,64]{2,1,0:T(8,128)S(1)} %fusion.1), custom_call_target="InvertDiagBlocksLowerTriangular" | custom-call | tf_op jit(solution)/shard_map/triangular_solve/custom-call.2 | solution.py:483
  148.7 0.3 fusion.29
  149.0 0.2 convolution_add_fusion
  149.3 0.2 fusion.67
  149.4 0.1 copy.50
  149.5 0.2 fusion.65
  149.7 0.2 fusion.66
  149.9 0.2 fusion.64
  150.1 0.1 copy.47
  150.2 0.2 fusion.62
  150.4 0.2 fusion.63
  150.6 0.1 copy.52
  150.7 0.1 copy.49
  150.7 0.1 copy.46
  151.0 5.8 %cholesky.81 = f32[64,64]{1,0:T(8,128)S(1)} custom-call(f32[64,64]{1,0:T(8,128)S(1)} %fusion.7), custom_call_target="Cholesky" | custom-call | tf_op jit(solution)/shard_map/jit(cholesky)/cholesky | solution.py:481
  156.8 0.6 compare_reduce_fusion
  157.5 0.7 fusion.2
  158.1 4.9 %custom-call.17 = f32[1,64,64]{1,2,0:T(8,128)S(1)} custom-call(f32[1,64,64]{2,1,0:T(8,128)S(1)} %fusion.2), custom_call_target="InvertDiagBlocksLowerTriangular" | custom-call | tf_op jit(solution)/shard_map/triangular_solve/custom-call.2 | solution.py:483
  163.0 0.2 fusion.3
  163.3 0.2 fusion.5
  163.5 0.2 fusion.46
  163.7 0.2 fusion.39
  164.0 0.1 maximum_bitcast_fusion.weights
  164.1 2.2 %copy-done.3 = f32[2,2,4,4,4,32,128]{6,5,4,3,2,1,0:T(8,128)S(1)} copy-done((f32[2,2,4,4,4,32,128]{6,5,4,3,2,1,0:T(8,128)S(1)}, f32[2,2,4,4,4,32,128]{6,5,4,3,2,1,0:T(8,128)}, u32[]{:S(2)}) %copy-start.3) | copy-done | bytes 4194328
  166.3 2.2 %copy-done.5 = f32[2,2,4,4,4,32,128]{6,5,4,3,2,1,0:T(8,128)S(1)} copy-done((f32[2,2,4,4,4,32,128]{6,5,4,3,2,1,0:T(8,128)S(1)}, f32[2,2,4,4,4,32,128]{6,5,4,3,2,1,0:T(8,128)}, u32[]{:S(2)}) %copy-start.5) | copy-done | bytes 4194328
  168.5 1.8 %last.1 = (f32[4,64,128]{2,1,0:T(8,128)}, f32[4,64,128]{2,1,0:T(8,128)}) custom-call(s32[512]{0:T(512)S(1)} %copy-done.10, f32[2,2,64,32,128]{4,3,2,1,0:T(8,128)S(1)} %bitcast.163, f32[2,2,64,32,128]{4,3,2,1,0:T(8,128)S(1)} %bitcast.165, f32[2,4,32,128]{3,2,1,0:T(8,128)S(1)} %get-tuple-element.26.owed, f32[128,192]{1,0:T(8,128)S(1)} %maximum_bitcast_fusion.weights), custom_call_target="tpu_custom_call" | custom-call | tf_op jit(solution)/shard_map/last/pallas_call | solution.py:570
  (29 shorter events, 0.4 us)
Async XLA Ops:
  2.4 1.8 %copy-start = (f32[4,11,128,128]{3,2,1,0:T(8,128)S(1)}, f32[4,11,128,128]{3,2,1,0:T(8,128)}, u32[]{:S(2)}) copy-start(f32[4,11,128,128]{3,2,1,0:T(8,128)} %off.5) | copy-start | bytes 8650756
  4.3 0.7 copy-start.8
  4.9 44.8 %copy-start.1 = (f32[4,11,128,128]{3,2,1,0:T(8,128)S(1)}, f32[4,11,128,128]{3,2,1,0:T(8,128)}, u32[]{:S(2)}) copy-start(f32[4,11,128,128]{3,2,1,0:T(8,128)} %off.5) | copy-start | bytes 8650756
  5.0 44.8 %copy-start.6 = (f32[2,4,128,128]{3,2,1,0:T(8,128)S(1)}, f32[2,4,128,128]{3,2,1,0:T(8,128)}, u32[]{:S(2)}) copy-start(f32[2,4,128,128]{3,2,1,0:T(8,128)} %coup.3) | copy-start | bytes 1572868
  5.0 44.8 %copy-start.7 = (f32[4,128,128]{2,1,0:T(8,128)S(1)}, f32[4,128,128]{2,1,0:T(8,128)}, u32[]{:S(2)}) copy-start(f32[4,128,128]{2,1,0:T(8,128)} %diag.3) | copy-start | bytes 786436
  5.0 44.8 %copy-start.9 = (s32[512]{0:T(512)S(1)}, s32[512]{0:T(512)}, u32[]{:S(2)}) copy-start(s32[512]{0:T(512)} %load.5) | copy-start | bytes 6148
  49.7 6.5 %copy-start.2 = (f32[2,2,4,4,4,32,128]{6,5,4,3,2,1,0:T(8,128)}, f32[2,2,4,4,4,32,128]{6,5,4,3,2,1,0:T(8,128)S(1)}, u32[]{:S(2)}) copy-start(f32[2,2,4,4,4,32,128]{6,5,4,3,2,1,0:T(8,128)S(1)} %get-tuple-element.17) | copy-start | bytes 12582916
  49.7 33.9 %copy-start.10 = (s32[512]{0:T(512)S(1)}, s32[512]{0:T(512)}, u32[]{:S(2)}) copy-start(s32[512]{0:T(512)} %moved.3) | copy-start | bytes 6148
  83.6 8.6 %copy-start.4 = (f32[2,2,4,4,4,32,128]{6,5,4,3,2,1,0:T(8,128)}, f32[2,2,4,4,4,32,128]{6,5,4,3,2,1,0:T(8,128)S(1)}, u32[]{:S(2)}) copy-start(f32[2,2,4,4,4,32,128]{6,5,4,3,2,1,0:T(8,128)S(1)} %get-tuple-element.22) | copy-start | bytes 12582916
  164.1 2.2 %copy-start.3 = (f32[2,2,4,4,4,32,128]{6,5,4,3,2,1,0:T(8,128)S(1)}, f32[2,2,4,4,4,32,128]{6,5,4,3,2,1,0:T(8,128)}, u32[]{:S(2)}) copy-start(f32[2,2,4,4,4,32,128]{6,5,4,3,2,1,0:T(8,128)} %copy-done.2) | copy-start | bytes 12582916
  166.3 2.2 %copy-start.5 = (f32[2,2,4,4,4,32,128]{6,5,4,3,2,1,0:T(8,128)S(1)}, f32[2,2,4,4,4,32,128]{6,5,4,3,2,1,0:T(8,128)}, u32[]{:S(2)}) copy-start(f32[2,2,4,4,4,32,128]{6,5,4,3,2,1,0:T(8,128)} %copy-done.4) | copy-start | bytes 12582916

commit v3 on v2

--- a/solution.py
+++ b/solution.py
@@ -80,60 +80,68 @@
     mine = unit(f0, s0)
     own = pltpu.make_async_copy(u.at[j], mine, local_sem)
     own.start()
-    up = net.copy(u.at[j], mine, to(1, 0))
-    down = net.copy(u.at[j], mine, to(3, 0))
+    near = [net.copy(u.at[j], mine, to(k, 0)) for k in (1, 3)]
     ups = [net.copy(u.at[j], mine, to(0, 1))]
     downs = [net.copy(u.at[j], mine, to(0, 3))]
+    far = net.copy(u.at[j], mine, to(2, 0))
     lo, hi = pl.ds(0, 2), pl.ds(2, 2)
-
-    def pass_on(piece):
+    order = [f0, plus(f0, 3), plus(f0, 1), plus(f0, 2)]
+    halves = []
+
+    def pass_on(p):
+        piece = unit(order[p], s0)
         ups.append(net.copy(piece, piece, to(0, 1)))
         downs.append(net.copy(piece, piece, to(0, 3)))
 
-    yield
-    up.wait_recv()
-    piece = unit(plus(f0, 3), s0)
-    up2 = net.copy(piece.at[lo], piece.at[lo], to(1, 0))
-    pass_on(piece)
-    yield
-    down.wait_recv()
-    piece = unit(plus(f0, 1), s0)
-    down2 = net.copy(piece.at[hi], piece.at[hi], to(3, 0))
-    pass_on(piece)
-    order = [f0, plus(f0, 3), plus(f0, 1), plus(f0, 2)]
-    ups2, downs2 = [], []
-    for p in range(4):
-        if p == 1:
-            yield
-            up2.wait_recv()
-            down2.wait_recv()
-            pass_on(unit(plus(f0, 2), s0))
-            own.wait()
-            exchanged = [net.copy(column(s0), column(s0), partner)]
-        yield
+    def forward(p):
         ups[p].wait_recv()
-        piece = unit(order[p], plus(s0, 3))
-        ups2.append(net.copy(piece.at[lo], piece.at[lo], to(0, 1)))
-        yield
+        piece = unit(order[p], plus(s0, 3)).at[lo]
+        halves.append(net.copy(piece, piece, to(0, 1)))
         downs[p].wait_recv()
-        piece = unit(order[p], plus(s0, 1))
-        downs2.append(net.copy(piece.at[hi], piece.at[hi], to(0, 3)))
-    for k in (3, 1):
-        exchanged.append(net.copy(column(plus(s0, k)), column(plus(s0, k)), partner))
-    for d in ups2 + downs2:
-        yield
+        piece = unit(order[p], plus(s0, 1)).at[hi]
+        halves.append(net.copy(piece, piece, to(0, 3)))
+
+    def swap(k):
+        return net.copy(column(plus(s0, k)), column(plus(s0, k)), partner)
+
+    for p in (1, 2):
+        yield
+        near[p - 1].wait_recv()
+        pass_on(p)
+    yield
+    forward(0)
+    yield
+    far.wait_recv()
+    pass_on(3)
+    piece = unit(order[3], s0)
+    last = net.copy(piece, piece, to(0, 2))
+    own.wait()
+    swapped = [swap(0)]
+    for p in (1, 2):
+        yield
+        forward(p)
+    yield
+    ups[3].wait_recv()
+    swapped.append(swap(3))
+    yield
+    downs[3].wait_recv()
+    swapped.append(swap(1))
+    yield
+    for d in halves:
         d.wait_recv()
-    exchanged.append(net.copy(column(plus(s0, 2)), column(plus(s0, 2)), partner))
-    for d in exchanged:
+    last.wait_recv()
+    swapped.append(swap(2))
+    for d in swapped:
         yield
         d.wait_recv()
 
 
-def scatter_steps(net, j, buf, owed, r, t0, t1, t2, t3, t4):
+def scatter_steps(net, j, buf, owed, r, t0, t1, t2, t3):
     c, y, z = net.c, net.y, net.z
     f0, s0 = (y, z) if j == 0 else (z, y)
 
-    def column(ref, si):
+    def column(ref, k):
+        si = plus(s0, k)
         return ref.at[j, si] if j == 0 else ref.at[j, :, si]
 
     def to(df, ds):
@@ -141,24 +149,23 @@
 
     partner = net.device(partner=True)
     lo, hi = pl.ds(0, 2), pl.ds(2, 2)
+    order = [2, 1, 3, 0]
+    rows = {k: plus(f0, k) for k in range(RING)}
     first = {}
-    for k in (2, 1, 3, 0):
-        si = plus(s0, k)
-        src = buf.at[1 - c]
-        first[k] = net.copy(column(src, si), column(t0, si), partner)
-    cols = {k: column(r, plus(s0, k)) for k in range(4)}
+    for k in order:
+        first[k] = net.copy(column(buf.at[1 - c], k), column(t0, k), partner)
+    cols = {k: column(r, k) for k in range(RING)}
 
     def start(k):
-        si = plus(s0, k)
-        a, b = column(buf.at[c], si), column(t0, si)
-        for fi in range(RING):
-            cols[k][fi] = a[fi] + b[fi]
+        a, b = column(buf.at[c], k), column(t0, k)
+        for i in order:
+            cols[k][rows[i]] = a[rows[i]] + b[rows[i]]
 
     yield
     first[2].wait_recv()
     start(2)
-    up = net.copy(cols[2].at[:, lo], t1.at[j, 0], to(0, 1))
-    down = net.copy(cols[2].at[:, hi], t1.at[j, 1], to(0, 3))
+    ups = {i: net.copy(cols[2].at[rows[i], lo], t1.at[j, 0, rows[i]], to(0, 1)) for i in order}
+    downs = {i: net.copy(cols[2].at[rows[i], hi], t1.at[j, 1, rows[i]], to(0, 3)) for i in order}
     yield
     first[1].wait_recv()
     start(1)
@@ -166,48 +173,31 @@
     first[3].wait_recv()
     start(3)
     yield
-    up.wait_recv()
-    for fi in range(RING):
-        cols[1][fi, lo] = cols[1][fi, lo] + t1[j, 0, fi]
-    up2 = net.copy(cols[1], t2.at[j, 0], to(0, 1))
-    yield
-    down.wait_recv()
-    for fi in range(RING):
-        cols[3][fi, hi] = cols[3][fi, hi] + t1[j, 1, fi]
-    down2 = net.copy(cols[3], t2.at[j, 1], to(0, 3))
-    yield
     first[0].wait_recv()
     start(0)
-    yield
-    up2.wait_recv()
-    down2.wait_recv()
-    mine = cols[0]
-
-    def add(k):
-        fi = plus(f0, k)
-        mine[fi] = mine[fi] + (t2[j, 0, fi] + t2[j, 1, fi])
-
-    add(2)
-    far = mine.at[plus(f0, 2)]
-    up3 = net.copy(far.at[lo], t3.at[j, 0], to(1, 0))
-    down3 = net.copy(far.at[hi], t3.at[j, 1], to(3, 0))
-    add(1)
-    add(3)
-    add(0)
-    yield
-    up3.wait_recv()
-    fi = plus(f0, 1)
-    mine[fi, lo] = mine[fi, lo] + t3[j, 0]
-    up4 = net.copy(mine.at[fi], t4.at[j, 0], to(1, 0))
-    yield
-    down3.wait_recv()
-    fi = plus(f0, 3)
-    mine[fi, hi] = mine[fi, hi] + t3[j, 1]
-    down4 = net.copy(mine.at[fi], t4.at[j, 1], to(3, 0))
-    yield
-    up4.wait_recv()
-    down4.wait_recv()
-    owed[j] = mine[f0] + (t4[j, 0] + t4[j, 1])
+    ups2, downs2 = {}, {}
+    for i in order:
+        q = rows[i]
+        yield
+        ups[i].wait_recv()
+        cols[1][q, lo] = cols[1][q, lo] + t1[j, 0, q]
+        ups2[i] = net.copy(cols[1].at[q], t2.at[j, 0, q], to(0, 1))
+        downs[i].wait_recv()
+        cols[3][q, hi] = cols[3][q, hi] + t1[j, 1, q]
+        downs2[i] = net.copy(cols[3].at[q], t2.at[j, 1, q], to(0, 3))
+    sent = []
+    for i in order:
+        q = rows[i]
+        yield
+        ups2[i].wait_recv()
+        downs2[i].wait_recv()
+        cols[0][q] = cols[0][q] + (t2[j, 0, q] + t2[j, 1, q])
+        if i:
+            sent.append(net.copy(cols[0].at[q], t3.at[j, i - 1], to(i, 0)))
+    for d in sent:
+        yield
+        d.wait_recv()
+    owed[j] = (cols[0][rows[0]] + t3[j, 0]) + (t3[j, 1] + t3[j, 2])
 
 
 def border_steps(net, u, border, local_sem):
@@ -270,16 +260,14 @@
     border = refs.pop(0) if gather else None
     owed = refs.pop(0) if scatter else None
     total = refs.pop(0) if reduce else None
-    parts = [refs.pop(0) for _ in range(6)] if scatter else None
+    parts = [refs.pop(0) for _ in range(5)] if scatter else None
     work = [refs.pop(0) for _ in range(3)] if reduce else None
     send, recv, local_sems = refs
     net = Net(send, recv)
     devices = [net.device(partner=True)]
-    devices += [net.device(dy=k) for k in (1, 3)] + [net.device(dz=k) for k in (1, 3)]
+    devices += [net.device(dy=k) for k in (2, 1, 3)] + [net.device(dz=k) for k in (2, 1, 3)]
     if gather or reduce:
-        devices += [net.device(dx=k) for k in (1, 2, 3)]
-    if reduce:
-        devices += [net.device(dy=2), net.device(dz=2)]
+        devices += [net.device(dx=k) for k in (2, 1, 3)]
     greet(net, devices)
     steps = []
     if reduce:
@@ -295,7 +283,7 @@
 
 def exchange(u, buf, m, ident):
     gather, scatter, reduce = u is not None, buf is not None, m is not None
-    n, w = (u if gather else buf).shape[-2:]
+    n, w = (u if gather else buf if scatter else m).shape[-2:]
     ins = [a for a in (u, buf, m) if a is not None]
     outs, scratch = [], []
     copies = 0
@@ -310,10 +298,9 @@
             pltpu.VMEM((2, RING, RING, 4, n, w), f32),
             pltpu.VMEM((2, 2, RING, 2, n, w), f32),
             pltpu.VMEM((2, 2, RING, 4, n, w), f32),
-            pltpu.VMEM((2, 2, 2, n, w), f32),
-            pltpu.VMEM((2, 2, 4, n, w), f32),
+            pltpu.VMEM((2, 3, 4, n, w), f32),
         ]
-        copies += 2 * 12
+        copies += 2 * 23
     if reduce:
         half = (m.shape[0] // 2, m.shape[1])
         outs.append(jax.ShapeDtypeStruct(m.shape, f32))
@@ -463,57 +450,136 @@
     g[...] = jnp.concatenate([total[:n], total[n:]], axis=1)
 
 
-def last_kernel(moved, p0, p1, owed, weights, sol, res):
+def solve(m, r):
+    n = m.shape[0]
+    t = jnp.concatenate([m, r], axis=1)
+    blocks = [t[8 * i : 8 * i + 8] for i in range(n // 8)]
+    shape = blocks[0].shape
+    row_id = lax.broadcasted_iota(jnp.int32, shape, 0)
+    for b in range(n // 8):
+        piv = blocks[b]
+        rows = [jnp.broadcast_to(piv[i : i + 1], shape) for i in range(8)]
+        lanes = [jnp.broadcast_to(piv[:, 8 * b + i : 8 * b + i + 1], shape) for i in range(8)]
+        d = [[jnp.broadcast_to(lanes[q][i : i + 1], shape) for q in range(8)] for i in range(8)]
+        for i in range(8):
+            inv = 1.0 / d[i][i]
+            rows[i] = rows[i] * inv
+            for q in range(i + 1, 8):
+                d[i][q] = d[i][q] * inv
+            for k in range(8):
+                if k != i:
+                    factor = d[k][i]
+                    rows[k] = rows[k] - factor * rows[i]
+                    for q in range(i + 1, 8):
+                        d[k][q] = d[k][q] - factor * d[i][q]
+        new = rows[0]
+        for i in range(1, 8):
+            new = jnp.where(row_id == i, rows[i], new)
+        for k in range(n // 8):
+            if k != b:
+                acc = blocks[k]
+                for i in range(8):
+                    column = blocks[k][:, 8 * b + i : 8 * b + i + 1]
+                    acc = acc - jnp.broadcast_to(column, shape) * rows[i]
+                blocks[k] = acc
+        blocks[b] = new
+        yield
+    return jnp.concatenate(blocks, axis=0)[:, n:]
+
+
+def both(*solves):
+    out = [None] * len(solves)
+    left = list(range(len(solves)))
+    while left:
+        for i in list(left):
+            try:
+                next(solves[i])
+            except StopIteration as e:
+                out[i] = e.value
+                left.remove(i)
+        yield
+    return out
+
+
+def finish(steps):
+    while True:
+        try:
+            next(steps)
+        except StopIteration as e:
+            return e.value
+
+
+def mm(a, b):
+    return lax.dot_general(a, b, (COLS, ((), ())), precision=highest, preferred_element_type=f32)
+
+
+def tmm(a, b):
+    return lax.dot_general(
+        a, b, (((0,), (0,)), ((), ())), precision=highest, preferred_element_type=f32
+    )
+
+
+def first_coefficients(g):
+    n = g.shape[0] // 2
+    g = 0.5 * (g + g.T)
+    n0, n1, n2 = g[:n, :n], 0.5 * (g[:n, n:] + g[n:, :n]), g[n:, n:]
+    eye = (
+        lax.broadcasted_iota(jnp.int32, (n, n), 0) == lax.broadcasted_iota(jnp.int32, (n, n), 1)
+    ).astype(f32)
+    delta, inverse = yield from both(solve(shift * n0 + n1, n1), solve(n0, eye))
+    b = (delta - eye) * (1.0 / shift)
+    yield
+    n1b, n2b, n0d = mm(n1, b), mm(n2, b), mm(n0, delta)
+    yield
+    bb = tmm(b, n2b)
+    fresh = tmm(delta, n0d) + (tmm(delta, n1b) + tmm(n1b, delta)) + bb
+    yield
+    a = delta + mm(inverse, fresh)
+    yield
+    pp = tmm(a, mm(n0, a)) + (tmm(a, n1b) + tmm(n1b, a)) + bb
+    pep = tmm(a, mm(n1, a)) + (tmm(a, n2b) + tmm(n2b, a))
+    yield
+    return delta, a, fresh, shift * pp + pep
+
+
+def coefficient_kernel(g, g3, w):
+    n = g.shape[0] // 2
+    delta, a, fresh, known = finish(first_coefficients(g[...]))
+    n3 = jnp.concatenate([g3[:, :n], g3[:, n:]], axis=0)
+    eye = (
+        lax.broadcasted_iota(jnp.int32, (n, n), 0) == lax.broadcasted_iota(jnp.int32, (n, n), 1)
+    ).astype(f32)
+    b = (delta - eye) * (1.0 / shift)
+    n3b = mm(n3, b)
+    pq = known + 0.5 * (tmm(b, n3b) + tmm(n3b, b))
+    alpha2 = finish(solve(pq, fresh))
+    ba, aa = mm(b, alpha2), mm(a, alpha2)
+    w[0:n] = jnp.concatenate([aa - b, delta - shift * aa], axis=1)
+    w[n : 2 * n] = jnp.concatenate([ba, b - shift * ba - aa], axis=1)
+    w[2 * n :] = jnp.concatenate([jnp.zeros_like(ba), -ba], axis=1)
+
+
+def last_kernel(moved, p0, p1, owed, weights, sol, res, basis, sems):
     first = (lax.axis_index("group") * 32 + lax.axis_index("bulk")) * 4
     base = lax.axis_index("group") * 128
     half = sol.shape[1]
+    n = half // 2
+    copies = []
     for s in range(sol.shape[0]):
         c, i = place(moved[first + s] - base)
-        x = jnp.concatenate([joined(p0, c, i), joined(p1, c, i), owed[0, s], owed[1, s]], axis=0)
-        out = lax.dot_general(
-            weights[...], x, (COLS, ((), ())), precision=highest, preferred_element_type=f32
-        )
+        for k, p in enumerate((p0, p1)):
+            for j in range(2):
+                dst = basis.at[s, pl.ds((2 * k + j) * n, n)]
+                d = pltpu.make_async_copy(p.at[c, j, i], dst, sems.at[s, 2 * k + j])
+                d.start()
+                copies.append(d)
+    for d in copies:
+        d.wait()
+    for s in range(sol.shape[0]):
+        x = jnp.concatenate([basis[s], owed[0, s], owed[1, s]], axis=0)
+        out = tmm(weights[...], x)
         sol[s] = out[:half]
         res[s] = out[half:]
-
-
-def chol_apply(matrix, right):
-    factor = jnp.linalg.cholesky(matrix)
-    middle = lax.linalg.triangular_solve(factor, right, left_side=True, lower=True)
-    return lax.linalg.triangular_solve(factor, middle, left_side=True, lower=True, transpose_a=True)
-
-
-def sym(m):
-    return 0.5 * (m + m.T)
-
-
-def mm(a, b):
-    return jnp.dot(a, b, precision=highest)
-
-
-def coefficients(n0, n1, n2, n3):
-    n = n0.shape[0]
-    eye = jnp.eye(n, dtype=n0.dtype)
-    n0, n1, n2, n3 = sym(n0), sym(n1), sym(n2), sym(n3)
-    delta = chol_apply(shift * n0 + n1, n1)
-    alpha = (eye - delta) / shift
-    b = -alpha
-    cross = mm(delta.T, mm(n1, b))
-    gram_new = sym(mm(delta.T, mm(n0, delta)) + cross + cross.T + mm(b.T, mm(n2, b)))
-    beta = chol_apply(n0, gram_new)
-    a = delta + beta
-    c1 = mm(a.T, mm(n1, b))
-    c2 = mm(a.T, mm(n2, b))
-    pp = mm(a.T, mm(n0, a)) + c1 + c1.T + mm(b.T, mm(n2, b))
-    pep = mm(a.T, mm(n1, a)) + c2 + c2.T + mm(b.T, mm(n3, b))
-    alpha2 = chol_apply(sym(shift * pp + pep), gram_new)
-    ba = mm(b, alpha2)
-    aa = mm(a, alpha2)
-    sol = (alpha + aa, ba, jnp.zeros_like(ba))
-    res = (delta - shift * aa, b - shift * ba - aa, -ba)
-    return jnp.concatenate(
-        [jnp.concatenate(sol, axis=0), jnp.concatenate(res, axis=0)], axis=1
-    ).T
 
 
 def local(rhs, diag, off, coup, col_index, load, new_slot):
@@ -565,13 +631,22 @@
         name="second",
     )(col_index, load, new_slot, p1.reshape(flat), border1, u1, diag, coup, off)
     owed, g3 = exchange(None, buf.reshape(panel_shape), g3, 2)
-    n3 = jnp.concatenate([g3[:, :n2], g3[:, n2:]], axis=0)
-    weights = coefficients(g01[:n2, :n2], g01[:n2, n2:], g01[n2:, n2:], n3)
+    weights = pl.pallas_call(
+        coefficient_kernel,
+        out_shape=jax.ShapeDtypeStruct((3 * n2, 2 * n2), f32),
+        in_specs=[vm, vm],
+        out_specs=vm,
+        name="coefficients",
+    )(g01, g3)
     sol, res = pl.pallas_call(
         last_kernel,
         out_shape=[jax.ShapeDtypeStruct(rhs.shape, f32)] * 2,
-        in_specs=[sm] + [vm] * 4,
+        in_specs=[sm, anys, anys, vm, vm],
         out_specs=[vm, vm],
+        scratch_shapes=[
+            pltpu.VMEM((rows, 2 * n2, w), f32),
+            pltpu.SemaphoreType.DMA((rows, 4)),
+        ],
         compiler_params=params,
         name="last",
     )(new_slot, p0.reshape(flat), p1.reshape(flat), owed, weights)

time: 171 us -> 131 us (0.77)
  other arithmetic: 36.5 us -> 0 us
  matrix products: 4.67 us -> 0 us
  Pallas kernels: 118 us -> 120 us
    another operation x15 -> x0, other arithmetic: 36.2 us -> none  [the longest x9 19.6 us: chol_apply(): factor = jnp.linalg.cholesky(matrix)]
    pallas_call x0 -> x1, Pallas kernels: none -> 9.46 us  [local(): pl.pallas_call(coefficient_kernel, out_shape=jax.ShapeDtypeStruct((3 * n2...]
    pallas_call x3, Pallas kernels: 98 us -> 89.4 us  [exchange(): pl.pallas_call(functools.partial(exchange_kernel, gather, scatter, reduce...]
    dot_general x16 -> x0, matrix products: 3.29 us -> none  [mm(): return jnp.dot(a, b, precision=highest)]
    unnamed x23 -> x29, local copies, waits for them, and re-layouts: 7.78 us -> 9.27 us
where the time goes in v3:
time: 131 us
  Pallas kernels  120 us (92%)
  local copies, waits for them, and re-layouts  10.2 us (8%)
    pallas_call x3, Pallas kernels, exchange(): pl.pallas_call(functools.partial(exchange_kernel, gather, scatter, reduce...  89.4 us
    pallas_call x1, Pallas kernels, local(): pl.pallas_call(coefficient_kernel, out_shape=jax.ShapeDtypeStruct((3 * n2...  9.46 us
    unnamed x29, local copies, waits for them, and re-layouts  9.27 us
    pallas_call x1, Pallas kernels, local(): pl.pallas_call(second_kernel, out_shape=[jax.ShapeDtypeStruct(flat, f32),...  8.55 us
    pallas_call x1, Pallas kernels, local(): pl.pallas_call(first_kernel, out_shape=[row_shape, jax.ShapeDtypeStruct((...  6.4 us
    pallas_call x1, Pallas kernels, local(): pl.pallas_call(returned_kernel, out_shape=jax.ShapeDtypeStruct(flat, f32)...  3.21 us

profile of v3, /device:TPU:1, one launch (start us, length us, event | category | flops | bytes accessed | tf_op | source)
XLA Modules:
  0.0 130.7 jit_solution(10946649998276689137)
XLA Ops:
  0.6 0.9 copy.17
  1.5 0.9 copy.13.col_hbm
  2.4 0.0 copy-start
  2.5 1.8 %copy-done = f32[4,11,128,128]{3,2,1,0:T(8,128)S(1)} copy-done((f32[4,11,128,128]{3,2,1,0:T(8,128)S(1)}, f32[4,11,128,128]{3,2,1,0:T(8,128)}, u32[]{:S(2)}) %copy-start) | copy-done | bytes 2883608
  4.3 0.0 copy-start.10
  4.3 0.7 copy-done.10
  4.9 0.0 copy-start.1
  5.0 0.0 copy-start.6
  5.0 0.0 copy-start.7
  5.0 0.0 copy-start.11
  5.0 3.2 %returned.1 = f32[2,2,64,32,128]{4,3,2,1,0:T(8,128)S(1)} custom-call(s32[512,11]{1,0:T(8,128)S(1)} %copy.13.col_hbm, s32[512]{0:T(512)S(1)} %copy-done.10, f32[2,4,32,128]{3,2,1,0:T(8,128)S(1)} %bitcast.14, f32[4,11,128,128]{3,2,1,0:T(8,128)S(1)} %copy-done), custom_call_target="tpu_custom_call" | custom-call | tf_op jit(solution)/shard_map/returned/pallas_call | solution.py:601
  8.2 33.4 %exchange0.1 = (f32[2,2,4,4,4,32,128]{6,5,4,3,2,1,0:T(8,128)S(1)}, f32[4,2,2,32,128]{4,3,2,1,0:T(8,128)S(1)}, f32[2,4,32,128]{3,2,1,0:T(8,128)S(1)}) custom-call(f32[2,4,32,128]{3,2,1,0:T(8,128)S(1)} %bitcast.15, f32[2,2,4,4,4,32,128]{6,5,4,3,2,1,0:T(8,128)S(1)} %bitcast.12), custom_call_target="tpu_custom_call" | custom-call | tf_op jit(solution)/shard_map/exchange0/pallas_call | solution.py:311
  41.6 0.0 copy-start.2
  41.6 0.0 copy-done.1
  41.6 0.0 copy-done.6
  41.6 0.0 copy-done.7
  41.6 0.0 copy-done.11
  41.6 0.0 copy-start.13
  41.6 6.4 %first.1 = (f32[2,4,32,128]{3,2,1,0:T(8,128)S(1)}, f32[128,128]{1,0:T(8,128)S(1)}) custom-call(s32[512,11]{1,0:T(8,128)S(1)} %copy.13.col_hbm, s32[512]{0:T(512)S(1)} %copy-done.11, f32[2,2,64,32,128]{4,3,2,1,0:T(8,128)S(1)} %bitcast.8, f32[4,2,2,32,128]{4,3,2,1,0:T(8,128)S(1)} %get-tuple-element.15.border, f32[2,4,32,128]{3,2,1,0:T(8,128)S(1)} %get-tuple-element.16.owed, ...), custom_call_target="tpu_custom_call" | custom-call | tf_op jit(solution)/shard_map/first/pallas_call | solution.py:611
  48.0 0.0 copy-done.2
  48.0 29.5 %exchange1.1 = (f32[2,2,4,4,4,32,128]{6,5,4,3,2,1,0:T(8,128)S(1)}, f32[4,2,2,32,128]{4,3,2,1,0:T(8,128)S(1)}, f32[128,128]{1,0:T(8,128)S(1)}) custom-call(f32[2,4,32,128]{3,2,1,0:T(8,128)S(1)} %get-tuple-element.17.refs_0_.u, f32[128,128]{1,0:T(8,128)S(1)} %get-tuple-element.18.refs_1_), custom_call_target="tpu_custom_call" | custom-call | tf_op jit(solution)/shard_map/exchange1/pallas_call | solution.py:311
  77.5 0.0 copy-start.4
  77.5 0.0 copy-start.9
  77.5 0.0 copy-done.13
  77.5 8.6 %second.1 = (f32[2,2,64,32,128]{4,3,2,1,0:T(8,128)S(1)}, f32[32,128]{1,0:T(8,128)S(1)}) custom-call(s32[512,11]{1,0:T(8,128)S(1)} %copy.13.col_hbm, s32[512]{0:T(512)S(1)} %copy-done.11, s32[512]{0:T(512)S(1)} %copy-done.13, f32[2,2,64,32,128]{4,3,2,1,0:T(8,128)S(1)} %bitcast.10, f32[4,2,2,32,128]{4,3,2,1,0:T(8,128)S(1)} %get-tuple-element.20.border, ...), custom_call_target="tpu_custom_call" | custom-call | tf_op jit(solution)/shard_map/second/pallas_call | solution.py:621
  86.1 0.0 copy-done.4
  86.1 0.0 copy-done.9
  86.1 26.6 %exchange2.1 = (f32[2,4,32,128]{3,2,1,0:T(8,128)S(1)}, f32[32,128]{1,0:T(8,128)S(1)}) custom-call(f32[2,2,4,4,4,32,128]{6,5,4,3,2,1,0:T(8,128)S(1)} %bitcast.13, f32[32,128]{1,0:T(8,128)S(1)} %get-tuple-element.22.refs_1_), custom_call_target="tpu_custom_call" | custom-call | tf_op jit(solution)/shard_map/exchange2/pallas_call | solution.py:311
  112.7 0.0 copy-start.12
  112.7 0.6 copy-done.12
  113.3 9.5 %coefficients.1.weights = f32[192,128]{1,0:T(8,128)} custom-call(f32[128,128]{1,0:T(8,128)} %copy-done.9, f32[32,128]{1,0:T(8,128)} %copy-done.12), custom_call_target="tpu_custom_call" | custom-call | tf_op jit(solution)/shard_map/coefficients/pallas_call | solution.py:634
  122.7 0.0 copy-start.3
  122.7 2.2 %copy-done.3 = f32[2,2,4,4,4,32,128]{6,5,4,3,2,1,0:T(8,128)S(1)} copy-done((f32[2,2,4,4,4,32,128]{6,5,4,3,2,1,0:T(8,128)S(1)}, f32[2,2,4,4,4,32,128]{6,5,4,3,2,1,0:T(8,128)}, u32[]{:S(2)}) %copy-start.3) | copy-done | bytes 4194328
  124.9 0.0 copy-start.5
  124.9 2.2 %copy-done.5 = f32[2,2,4,4,4,32,128]{6,5,4,3,2,1,0:T(8,128)S(1)} copy-done((f32[2,2,4,4,4,32,128]{6,5,4,3,2,1,0:T(8,128)S(1)}, f32[2,2,4,4,4,32,128]{6,5,4,3,2,1,0:T(8,128)}, u32[]{:S(2)}) %copy-start.5) | copy-done | bytes 4194328
  127.1 0.0 copy-start.8
  127.1 0.9 copy-done.8
  128.0 2.5 %last.1 = (f32[4,64,128]{2,1,0:T(8,128)}, f32[4,64,128]{2,1,0:T(8,128)}) custom-call(s32[512]{0:T(512)S(1)} %copy-done.13, f32[2,2,64,32,128]{4,3,2,1,0:T(8,128)S(1)} %bitcast.9, f32[2,2,64,32,128]{4,3,2,1,0:T(8,128)S(1)} %bitcast.11, f32[2,4,32,128]{3,2,1,0:T(8,128)S(1)} %get-tuple-element.23.owed, f32[192,128]{1,0:T(8,128)S(1)} %copy-done.8), custom_call_target="tpu_custom_call" | custom-call | tf_op jit(solution)/shard_map/last/pallas_call | solution.py:641
Async XLA Ops:
  2.4 1.8 %copy-start = (f32[4,11,128,128]{3,2,1,0:T(8,128)S(1)}, f32[4,11,128,128]{3,2,1,0:T(8,128)}, u32[]{:S(2)}) copy-start(f32[4,11,128,128]{3,2,1,0:T(8,128)} %off.5) | copy-start | bytes 8650756
  4.3 0.7 copy-start.10
  4.9 36.6 %copy-start.1 = (f32[4,11,128,128]{3,2,1,0:T(8,128)S(1)}, f32[4,11,128,128]{3,2,1,0:T(8,128)}, u32[]{:S(2)}) copy-start(f32[4,11,128,128]{3,2,1,0:T(8,128)} %off.5) | copy-start | bytes 8650756
  5.0 36.6 %copy-start.6 = (f32[2,4,128,128]{3,2,1,0:T(8,128)S(1)}, f32[2,4,128,128]{3,2,1,0:T(8,128)}, u32[]{:S(2)}) copy-start(f32[2,4,128,128]{3,2,1,0:T(8,128)} %coup.3) | copy-start | bytes 1572868
  5.0 36.6 %copy-start.7 = (f32[4,128,128]{2,1,0:T(8,128)S(1)}, f32[4,128,128]{2,1,0:T(8,128)}, u32[]{:S(2)}) copy-start(f32[4,128,128]{2,1,0:T(8,128)} %diag.3) | copy-start | bytes 786436
  5.0 36.6 %copy-start.11 = (s32[512]{0:T(512)S(1)}, s32[512]{0:T(512)}, u32[]{:S(2)}) copy-start(s32[512]{0:T(512)} %load.5) | copy-start | bytes 6148
  41.6 6.5 %copy-start.2 = (f32[2,2,4,4,4,32,128]{6,5,4,3,2,1,0:T(8,128)}, f32[2,2,4,4,4,32,128]{6,5,4,3,2,1,0:T(8,128)S(1)}, u32[]{:S(2)}) copy-start(f32[2,2,4,4,4,32,128]{6,5,4,3,2,1,0:T(8,128)S(1)} %get-tuple-element.14) | copy-start | bytes 12582916
  41.6 35.9 %copy-start.13 = (s32[512]{0:T(512)S(1)}, s32[512]{0:T(512)}, u32[]{:S(2)}) copy-start(s32[512]{0:T(512)} %moved.3) | copy-start | bytes 6148
  77.5 8.6 %copy-start.4 = (f32[2,2,4,4,4,32,128]{6,5,4,3,2,1,0:T(8,128)}, f32[2,2,4,4,4,32,128]{6,5,4,3,2,1,0:T(8,128)S(1)}, u32[]{:S(2)}) copy-start(f32[2,2,4,4,4,32,128]{6,5,4,3,2,1,0:T(8,128)S(1)} %get-tuple-element.19) | copy-start | bytes 12582916
  77.5 8.6 %copy-start.9 = (f32[128,128]{1,0:T(8,128)}, f32[128,128]{1,0:T(8,128)S(1)}, u32[]{:S(2)}) copy-start(f32[128,128]{1,0:T(8,128)S(1)} %get-tuple-element.24.g) | copy-start | bytes 196612
  112.7 0.6 copy-start.12
  122.7 2.2 %copy-start.3 = (f32[2,2,4,4,4,32,128]{6,5,4,3,2,1,0:T(8,128)S(1)}, f32[2,2,4,4,4,32,128]{6,5,4,3,2,1,0:T(8,128)}, u32[]{:S(2)}) copy-start(f32[2,2,4,4,4,32,128]{6,5,4,3,2,1,0:T(8,128)} %copy-done.2) | copy-start | bytes 12582916
  124.9 2.2 %copy-start.5 = (f32[2,2,4,4,4,32,128]{6,5,4,3,2,1,0:T(8,128)S(1)}, f32[2,2,4,4,4,32,128]{6,5,4,3,2,1,0:T(8,128)}, u32[]{:S(2)}) copy-start(f32[2,2,4,4,4,32,128]{6,5,4,3,2,1,0:T(8,128)} %copy-done.4) | copy-start | bytes 12582916
  127.1 0.9 copy-start.8

commit v4 on v3

v4 whole, which is shorter than its diff:
```python
import functools

import jax
import jax.numpy as jnp
from jax import lax
from jax.experimental import pallas as pl
from jax.experimental.pallas import tpu as pltpu
from jax.sharding import PartitionSpec as P

highest = lax.Precision.HIGHEST
shift = 4.0
f32 = jnp.float32
bf16 = jnp.bfloat16
RING = 4
MESH = pl.DeviceIdType.MESH


class Net:
    def __init__(self, send, recv):
        self.g = lax.axis_index("group")
        b = lax.axis_index("bulk")
        self.c = lax.rem(b, 2)
        self.y = lax.rem(b // 2, RING)
        self.z = b // (2 * RING)
        self.send, self.recv = send, recv
        self.count = 0
        self.pending = []

    def device(self, dx=0, dy=0, dz=0, partner=False):
        c = 1 - self.c if partner else self.c
        y = lax.rem(self.y + dy, RING)
        z = lax.rem(self.z + dz, RING)
        return (lax.rem(self.g + dx, RING), (z * RING + y) * 2 + c)

    def copy(self, src, dst, device):
        i = self.count
        self.count += 1
        d = pltpu.make_async_remote_copy(
            src_ref=src,
            dst_ref=dst,
            send_sem=self.send.at[i],
            recv_sem=self.recv.at[i],
            device_id=device,
            device_id_type=MESH,
        )
        d.start()
        self.pending.append(d)
        return d

    def drain(self):
        for d in self.pending:
            d.wait_send()


def plus(a, k):
    return lax.rem(a + k, RING)


def greet(net, devices):
    barrier = pltpu.get_barrier_semaphore()
    for d in devices:
        pl.semaphore_signal(barrier, inc=1, device_id=d, device_id_type=MESH)
    pl.semaphore_wait(barrier, len(devices))


def gather_steps(net, j, u, panel, local_sem):
    c, y, z = net.c, net.y, net.z
    f0, s0 = (y, z) if j == 0 else (z, y)

    def unit(fi, si):
        return panel.at[c, j, si, fi] if j == 0 else panel.at[c, j, fi, si]

    def column(si):
        return panel.at[c, j, si] if j == 0 else panel.at[c, j, :, si]

    def to(df, ds):
        return net.device(dy=df, dz=ds) if j == 0 else net.device(dy=ds, dz=df)

    partner = net.device(partner=True)
    mine = unit(f0, s0)
    own = pltpu.make_async_copy(u.at[j], mine, local_sem)
    own.start()
    near = [net.copy(u.at[j], mine, to(k, 0)) for k in (1, 3)]
    ups = [net.copy(u.at[j], mine, to(0, 1))]
    downs = [net.copy(u.at[j], mine, to(0, 3))]
    far = net.copy(u.at[j], mine, to(2, 0))
    lo, hi = pl.ds(0, 2), pl.ds(2, 2)
    order = [f0, plus(f0, 3), plus(f0, 1), plus(f0, 2)]
    halves = []

    def pass_on(p):
        piece = unit(order[p], s0)
        ups.append(net.copy(piece, piece, to(0, 1)))
        downs.append(net.copy(piece, piece, to(0, 3)))

    def forward(p):
        ups[p].wait_recv()
        piece = unit(order[p], plus(s0, 3)).at[lo]
        halves.append(net.copy(piece, piece, to(0, 1)))
        downs[p].wait_recv()
        piece = unit(order[p], plus(s0, 1)).at[hi]
        halves.append(net.copy(piece, piece, to(0, 3)))

    def swap(k):
        return net.copy(column(plus(s0, k)), column(plus(s0, k)), partner)

    for p in (1, 2):
        yield
        near[p - 1].wait_recv()
        pass_on(p)
    yield
    forward(0)
    yield
    far.wait_recv()
    pass_on(3)
    piece = unit(order[3], s0)
    last = net.copy(piece, piece, to(0, 2))
    own.wait()
    swapped = [swap(0)]
    for p in (1, 2):
        yield
        forward(p)
    yield
    ups[3].wait_recv()
    swapped.append(swap(3))
    yield
    downs[3].wait_recv()
    swapped.append(swap(1))
    yield
    for d in halves:
        d.wait_recv()
    last.wait_recv()
    swapped.append(swap(2))
    for d in swapped:
        yield
        d.wait_recv()


def scatter_steps(net, j, owed, stage, r, t0, t1, t2, t3):
    y, z = net.y, net.z
    f0, s0 = (y, z) if j == 0 else (z, y)

    def column(ref, k):
        si = plus(s0, k)
        return ref.at[j, si] if j == 0 else ref.at[j, :, si]

    def to(df, ds):
        return net.device(dy=df, dz=ds) if j == 0 else net.device(dy=ds, dz=df)

    partner = net.device(partner=True)
    lo, hi = pl.ds(0, 2), pl.ds(2, 2)
    order = [2, 1, 3, 0]
    rows = {k: plus(f0, k) for k in range(RING)}
    first = {}
    for k in order:
        first[k] = net.copy(column(stage, k), column(t0, k), partner)
    cols = {k: column(r, k) for k in range(RING)}

    def start(k):
        b = column(t0, k)
        for i in order:
            cols[k][rows[i]] = cols[k][rows[i]] + b[rows[i]]

    yield
    first[2].wait_recv()
    start(2)
    ups = {i: net.copy(cols[2].at[rows[i], lo], t1.at[j, 0, rows[i]], to(0, 1)) for i in order}
    downs = {i: net.copy(cols[2].at[rows[i], hi], t1.at[j, 1, rows[i]], to(0, 3)) for i in order}
    yield
    first[1].wait_recv()
    start(1)
    yield
    first[3].wait_recv()
    start(3)
    yield
    first[0].wait_recv()
    start(0)
    ups2, downs2 = {}, {}
    for i in order:
        q = rows[i]
        yield
        ups[i].wait_recv()
        cols[1][q, lo] = cols[1][q, lo] + t1[j, 0, q]
        ups2[i] = net.copy(cols[1].at[q], t2.at[j, 0, q], to(0, 1))
        downs[i].wait_recv()
        cols[3][q, hi] = cols[3][q, hi] + t1[j, 1, q]
        downs2[i] = net.copy(cols[3].at[q], t2.at[j, 1, q], to(0, 3))
    sent = []
    for i in order:
        q = rows[i]
        yield
        ups2[i].wait_recv()
        downs2[i].wait_recv()
        cols[0][q] = cols[0][q] + (t2[j, 0, q] + t2[j, 1, q])
        if i:
            sent.append(net.copy(cols[0].at[q], t3.at[j, i - 1], to(i, 0)))
    for d in sent:
        yield
        d.wait_recv()
    owed[j] = (cols[0][rows[0]] + t3[j, 0]) + (t3[j, 1] + t3[j, 2])


def border_steps(net, u, border, local_sem):
    src = u.at[:, pl.ds(0, 2)]
    own = pltpu.make_async_copy(src, border.at[net.g], local_sem)
    own.start()
    sent = [net.copy(src, border.at[net.g], net.device(dx=k)) for k in (1, 3, 2)]
    yield
    own.wait()
    for d in sent:
        d.wait_recv()


def reduce_steps(net, m, out, acc, slots, halves):
    c = net.c
    rows = acc.shape[1]
    partner = net.device(partner=True)
    d = net.copy(m.at[pl.ds((1 - c) * rows, rows)], halves, partner)
    yield
    d.wait_recv()
    acc[0] = m[pl.ds(c * rows, rows)] + halves[...]
    for t in range(3):
        sent = []
        for k in (1, 3, 2):
            step = [0, 0, 0]
            step[t] = k * (1 - c)
            step[(t + 1) % 3] = step[(t + 1) % 3] + k * c
            sent.append(
                net.copy(acc.at[t], slots.at[t, k - 1], net.device(step[0], step[1], step[2]))
            )
        yield
        for d in sent:
            d.wait_recv()
        acc[t + 1] = (acc[t] + slots[t, 0]) + (slots[t, 1] + slots[t, 2])
    out[pl.ds(c * rows, rows)] = acc[3]
    d = net.copy(acc.at[3], out.at[pl.ds(c * rows, rows)], partner)
    yield
    d.wait_recv()


def run(steps):
    steps = list(steps)
    while steps:
        left = []
        for s in steps:
            try:
                next(s)
                left.append(s)
            except StopIteration:
                pass
        steps = left


def split(a):
    top = a.astype(bf16)
    return top, (a - top.astype(f32)).astype(bf16)


def dot3(a, b, dims):
    dot = functools.partial(
        lax.dot_general, dimension_numbers=(dims, ((), ())), preferred_element_type=f32
    )
    return dot(a[0], b[0]) + (dot(a[0], b[1]) + dot(a[1], b[0]))


ROWS = ((1,), (1,))
COLS = ((1,), (0,))


ROW_COUNT = 4
OFFS = 11
ENTRIES = ROW_COUNT * OFFS
PART_ROWS = 128
NONE = ENTRIES
OWN = ENTRIES + 1
FIRST = 0
SECOND = 2 * PART_ROWS
PLACE = SECOND + 3 * PART_ROWS
LIVE = PLACE + ENTRIES
MINE = LIVE + ENTRIES
SPARE = MINE + ROW_COUNT
TABLE = SPARE + 4


def position(slot):
    return lax.rem(slot // 4, 2) * 64 + (slot // 8) * 4 + lax.rem(slot, 4)


def table_kernel(col_hbm, load, moved, table, cols, sem):
    first = (lax.axis_index("group") * 32 + lax.axis_index("bulk")) * ROW_COUNT
    base = lax.axis_index("group") * PART_ROWS
    d = pltpu.make_async_copy(col_hbm.at[pl.ds(first, ROW_COUNT)], cols, sem)
    d.start()

    def clear(i, _):
        for k in range(5):
            table[k * PART_ROWS + i] = NONE
        return 0

    lax.fori_loop(0, PART_ROWS, clear, 0)
    for i in range(SPARE, TABLE):
        table[i] = NONE
    d.wait()
    for s in range(ROW_COUNT):
        live_count = load[first + s]
        target = position(moved[first + s] - base)
        table[SECOND + 2 * PART_ROWS + target] = OWN + s
        table[MINE + s] = target

        def entry(t, _):
            e = s * OFFS + t
            slot = cols[s, t]
            live = t < live_count
            p = position(slot - base)
            q = position(moved[slot] - base)
            table[PLACE + e] = p
            table[LIVE + e] = live.astype(jnp.int32)
            i = FIRST + p + jnp.where(table[FIRST + p] == NONE, 0, PART_ROWS)
            table[jnp.where(live, i, SPARE)] = e
            i = SECOND + q + jnp.where(table[SECOND + q] == NONE, 0, PART_ROWS)
            table[jnp.where(live, i, SPARE)] = e
            return 0

        lax.fori_loop(0, OFFS, entry, 0)


def gram(a, b):
    return lax.dot_general(a, b, (ROWS, ((), ())), precision=highest, preferred_element_type=f32)


def whole(ref, *idx):
    return jnp.concatenate([ref[(0,) + idx], ref[(1,) + idx]], axis=0)


def panel_row(panel, p):
    c, z = p // 64, lax.rem(p // 16, RING)
    y, k = lax.rem(p // 4, RING), lax.rem(p, 4)
    return jnp.concatenate([panel[c, 0, z, y, k], panel[c, 1, z, y, k]], axis=0)


def solve(m, r):
    n = m.shape[0]
    t = jnp.concatenate([m, r], axis=1)
    blocks = [t[8 * i : 8 * i + 8] for i in range(n // 8)]
    shape = blocks[0].shape
    row_id = lax.broadcasted_iota(jnp.int32, shape, 0)
    for b in range(n // 8):
        piv = blocks[b]
        rows = [jnp.broadcast_to(piv[i : i + 1], shape) for i in range(8)]
        lanes = [jnp.broadcast_to(piv[:, 8 * b + i : 8 * b + i + 1], shape) for i in range(8)]
        d = [[jnp.broadcast_to(lanes[q][i : i + 1], shape) for q in range(8)] for i in range(8)]
        for i in range(8):
            inv = 1.0 / d[i][i]
            rows[i] = rows[i] * inv
            for q in range(i + 1, 8):
                d[i][q] = d[i][q] * inv
            for k in range(8):
                if k != i:
                    factor = d[k][i]
                    rows[k] = rows[k] - factor * rows[i]
                    for q in range(i + 1, 8):
                        d[k][q] = d[k][q] - factor * d[i][q]
        new = rows[0]
        for i in range(1, 8):
            new = jnp.where(row_id == i, rows[i], new)
        for k in range(n // 8):
            if k != b:
                acc = blocks[k]
                for i in range(8):
                    column = blocks[k][:, 8 * b + i : 8 * b + i + 1]
                    acc = acc - jnp.broadcast_to(column, shape) * rows[i]
                blocks[k] = acc
        blocks[b] = new
        yield
    return jnp.concatenate(blocks, axis=0)[:, n:]


def both(*solves):
    out = [None] * len(solves)
    left = list(range(len(solves)))
    while left:
        for i in list(left):
            try:
                next(solves[i])
            except StopIteration as e:
                out[i] = e.value
                left.remove(i)
        yield
    return out


def finish(steps):
    while True:
        try:
            next(steps)
        except StopIteration as e:
            return e.value


def mm(a, b):
    return lax.dot_general(a, b, (COLS, ((), ())), precision=highest, preferred_element_type=f32)


def tmm(a, b):
    return lax.dot_general(
        a, b, (((0,), (0,)), ((), ())), precision=highest, preferred_element_type=f32
    )


def first_coefficients(g):
    n = g.shape[0] // 2
    g = 0.5 * (g + g.T)
    n0, n1, n2 = g[:n, :n], 0.5 * (g[:n, n:] + g[n:, :n]), g[n:, n:]
    eye = (
        lax.broadcasted_iota(jnp.int32, (n, n), 0) == lax.broadcasted_iota(jnp.int32, (n, n), 1)
    ).astype(f32)
    delta, inverse = yield from both(solve(shift * n0 + n1, n1), solve(n0, eye))
    b = (delta - eye) * (1.0 / shift)
    yield
    n1b, n2b, n0d = mm(n1, b), mm(n2, b), mm(n0, delta)
    yield
    bb = tmm(b, n2b)
    fresh = tmm(delta, n0d) + (tmm(delta, n1b) + tmm(n1b, delta)) + bb
    yield
    a = delta + mm(inverse, fresh)
    yield
    pp = tmm(a, mm(n0, a)) + (tmm(a, n1b) + tmm(n1b, a)) + bb
    pep = tmm(a, mm(n1, a)) + (tmm(a, n2b) + tmm(n2b, a))
    yield
    return delta, a, fresh, shift * pp + pep


def last_coefficients(first, n3):
    delta, a, fresh, known = first
    n = delta.shape[0]
    eye = (
        lax.broadcasted_iota(jnp.int32, (n, n), 0) == lax.broadcasted_iota(jnp.int32, (n, n), 1)
    ).astype(f32)
    b = (delta - eye) * (1.0 / shift)
    n3b = mm(n3, b)
    pq = known + 0.5 * (tmm(b, n3b) + tmm(n3b, b))
    yield
    alpha2 = yield from solve(pq, fresh)
    ba, aa = mm(b, alpha2), mm(a, alpha2)
    return (
        jnp.concatenate([aa - b, delta - shift * aa], axis=1),
        jnp.concatenate([ba, b - shift * ba - aa], axis=1),
        jnp.concatenate([jnp.zeros_like(ba), -ba], axis=1),
    )


def fused_kernel(table, rhs, diag_in, off_in, coup_in, sol, res, *refs):
    refs = iter(refs)

    def take(count):
        return [next(refs) for _ in range(count)]

    u0, u1, diag, off, coup, products, part = take(7)
    panel0, border0, panel1, border1 = take(4)
    owed0, stage0, r0 = take(3)
    parts0 = take(4)
    owed1, stage1, r1 = take(3)
    parts1 = take(4)
    g01, total01 = take(2)
    work01 = take(3)
    g3, total3 = take(2)
    work3 = take(3)
    send, recv, local_sems, in_sems = take(4)
    n = u0.shape[2]
    net = Net(send, recv)
    c = net.c
    loads = [
        pltpu.make_async_copy(rhs.at[:, pl.ds(j * n, n)], u0.at[j], in_sems.at[j]) for j in range(2)
    ] + [
        pltpu.make_async_copy(a, b, in_sems.at[2 + i])
        for i, (a, b) in enumerate(((off_in, off), (diag_in, diag), (coup_in, coup)))
    ]
    for d in loads:
        d.start()
    greet(
        net,
        [net.device(partner=True)]
        + [net.device(dy=k) for k in (2, 1, 3)]
        + [net.device(dz=k) for k in (2, 1, 3)]
        + [net.device(dx=k) for k in (2, 1, 3)],
    )
    for k in range(NONE, products.shape[0]):
        products[k] = jnp.zeros(products.shape[1:], f32)

    def returned(u):
        def row(s, _):
            v = split(whole(u, s))
            for t in range(OFFS):
                p = dot3(v, split(off[s, t]), COLS)
                products[s * OFFS + t, 0] = p[:n]
                products[s * OFFS + t, 1] = p[n:]
            return 0

        lax.fori_loop(0, ROW_COUNT, row, 0)

    def fill(dst, core, start, count):
        def plane(z, _):
            for y in range(RING):
                for k in range(4):
                    p = core * 64 + (z * RING + y) * 4 + k
                    es = [table[start + i * PART_ROWS + p] for i in range(count)]
                    for j in range(2):
                        v = products[es[0], j]
                        for e in es[1:]:
                            v = v + products[e, j]
                        dst[j, z, y, k] = v
            return 0

        lax.fori_loop(0, RING, plane, 0)

    def crossed(border, s):
        out = None
        for h in range(RING):
            p = dot3(split(jnp.concatenate([border[h, 0, s], border[h, 1, s]], axis=0)), split(coup[s, h]), ROWS)
            out = p if out is None else out + p
        return out

    def tiles_of(panel, s):
        out = None
        for t in range(OFFS):
            e = s * OFFS + t
            live = table[LIVE + e].astype(f32)
            v = panel_row(panel, table[PLACE + e]) * live
            p = dot3(split(v), split(off[s, t]), ROWS)
            out = p if out is None else out + p
        return out

    def rest_steps(u, border, border_done):
        for s in range(ROW_COUNT):
            part[s] = dot3(split(whole(u, s)), split(diag[s]), ROWS)
        while not border_done:
            yield
        for s in range(coup.shape[0]):
            part[s] = part[s] + crossed(border, s)
            yield

    def marked(steps, mark):
        out = yield from steps
        mark.append(out)

    def started(steps):
        next(steps)
        return steps

    loads[0].wait()
    loads[1].wait()
    got_panel, got_border = [], []
    going = [
        started(marked(gather_steps(net, j, u0, panel0, local_sems.at[j]), got_panel))
        for j in range(2)
    ]
    going.append(started(marked(border_steps(net, u0, border0, local_sems.at[2]), got_border)))
    for d in loads[2:]:
        d.wait()
    returned(u0)
    fill(stage0, 1 - c, FIRST, 2)
    scatters = [scatter_steps(net, j, owed0, stage0, r0, *parts0) for j in range(2)]
    fill(r0, c, FIRST, 2)
    scatters = [started(s) for s in scatters]

    def forward_steps():
        yield from rest_steps(u0, border0, got_border)
        while len(got_panel) < 2:
            yield
        for s in range(ROW_COUNT):
            part[s] = part[s] + tiles_of(panel0, s)
            yield

    run(scatters + going + [forward_steps()])
    for s in range(ROW_COUNT):
        for j in range(2):
            u1[j, s] = part[s, j * n : (j + 1) * n] + owed0[j, s]

    got_panel, got_border = [], []
    going = [
        started(marked(gather_steps(net, j, u1, panel1, local_sems.at[3 + j]), got_panel))
        for j in range(2)
    ]
    going.append(started(marked(border_steps(net, u1, border1, local_sems.at[5]), got_border)))
    total = None
    for s in range(ROW_COUNT):
        x = jnp.concatenate([whole(u0, s), whole(u1, s)], axis=0)
        total = gram(x, x) if total is None else total + gram(x, x)
    g01[...] = total
    going.append(started(reduce_steps(net, g01, total01, *work01)))
    returned(u1)
    run(going + [rest_steps(u1, border1, got_border)])

    def second_row(s, total):
        tiles = tiles_of(panel1, s)
        w = tiles + part[s]
        products[OWN + s, 0] = w[:n]
        products[OWN + s, 1] = w[n:]
        return total + gram(whole(u1, s), w + tiles)

    total = lax.fori_loop(0, ROW_COUNT, second_row, jnp.zeros((2 * n, 2 * n), f32))
    g3[...] = jnp.concatenate([total[:n], total[n:]], axis=1)
    known, reduced, weights, scattered = [], [], [], []
    going = [started(marked(reduce_steps(net, g3, total3, *work3), reduced))]
    fill(stage1, 1 - c, SECOND, 3)
    scatters = [marked(scatter_steps(net, j, owed1, stage1, r1, *parts1), scattered) for j in range(2)]
    fill(r1, c, SECOND, 3)
    going += [started(s) for s in scatters]

    def weight_steps():
        first = yield from first_coefficients(total01[...])
        while not reduced:
            yield
        n3 = jnp.concatenate([total3[:, : 2 * n], total3[:, 2 * n :]], axis=0)
        return (yield from last_coefficients(first, n3))

    run(going + [marked(weight_steps(), weights)])
    w0, w1, w2 = weights[0]
    for s in range(ROW_COUNT):
        p = table[MINE + s]
        out = (
            tmm(w0, panel_row(panel0, p)) + tmm(w1, panel_row(panel1, p))
        ) + tmm(w2, whole(owed1, s))
        sol[s] = out[: 2 * n]
        res[s] = out[2 * n :]
    net.drain()


def local(rhs, diag, off, coup, col_index, load, new_slot):
    rows, n2, w = rhs.shape
    n = n2 // 2
    vm = pl.BlockSpec(memory_space=pltpu.VMEM)
    sm = pl.BlockSpec(memory_space=pltpu.SMEM)
    anys = pl.BlockSpec(memory_space=pl.ANY)
    table = pl.pallas_call(
        table_kernel,
        out_shape=jax.ShapeDtypeStruct((TABLE,), jnp.int32),
        in_specs=[anys, sm, sm],
        out_specs=sm,
        scratch_shapes=[pltpu.SMEM((rows, off.shape[1]), jnp.int32), pltpu.SemaphoreType.DMA(())],
        name="tables",
    )(col_index, load, new_slot)

    def vmem(*shape):
        return pltpu.VMEM(shape, f32)

    panels = [vmem(2, 2, RING, RING, 4, n, w), vmem(RING, 2, 2, n, w)]
    scatter = [
        vmem(2, rows, n, w),
        vmem(2, RING, RING, 4, n, w),
        vmem(2, RING, RING, 4, n, w),
        vmem(2, RING, RING, 4, n, w),
        vmem(2, 2, RING, 2, n, w),
        vmem(2, 2, RING, 4, n, w),
        vmem(2, 3, 4, n, w),
    ]

    def reduction(m, k):
        return [vmem(m, k), vmem(m, k), vmem(4, m // 2, k), vmem(3, 3, m // 2, k), vmem(m // 2, k)]

    copies = 2 * (2 * 22 + 3 + 2 * 23 + 11)
    scratch = (
        [vmem(2, rows, n, w), vmem(2, rows, n, w), vmem(*diag.shape), vmem(*off.shape), vmem(*coup.shape)]
        + [vmem(OWN + rows, 2, n, w), vmem(rows, n2, w)]
        + panels
        + panels
        + scatter
        + scatter
        + reduction(2 * n2, 2 * n2)
        + reduction(n, 2 * n2)
        + [pltpu.SemaphoreType.DMA((copies,))] * 2
        + [pltpu.SemaphoreType.DMA((6,)), pltpu.SemaphoreType.DMA((5,))]
    )
    return pl.pallas_call(
        fused_kernel,
        out_shape=[jax.ShapeDtypeStruct(rhs.shape, f32)] * 2,
        in_specs=[sm] + [anys] * 4,
        out_specs=[vm, vm],
        scratch_shapes=scratch,
        compiler_params=pltpu.CompilerParams(
            collective_id=0, has_side_effects=True, vmem_limit_bytes=56 << 20
        ),
        name="fused",
    )(table, rhs, diag, off, coup)


def solution(mesh):
    return jax.shard_map(
        local,
        mesh=mesh,
        in_specs=(
            P(("group", "bulk"), None, None),
            P(("group", "bulk"), None, None),
            P(("group", "bulk"), None, None, None),
            P(("group", "bulk"), None, None, None),
            P(),
            P(),
            P(),
        ),
        out_specs=(P(("group", "bulk"), None, None), P(("group", "bulk"), None, None)),
        check_vma=False,
    )
```

time: 131 us -> 112 us (0.85)
  Pallas kernels: 120 us -> 107 us
  local copies, waits for them, and re-layouts: 10.2 us -> 4.73 us
    pallas_call x8 -> x2, Pallas kernels: 120 us -> 107 us  [the longest x1 103 us: local(): pl.pallas_call(fused_kernel, out_shape=[jax.ShapeDtypeStruct(rhs.shape, f...]
    unnamed x29 -> x3, local copies, waits for them, and re-layouts: 9.27 us -> 4.73 us
where the time goes in v4:
time: 112 us
  Pallas kernels  107 us (96%)
  local copies, waits for them, and re-layouts  4.73 us (4%)
    pallas_call x1, Pallas kernels, local(): pl.pallas_call(fused_kernel, out_shape=[jax.ShapeDtypeStruct(rhs.shape, f...  103 us
    unnamed x3, local copies, waits for them, and re-layouts  4.73 us
    pallas_call x1, Pallas kernels, local(): pl.pallas_call(table_kernel, out_shape=jax.ShapeDtypeStruct((TABLE,), jnp...  4.14 us

profile of v4, /device:TPU:1, one launch (start us, length us, event | category | flops | bytes accessed | tf_op | source)
XLA Modules:
  0.0 112.1 jit_solution(17925022580663605030)
XLA Ops:
  0.6 1.6 %copy.9.col_hbm = s32[512,11]{1,0:T(8,128)} copy(s32[512,11]{0,1:T(8,128)} %param.11) | data formatting | bytes 45056 | tf_op args[4]
  2.2 4.1 %tables.1.table = s32[736]{0:T(1024)} custom-call(s32[512,11]{1,0:T(8,128)} %copy.9.col_hbm, s32[512]{0:T(512)} %load.1, s32[512]{0:T(512)} %moved.1), custom_call_target="tpu_custom_call" | custom-call | tf_op jit(solution)/shard_map/tables/pallas_call | solution.py:635
  6.4 102.6 %fused.1 = (f32[4,64,128]{2,1,0:T(8,128)}, f32[4,64,128]{2,1,0:T(8,128)}) custom-call(s32[736]{0:T(1024)} %tables.1.table, f32[4,64,128]{2,1,0:T(8,128)} %rhs.1, f32[4,128,128]{2,1,0:T(8,128)} %diag_in.1, f32[4,11,128,128]{3,2,1,0:T(8,128)} %off_in.1, f32[2,4,128,128]{3,2,1,0:T(8,128)} %coup_in.1), custom_call_target="tpu_custom_call" | custom-call | tf_op jit(solution)/shard_map/fused/pallas_call | solution.py:674
  108.9 1.6 %copy.12 = f32[4,64,128]{2,1,0:T(8,128)} copy(f32[4,64,128]{2,1,0:T(8,128)} %get-tuple-element.4) | data formatting | bytes 262144
  110.5 1.6 %copy.13 = f32[4,64,128]{2,1,0:T(8,128)} copy(f32[4,64,128]{2,1,0:T(8,128)} %get-tuple-element.5) | data formatting | bytes 262144

commit v5 on v4

--- a/solution.py
+++ b/solution.py
@@ -211,7 +211,7 @@
         d.wait_recv()
 
 
-def reduce_steps(net, m, out, acc, slots, halves):
+def reduce_steps(net, m, out, acc, slots, plane_slots, halves):
     c = net.c
     rows = acc.shape[1]
     partner = net.device(partner=True)
@@ -219,36 +219,45 @@
     yield
     d.wait_recv()
     acc[0] = m[pl.ds(c * rows, rows)] + halves[...]
-    for t in range(3):
-        sent = []
-        for k in (1, 3, 2):
-            step = [0, 0, 0]
-            step[t] = k * (1 - c)
-            step[(t + 1) % 3] = step[(t + 1) % 3] + k * c
-            sent.append(
-                net.copy(acc.at[t], slots.at[t, k - 1], net.device(step[0], step[1], step[2]))
-            )
-        yield
-        for d in sent:
-            d.wait_recv()
-        acc[t + 1] = (acc[t] + slots[t, 0]) + (slots[t, 1] + slots[t, 2])
-    out[pl.ds(c * rows, rows)] = acc[3]
-    d = net.copy(acc.at[3], out.at[pl.ds(c * rows, rows)], partner)
+    sent = [net.copy(acc.at[0], slots.at[k - 1], net.device(dx=k)) for k in (1, 3, 2)]
+    yield
+    for d in sent:
+        d.wait_recv()
+    acc[1] = (acc[0] + slots[0]) + (slots[1] + slots[2])
+    sent = [
+        net.copy(acc.at[1], plane_slots.at[k - 1], net.device(dy=k % RING, dz=k // RING))
+        for k in FAR_FIRST
+    ]
+    yield
+    for d in sent:
+        d.wait_recv()
+    terms = [acc[1]] + [plane_slots[k] for k in range(RING * RING - 1)]
+    while len(terms) > 1:
+        terms = [a + b for a, b in zip(terms[::2], terms[1::2])]
+    acc[2] = terms[0]
+    out[pl.ds(c * rows, rows)] = terms[0]
+    d = net.copy(acc.at[2], out.at[pl.ds(c * rows, rows)], partner)
     yield
     d.wait_recv()
 
 
-def run(steps):
-    steps = list(steps)
-    while steps:
-        left = []
+def hops(k):
+    return min(k % RING, RING - k % RING) + min(k // RING, RING - k // RING)
+
+
+FAR_FIRST = sorted(range(1, RING * RING), key=lambda k: -hops(k))
+
+
+def advance(steps, count=1):
+    for _ in range(count):
         for s in steps:
-            try:
-                next(s)
-                left.append(s)
-            except StopIteration:
-                pass
-        steps = left
+            next(s, None)
+
+
+def run(*steps):
+    for s in steps:
+        for _ in s:
+            pass
 
 
 def split(a):
@@ -273,55 +282,8 @@
 PART_ROWS = 128
 NONE = ENTRIES
 OWN = ENTRIES + 1
-FIRST = 0
-SECOND = 2 * PART_ROWS
-PLACE = SECOND + 3 * PART_ROWS
-LIVE = PLACE + ENTRIES
-MINE = LIVE + ENTRIES
-SPARE = MINE + ROW_COUNT
-TABLE = SPARE + 4
-
-
 def position(slot):
     return lax.rem(slot // 4, 2) * 64 + (slot // 8) * 4 + lax.rem(slot, 4)
-
-
-def table_kernel(col_hbm, load, moved, table, cols, sem):
-    first = (lax.axis_index("group") * 32 + lax.axis_index("bulk")) * ROW_COUNT
-    base = lax.axis_index("group") * PART_ROWS
-    d = pltpu.make_async_copy(col_hbm.at[pl.ds(first, ROW_COUNT)], cols, sem)
-    d.start()
-
-    def clear(i, _):
-        for k in range(5):
-            table[k * PART_ROWS + i] = NONE
-        return 0
-
-    lax.fori_loop(0, PART_ROWS, clear, 0)
-    for i in range(SPARE, TABLE):
-        table[i] = NONE
-    d.wait()
-    for s in range(ROW_COUNT):
-        live_count = load[first + s]
-        target = position(moved[first + s] - base)
-        table[SECOND + 2 * PART_ROWS + target] = OWN + s
-        table[MINE + s] = target
-
-        def entry(t, _):
-            e = s * OFFS + t
-            slot = cols[s, t]
-            live = t < live_count
-            p = position(slot - base)
-            q = position(moved[slot] - base)
-            table[PLACE + e] = p
-            table[LIVE + e] = live.astype(jnp.int32)
-            i = FIRST + p + jnp.where(table[FIRST + p] == NONE, 0, PART_ROWS)
-            table[jnp.where(live, i, SPARE)] = e
-            i = SECOND + q + jnp.where(table[SECOND + q] == NONE, 0, PART_ROWS)
-            table[jnp.where(live, i, SPARE)] = e
-            return 0
-
-        lax.fori_loop(0, OFFS, entry, 0)
 
 
 def gram(a, b):
@@ -449,7 +411,7 @@
     )
 
 
-def fused_kernel(table, rhs, diag_in, off_in, coup_in, sol, res, *refs):
+def fused_kernel(cols, load, moved, rhs, diag_in, off_in, coup_in, weights_out, basis, *refs):
     refs = iter(refs)
 
     def take(count):
@@ -462,11 +424,11 @@
     owed1, stage1, r1 = take(3)
     parts1 = take(4)
     g01, total01 = take(2)
-    work01 = take(3)
+    work01 = take(4)
     g3, total3 = take(2)
-    work3 = take(3)
-    send, recv, local_sems, in_sems = take(4)
-    n = u0.shape[2]
+    work3 = take(4)
+    index, table, send, recv, local_sems, in_sems = take(6)
+    n, w = u0.shape[2:]
     net = Net(send, recv)
     c = net.c
     loads = [
@@ -477,17 +439,40 @@
     ]
     for d in loads:
         d.start()
-    greet(
-        net,
-        [net.device(partner=True)]
-        + [net.device(dy=k) for k in (2, 1, 3)]
-        + [net.device(dz=k) for k in (2, 1, 3)]
-        + [net.device(dx=k) for k in (2, 1, 3)],
-    )
+    barrier = pltpu.get_barrier_semaphore()
+    greeted = [net.device(partner=True)] + [net.device(dx=k) for k in (2, 1, 3)]
+    greeted += [net.device(dy=k % RING, dz=k // RING) for k in FAR_FIRST]
+    for d in greeted:
+        pl.semaphore_signal(barrier, inc=1, device_id=d, device_id_type=MESH)
+    first = (net.g * 32 + lax.axis_index("bulk")) * ROW_COUNT
+
+    lane = lax.broadcasted_iota(jnp.int32, (1, PART_ROWS), 1)
+    tops = [jnp.full((1, PART_ROWS), -1, jnp.int32)] * 2
+    lows = [jnp.full((1, PART_ROWS), NONE + 1, jnp.int32)] * 2
+    own_row = jnp.full((1, PART_ROWS), NONE, jnp.int32)
+    mine = []
+    for s in range(ROW_COUNT):
+        count = load[first + s]
+        mine.append(position(lax.rem(moved[first + s], PART_ROWS)))
+        own_row = jnp.where(lane == mine[s], OWN + s, own_row)
+        for t in range(OFFS):
+            e = s * OFFS + t
+            slot = cols[t, first + s]
+            for i, p in enumerate((position(lax.rem(slot, PART_ROWS)), position(lax.rem(moved[slot], PART_ROWS)))):
+                hit = lane == jnp.where(t < count, p, -1)
+                tops[i] = jnp.where(hit, e, tops[i])
+                lows[i] = jnp.where(hit, jnp.minimum(lows[i], e), lows[i])
+    for i in range(2):
+        index[2 * i : 2 * i + 1] = jnp.where(tops[i] < 0, NONE, tops[i])
+        index[2 * i + 1 : 2 * i + 2] = jnp.where(lows[i] == tops[i], NONE, jnp.minimum(lows[i], NONE))
+    index[4:5] = own_row
+    index[5:8] = jnp.full((3, PART_ROWS), NONE, jnp.int32)
+    indexed = pltpu.make_async_copy(index, table, in_sems.at[5])
+    indexed.start()
     for k in range(NONE, products.shape[0]):
         products[k] = jnp.zeros(products.shape[1:], f32)
 
-    def returned(u):
+    def returned(u, begin, end):
         def row(s, _):
             v = split(whole(u, s))
             for t in range(OFFS):
@@ -496,14 +481,14 @@
                 products[s * OFFS + t, 1] = p[n:]
             return 0
 
-        lax.fori_loop(0, ROW_COUNT, row, 0)
+        lax.fori_loop(begin, end, row, 0)
 
     def fill(dst, core, start, count):
         def plane(z, _):
             for y in range(RING):
                 for k in range(4):
                     p = core * 64 + (z * RING + y) * 4 + k
-                    es = [table[start + i * PART_ROWS + p] for i in range(count)]
+                    es = [table[start + i, p] for i in range(count)]
                     for j in range(2):
                         v = products[es[0], j]
                         for e in es[1:]:
@@ -523,107 +508,132 @@
     def tiles_of(panel, s):
         out = None
         for t in range(OFFS):
-            e = s * OFFS + t
-            live = table[LIVE + e].astype(f32)
-            v = panel_row(panel, table[PLACE + e]) * live
+            live = (t < load[first + s]).astype(f32)
+            v = panel_row(panel, position(lax.rem(cols[t, first + s], PART_ROWS))) * live
             p = dot3(split(v), split(off[s, t]), ROWS)
             out = p if out is None else out + p
         return out
 
-    def rest_steps(u, border, border_done):
+    def set_rest(u):
         for s in range(ROW_COUNT):
             part[s] = dot3(split(whole(u, s)), split(diag[s]), ROWS)
-        while not border_done:
-            yield
+
+    def add_crossed(border):
         for s in range(coup.shape[0]):
             part[s] = part[s] + crossed(border, s)
-            yield
-
-    def marked(steps, mark):
-        out = yield from steps
-        mark.append(out)
-
-    def started(steps):
-        next(steps)
-        return steps
-
+
+    loads[2].wait()
     loads[0].wait()
     loads[1].wait()
-    got_panel, got_border = [], []
-    going = [
-        started(marked(gather_steps(net, j, u0, panel0, local_sems.at[j]), got_panel))
-        for j in range(2)
-    ]
-    going.append(started(marked(border_steps(net, u0, border0, local_sems.at[2]), got_border)))
-    for d in loads[2:]:
-        d.wait()
-    returned(u0)
-    fill(stage0, 1 - c, FIRST, 2)
+    returned(u0, 0, ROW_COUNT // 2)
+    pl.semaphore_wait(barrier, len(greeted))
+    gathers = [gather_steps(net, j, u0, panel0, local_sems.at[j]) for j in range(2)]
+    borders = border_steps(net, u0, border0, local_sems.at[2])
+    advance(gathers)
+    advance([borders])
+    returned(u0, ROW_COUNT // 2, ROW_COUNT)
+    indexed.wait()
+    fill(stage0, 1 - c, 0, 2)
     scatters = [scatter_steps(net, j, owed0, stage0, r0, *parts0) for j in range(2)]
-    fill(r0, c, FIRST, 2)
-    scatters = [started(s) for s in scatters]
-
-    def forward_steps():
-        yield from rest_steps(u0, border0, got_border)
-        while len(got_panel) < 2:
-            yield
-        for s in range(ROW_COUNT):
-            part[s] = part[s] + tiles_of(panel0, s)
-            yield
-
-    run(scatters + going + [forward_steps()])
+    fill(r0, c, 0, 2)
+    advance(scatters)
+    advance(gathers, 2)
+    advance(scatters)
+    advance(gathers, 2)
+    advance(scatters, 3)
+    run(borders)
+    loads[3].wait()
+    loads[4].wait()
+    advance(gathers, 2)
+    advance(scatters, 4)
+    set_rest(u0)
+    add_crossed(border0)
+    advance(gathers, 2)
+    advance(scatters, 2)
+    run(*gathers)
+    for s in range(ROW_COUNT):
+        part[s] = part[s] + tiles_of(panel0, s)
+        if s % 2 == 0:
+            advance(scatters)
+    run(*scatters)
     for s in range(ROW_COUNT):
         for j in range(2):
             u1[j, s] = part[s, j * n : (j + 1) * n] + owed0[j, s]
 
-    got_panel, got_border = [], []
-    going = [
-        started(marked(gather_steps(net, j, u1, panel1, local_sems.at[3 + j]), got_panel))
-        for j in range(2)
-    ]
-    going.append(started(marked(border_steps(net, u1, border1, local_sems.at[5]), got_border)))
-    total = None
+    gathers = [gather_steps(net, j, u1, panel1, local_sems.at[3 + j]) for j in range(2)]
+    borders = border_steps(net, u1, border1, local_sems.at[5])
+    advance(gathers)
+    advance([borders])
+    x = [jnp.concatenate([whole(u0, s), whole(u1, s)], axis=0) for s in range(ROW_COUNT)]
+    x = jnp.concatenate(x, axis=1)
+    g01[...] = gram(x, x)
+    sums = reduce_steps(net, g01, total01, *work01)
+    advance([sums])
+    returned(u1, 0, ROW_COUNT)
+    advance(gathers, 2)
+    advance([sums])
+    advance(gathers, 2)
+    run(borders)
+    set_rest(u1)
+    add_crossed(border1)
+    advance(gathers, 1)
+    advance([sums])
+    advance(gathers, 3)
     for s in range(ROW_COUNT):
-        x = jnp.concatenate([whole(u0, s), whole(u1, s)], axis=0)
-        total = gram(x, x) if total is None else total + gram(x, x)
-    g01[...] = total
-    going.append(started(reduce_steps(net, g01, total01, *work01)))
-    returned(u1)
-    run(going + [rest_steps(u1, border1, got_border)])
+        basis[0 : 2 * n, s * w : (s + 1) * w] = panel_row(panel0, mine[s])
+    advance([sums])
+    run(*gathers)
+    run(sums)
 
     def second_row(s, total):
         tiles = tiles_of(panel1, s)
-        w = tiles + part[s]
-        products[OWN + s, 0] = w[:n]
-        products[OWN + s, 1] = w[n:]
-        return total + gram(whole(u1, s), w + tiles)
+        v = tiles + part[s]
+        products[OWN + s, 0] = v[:n]
+        products[OWN + s, 1] = v[n:]
+        return total + gram(whole(u1, s), v + tiles)
 
     total = lax.fori_loop(0, ROW_COUNT, second_row, jnp.zeros((2 * n, 2 * n), f32))
     g3[...] = jnp.concatenate([total[:n], total[n:]], axis=1)
-    known, reduced, weights, scattered = [], [], [], []
-    going = [started(marked(reduce_steps(net, g3, total3, *work3), reduced))]
-    fill(stage1, 1 - c, SECOND, 3)
-    scatters = [marked(scatter_steps(net, j, owed1, stage1, r1, *parts1), scattered) for j in range(2)]
-    fill(r1, c, SECOND, 3)
-    going += [started(s) for s in scatters]
-
-    def weight_steps():
-        first = yield from first_coefficients(total01[...])
-        while not reduced:
-            yield
-        n3 = jnp.concatenate([total3[:, : 2 * n], total3[:, 2 * n :]], axis=0)
-        return (yield from last_coefficients(first, n3))
-
-    run(going + [marked(weight_steps(), weights)])
-    w0, w1, w2 = weights[0]
+    sums = reduce_steps(net, g3, total3, *work3)
+    advance([sums])
+    fill(stage1, 1 - c, 2, 3)
+    scatters = [scatter_steps(net, j, owed1, stage1, r1, *parts1) for j in range(2)]
+    fill(r1, c, 2, 3)
+    advance(scatters)
+    advance([sums])
+    advance(scatters)
+    solving = both(first_coefficients(total01[...]))
+    advance([solving], 5)
+    advance([sums])
+    advance(scatters, 3)
+    advance([solving], 2)
+    advance(scatters, 4)
     for s in range(ROW_COUNT):
-        p = table[MINE + s]
-        out = (
-            tmm(w0, panel_row(panel0, p)) + tmm(w1, panel_row(panel1, p))
-        ) + tmm(w2, whole(owed1, s))
-        sol[s] = out[: 2 * n]
-        res[s] = out[2 * n :]
+        basis[2 * n : 4 * n, s * w : (s + 1) * w] = panel_row(panel1, mine[s])
+    known = finish(solving)[0]
+    advance(scatters, 1)
+    run(sums)
+    n3 = jnp.concatenate([total3[:, : 2 * n], total3[:, 2 * n :]], axis=0)
+    solving = both(last_coefficients(known, n3))
+    for _ in range(3):
+        advance([solving], 3)
+        advance(scatters)
+    weights = finish(solving)[0]
+    for i in range(3):
+        weights_out[2 * n * i : 2 * n * (i + 1)] = weights[i]
+    run(*scatters)
+    for s in range(ROW_COUNT):
+        basis[4 * n :, s * w : (s + 1) * w] = whole(owed1, s)
     net.drain()
+
+
+def last_kernel(weights, basis, sol, res):
+    n = sol.shape[1]
+    w = sol.shape[2]
+    out = tmm(weights[...], basis[...])
+    for s in range(sol.shape[0]):
+        sol[s] = out[:n, s * w : (s + 1) * w]
+        res[s] = out[n:, s * w : (s + 1) * w]
 
 
 def local(rhs, diag, off, coup, col_index, load, new_slot):
@@ -632,15 +642,6 @@
     vm = pl.BlockSpec(memory_space=pltpu.VMEM)
     sm = pl.BlockSpec(memory_space=pltpu.SMEM)
     anys = pl.BlockSpec(memory_space=pl.ANY)
-    table = pl.pallas_call(
-        table_kernel,
-        out_shape=jax.ShapeDtypeStruct((TABLE,), jnp.int32),
-        in_specs=[anys, sm, sm],
-        out_specs=sm,
-        scratch_shapes=[pltpu.SMEM((rows, off.shape[1]), jnp.int32), pltpu.SemaphoreType.DMA(())],
-        name="tables",
-    )(col_index, load, new_slot)
-
     def vmem(*shape):
         return pltpu.VMEM(shape, f32)
 
@@ -656,9 +657,13 @@
     ]
 
     def reduction(m, k):
-        return [vmem(m, k), vmem(m, k), vmem(4, m // 2, k), vmem(3, 3, m // 2, k), vmem(m // 2, k)]
-
-    copies = 2 * (2 * 22 + 3 + 2 * 23 + 11)
+        half = m // 2
+        return [vmem(m, k), vmem(m, k), vmem(3, half, k), vmem(3, half, k)] + [
+            vmem(RING * RING - 1, half, k),
+            vmem(half, k),
+        ]
+
+    copies = 2 * (2 * 22 + 3 + 2 * 23 + 20)
     scratch = (
         [vmem(2, rows, n, w), vmem(2, rows, n, w), vmem(*diag.shape), vmem(*off.shape), vmem(*coup.shape)]
         + [vmem(OWN + rows, 2, n, w), vmem(rows, n2, w)]
@@ -668,20 +673,31 @@
         + scatter
         + reduction(2 * n2, 2 * n2)
         + reduction(n, 2 * n2)
+        + [pltpu.VMEM((8, PART_ROWS), jnp.int32), pltpu.SMEM((8, PART_ROWS), jnp.int32)]
         + [pltpu.SemaphoreType.DMA((copies,))] * 2
-        + [pltpu.SemaphoreType.DMA((6,)), pltpu.SemaphoreType.DMA((5,))]
+        + [pltpu.SemaphoreType.DMA((6,)), pltpu.SemaphoreType.DMA((6,))]
     )
-    return pl.pallas_call(
+    weights, basis = pl.pallas_call(
         fused_kernel,
-        out_shape=[jax.ShapeDtypeStruct(rhs.shape, f32)] * 2,
-        in_specs=[sm] + [anys] * 4,
+        out_shape=[
+            jax.ShapeDtypeStruct((3 * n2, 2 * n2), f32),
+            jax.ShapeDtypeStruct((3 * n2, rows * w), f32),
+        ],
+        in_specs=[sm] * 3 + [anys] * 4,
         out_specs=[vm, vm],
         scratch_shapes=scratch,
         compiler_params=pltpu.CompilerParams(
             collective_id=0, has_side_effects=True, vmem_limit_bytes=56 << 20
         ),
         name="fused",
-    )(table, rhs, diag, off, coup)
+    )(col_index.T, load, new_slot, rhs, diag, off, coup)
+    return pl.pallas_call(
+        last_kernel,
+        out_shape=[jax.ShapeDtypeStruct(rhs.shape, f32)] * 2,
+        in_specs=[vm, vm],
+        out_specs=[vm, vm],
+        name="last",
+    )(weights, basis)
 
 
 def solution(mesh):

time: 112 us -> 92.6 us (0.83)
  Pallas kernels: 107 us -> 91.7 us
  local copies, waits for them, and re-layouts: 4.73 us -> 0 us
    pallas_call x2, Pallas kernels: 107 us -> 91.7 us  [the longest x1 89.5 us: local(): pl.pallas_call(fused_kernel, out_shape=[jax.ShapeDtypeStruct((3 * n2, 2 *...]
    unnamed x3 -> x0, local copies, waits for them, and re-layouts: 4.73 us -> none
where the time goes in v5:
time: 92.6 us; the launch traced here: 92.3 us
  Pallas kernels  91.7 us (99%)
    pallas_call x1, Pallas kernels, local(): pl.pallas_call(fused_kernel, out_shape=[jax.ShapeDtypeStruct((3 * n2, 2 *...  89.5 us
    pallas_call x1, Pallas kernels, local(): pl.pallas_call(last_kernel, out_shape=[jax.ShapeDtypeStruct(rhs.shape, f3...  2.15 us

profile of v5, /device:TPU:1, one launch (start us, length us, event | category | flops | bytes accessed | tf_op | source)
XLA Modules:
  0.0 92.3 jit_solution(7323079719606042160)
XLA Ops:
  0.6 89.5 %fused.1 = (f32[192,128]{1,0:T(8,128)}, f32[192,512]{1,0:T(8,128)}) custom-call(s32[11,512]{1,0:T(8,128)} %bitcast.1, s32[512]{0:T(512)} %load.1, s32[512]{0:T(512)} %moved.1, f32[4,64,128]{2,1,0:T(8,128)} %rhs.1, f32[4,128,128]{2,1,0:T(8,128)} %diag_in.1, f32[4,11,128,128]{3,2,1,0:T(8,128)} %off_in.1, f32[2,4,128,128]{3,2,1,0:T(8,128)} %coup_in.1), custom_call_target="tpu_custom_call" | custom-call | tf_op jit(solution)/shard_map/fused/pallas_call | solution.py:680
  90.2 2.2 %last.1 = (f32[4,64,128]{2,1,0:T(8,128)}, f32[4,64,128]{2,1,0:T(8,128)}) custom-call(f32[192,128]{1,0:T(8,128)} %get-tuple-element.4.weights, f32[192,512]{1,0:T(8,128)} %get-tuple-element.5.basis), custom_call_target="tpu_custom_call" | custom-call | tf_op jit(solution)/shard_map/last/pallas_call | solution.py:694

commit v6 on v5

--- a/solution.py
+++ b/solution.py
@@ -154,6 +154,8 @@
     first = {}
     for k in order:
         first[k] = net.copy(column(stage, k), column(t0, k), partner)
+        if k == 2:
+            yield
     cols = {k: column(r, k) for k in range(RING)}
 
     def start(k):
@@ -211,6 +213,33 @@
         d.wait_recv()
 
 
+def axis_reduce_steps(net, m, out, acc, slots, halves):
+    c = net.c
+    rows = acc.shape[1]
+    partner = net.device(partner=True)
+    d = net.copy(m.at[pl.ds((1 - c) * rows, rows)], halves, partner)
+    yield
+    d.wait_recv()
+    acc[0] = m[pl.ds(c * rows, rows)] + halves[...]
+    for t in range(3):
+        sent = []
+        for k in (1, 3, 2):
+            step = [0, 0, 0]
+            step[t] = k * (1 - c)
+            step[(t + 1) % 3] = step[(t + 1) % 3] + k * c
+            sent.append(
+                net.copy(acc.at[t], slots.at[t, k - 1], net.device(step[0], step[1], step[2]))
+            )
+        yield
+        for d in sent:
+            d.wait_recv()
+        acc[t + 1] = (acc[t] + slots[t, 0]) + (slots[t, 1] + slots[t, 2])
+    out[pl.ds(c * rows, rows)] = acc[3]
+    d = net.copy(acc.at[3], out.at[pl.ds(c * rows, rows)], partner)
+    yield
+    d.wait_recv()
+
+
 def reduce_steps(net, m, out, acc, slots, plane_slots, halves):
     c = net.c
     rows = acc.shape[1]
@@ -266,10 +295,15 @@
 
 
 def dot3(a, b, dims):
-    dot = functools.partial(
-        lax.dot_general, dimension_numbers=(dims, ((), ())), preferred_element_type=f32
+    axis = dims[1][0]
+    left = [x[i] for i in (0, 1, 0) for x in a]
+    right = [x[i] for i in (0, 0, 1) for x in b]
+    return lax.dot_general(
+        jnp.concatenate(left, axis=1),
+        jnp.concatenate(right, axis=axis),
+        (dims, ((), ())),
+        preferred_element_type=f32,
     )
-    return dot(a[0], b[0]) + (dot(a[0], b[1]) + dot(a[1], b[0]))
 
 
 ROWS = ((1,), (1,))
@@ -282,10 +316,6 @@
 PART_ROWS = 128
 NONE = ENTRIES
 OWN = ENTRIES + 1
-def position(slot):
-    return lax.rem(slot // 4, 2) * 64 + (slot // 8) * 4 + lax.rem(slot, 4)
-
-
 def gram(a, b):
     return lax.dot_general(a, b, (ROWS, ((), ())), precision=highest, preferred_element_type=f32)
 
@@ -294,9 +324,12 @@
     return jnp.concatenate([ref[(0,) + idx], ref[(1,) + idx]], axis=0)
 
 
-def panel_row(panel, p):
-    c, z = p // 64, lax.rem(p // 16, RING)
-    y, k = lax.rem(p // 4, RING), lax.rem(p, 4)
+def bits(a, low, mask):
+    return jnp.bitwise_and(lax.shift_right_logical(a, low), mask)
+
+
+def panel_row(panel, slot):
+    c, z, y, k = bits(slot, 2, 1), bits(slot, 5, 3), bits(slot, 3, 3), bits(slot, 0, 3)
     return jnp.concatenate([panel[c, 0, z, y, k], panel[c, 1, z, y, k]], axis=0)
 
 
@@ -424,7 +457,7 @@
     owed1, stage1, r1 = take(3)
     parts1 = take(4)
     g01, total01 = take(2)
-    work01 = take(4)
+    work01 = take(3)
     g3, total3 = take(2)
     work3 = take(4)
     index, table, send, recv, local_sems, in_sems = take(6)
@@ -447,19 +480,20 @@
     first = (net.g * 32 + lax.axis_index("bulk")) * ROW_COUNT
 
     lane = lax.broadcasted_iota(jnp.int32, (1, PART_ROWS), 1)
+    lane = bits(lane, 6, 1) * 4 + bits(lane, 2, 15) * 8 + bits(lane, 0, 3)
     tops = [jnp.full((1, PART_ROWS), -1, jnp.int32)] * 2
     lows = [jnp.full((1, PART_ROWS), NONE + 1, jnp.int32)] * 2
     own_row = jnp.full((1, PART_ROWS), NONE, jnp.int32)
     mine = []
     for s in range(ROW_COUNT):
         count = load[first + s]
-        mine.append(position(lax.rem(moved[first + s], PART_ROWS)))
-        own_row = jnp.where(lane == mine[s], OWN + s, own_row)
+        mine.append(moved[first + s])
+        own_row = jnp.where(lane == bits(mine[s], 0, PART_ROWS - 1), OWN + s, own_row)
         for t in range(OFFS):
             e = s * OFFS + t
             slot = cols[t, first + s]
-            for i, p in enumerate((position(lax.rem(slot, PART_ROWS)), position(lax.rem(moved[slot], PART_ROWS)))):
-                hit = lane == jnp.where(t < count, p, -1)
+            for i, p in enumerate((slot, moved[slot])):
+                hit = lane == jnp.where(t < count, bits(p, 0, PART_ROWS - 1), -1)
                 tops[i] = jnp.where(hit, e, tops[i])
                 lows[i] = jnp.where(hit, jnp.minimum(lows[i], e), lows[i])
     for i in range(2):
@@ -476,7 +510,7 @@
         def row(s, _):
             v = split(whole(u, s))
             for t in range(OFFS):
-                p = dot3(v, split(off[s, t]), COLS)
+                p = dot3([v], [split(off[s, t])], COLS)
                 products[s * OFFS + t, 0] = p[:n]
                 products[s * OFFS + t, 1] = p[n:]
             return 0
@@ -499,47 +533,42 @@
         lax.fori_loop(0, RING, plane, 0)
 
     def crossed(border, s):
-        out = None
-        for h in range(RING):
-            p = dot3(split(jnp.concatenate([border[h, 0, s], border[h, 1, s]], axis=0)), split(coup[s, h]), ROWS)
-            out = p if out is None else out + p
-        return out
+        v = [split(jnp.concatenate([border[h, 0, s], border[h, 1, s]], axis=0)) for h in range(RING)]
+        return dot3(v, [split(coup[s, h]) for h in range(RING)], ROWS)
 
     def tiles_of(panel, s):
-        out = None
+        v = []
         for t in range(OFFS):
             live = (t < load[first + s]).astype(f32)
-            v = panel_row(panel, position(lax.rem(cols[t, first + s], PART_ROWS))) * live
-            p = dot3(split(v), split(off[s, t]), ROWS)
-            out = p if out is None else out + p
-        return out
+            v.append(split(panel_row(panel, cols[t, first + s]) * live))
+        return dot3(v, [split(off[s, t]) for t in range(OFFS)], ROWS)
 
     def set_rest(u):
         for s in range(ROW_COUNT):
-            part[s] = dot3(split(whole(u, s)), split(diag[s]), ROWS)
+            part[s] = dot3([split(whole(u, s))], [split(diag[s])], ROWS)
 
     def add_crossed(border):
         for s in range(coup.shape[0]):
             part[s] = part[s] + crossed(border, s)
 
-    loads[2].wait()
     loads[0].wait()
     loads[1].wait()
-    returned(u0, 0, ROW_COUNT // 2)
     pl.semaphore_wait(barrier, len(greeted))
     gathers = [gather_steps(net, j, u0, panel0, local_sems.at[j]) for j in range(2)]
     borders = border_steps(net, u0, border0, local_sems.at[2])
     advance(gathers)
     advance([borders])
-    returned(u0, ROW_COUNT // 2, ROW_COUNT)
+    loads[2].wait()
+    returned(u0, 0, ROW_COUNT)
     indexed.wait()
     fill(stage0, 1 - c, 0, 2)
     scatters = [scatter_steps(net, j, owed0, stage0, r0, *parts0) for j in range(2)]
+    advance(scatters, 2)
+    advance(gathers, 2)
     fill(r0, c, 0, 2)
+    advance(gathers)
     advance(scatters)
-    advance(gathers, 2)
-    advance(scatters)
-    advance(gathers, 2)
+    advance(gathers)
     advance(scatters, 3)
     run(borders)
     loads[3].wait()
@@ -549,11 +578,11 @@
     set_rest(u0)
     add_crossed(border0)
     advance(gathers, 2)
-    advance(scatters, 2)
+    advance(scatters, 1)
     run(*gathers)
     for s in range(ROW_COUNT):
         part[s] = part[s] + tiles_of(panel0, s)
-        if s % 2 == 0:
+        if s < 3:
             advance(scatters)
     run(*scatters)
     for s in range(ROW_COUNT):
@@ -567,23 +596,27 @@
     x = [jnp.concatenate([whole(u0, s), whole(u1, s)], axis=0) for s in range(ROW_COUNT)]
     x = jnp.concatenate(x, axis=1)
     g01[...] = gram(x, x)
-    sums = reduce_steps(net, g01, total01, *work01)
+    sums = axis_reduce_steps(net, g01, total01, *work01)
     advance([sums])
-    returned(u1, 0, ROW_COUNT)
+    returned(u1, 0, 2)
     advance(gathers, 2)
     advance([sums])
-    advance(gathers, 2)
+    advance(gathers, 1)
+    returned(u1, 2, 3)
+    advance(gathers, 1)
+    returned(u1, 3, 4)
+    advance(gathers, 1)
     run(borders)
+    advance(gathers, 1)
+    advance([sums])
     set_rest(u1)
     add_crossed(border1)
-    advance(gathers, 1)
-    advance([sums])
-    advance(gathers, 3)
     for s in range(ROW_COUNT):
         basis[0 : 2 * n, s * w : (s + 1) * w] = panel_row(panel0, mine[s])
+    advance(gathers, 2)
     advance([sums])
+    advance(gathers, 1)
     run(*gathers)
-    run(sums)
 
     def second_row(s, total):
         tiles = tiles_of(panel1, s)
@@ -594,14 +627,17 @@
 
     total = lax.fori_loop(0, ROW_COUNT, second_row, jnp.zeros((2 * n, 2 * n), f32))
     g3[...] = jnp.concatenate([total[:n], total[n:]], axis=1)
+    early = sums
     sums = reduce_steps(net, g3, total3, *work3)
     advance([sums])
+    advance([early])
     fill(stage1, 1 - c, 2, 3)
     scatters = [scatter_steps(net, j, owed1, stage1, r1, *parts1) for j in range(2)]
+    advance(scatters, 2)
+    advance([sums])
     fill(r1, c, 2, 3)
     advance(scatters)
-    advance([sums])
-    advance(scatters)
+    run(early)
     solving = both(first_coefficients(total01[...]))
     advance([solving], 5)
     advance([sums])
@@ -656,6 +692,10 @@
         vmem(2, 3, 4, n, w),
     ]
 
+    def axis_reduction(m, k):
+        half = m // 2
+        return [vmem(m, k), vmem(m, k), vmem(4, half, k), vmem(3, 3, half, k), vmem(half, k)]
+
     def reduction(m, k):
         half = m // 2
         return [vmem(m, k), vmem(m, k), vmem(3, half, k), vmem(3, half, k)] + [
@@ -671,7 +711,7 @@
         + panels
         + scatter
         + scatter
-        + reduction(2 * n2, 2 * n2)
+        + axis_reduction(2 * n2, 2 * n2)
         + reduction(n, 2 * n2)
         + [pltpu.VMEM((8, PART_ROWS), jnp.int32), pltpu.SMEM((8, PART_ROWS), jnp.int32)]
         + [pltpu.SemaphoreType.DMA((copies,))] * 2

time: 92.6 us -> 84.6 us (0.914)
  Pallas kernels: 91.7 us -> 83.7 us
    pallas_call x1, Pallas kernels: 89.5 us -> 81.5 us  [local(): pl.pallas_call(fused_kernel, out_shape=[jax.ShapeDtypeStruct((3 * n2, 2 *...]
where the time goes in v6:
time: 84.6 us; the launch traced here: 84.3 us
  Pallas kernels  83.7 us (99%)
    pallas_call x1, Pallas kernels, local(): pl.pallas_call(fused_kernel, out_shape=[jax.ShapeDtypeStruct((3 * n2, 2 *...  81.5 us
    pallas_call x1, Pallas kernels, local(): pl.pallas_call(last_kernel, out_shape=[jax.ShapeDtypeStruct(rhs.shape, f3...  2.16 us

profile of v6, /device:TPU:1, one launch (start us, length us, event | category | flops | bytes accessed | tf_op | source)
XLA Modules:
  0.0 84.3 jit_solution(6997741690887417167)
XLA Ops:
  0.6 81.5 %fused.1 = (f32[192,128]{1,0:T(8,128)}, f32[192,512]{1,0:T(8,128)}) custom-call(s32[11,512]{1,0:T(8,128)} %bitcast.1, s32[512]{0:T(512)} %load.1, s32[512]{0:T(512)} %moved.1, f32[4,64,128]{2,1,0:T(8,128)} %rhs.1, f32[4,128,128]{2,1,0:T(8,128)} %diag_in.1, f32[4,11,128,128]{3,2,1,0:T(8,128)} %off_in.1, f32[2,4,128,128]{3,2,1,0:T(8,128)} %coup_in.1), custom_call_target="tpu_custom_call" | custom-call | tf_op jit(solution)/shard_map/fused/pallas_call | solution.py:720
  82.2 2.2 %last.1 = (f32[4,64,128]{2,1,0:T(8,128)}, f32[4,64,128]{2,1,0:T(8,128)}) custom-call(f32[192,128]{1,0:T(8,128)} %get-tuple-element.4.weights, f32[192,512]{1,0:T(8,128)} %get-tuple-element.5.basis), custom_call_target="tpu_custom_call" | custom-call | tf_op jit(solution)/shard_map/last/pallas_call | solution.py:734

commit v7 on v6

--- a/solution.py
+++ b/solution.py
@@ -444,7 +444,7 @@
     )
 
 
-def fused_kernel(cols, load, moved, rhs, diag_in, off_in, coup_in, weights_out, basis, *refs):
+def fused_kernel(cols_in, load_in, moved_in, rhs, diag_in, off_in, coup_in, weights_out, basis, *refs):
     refs = iter(refs)
 
     def take(count):
@@ -460,10 +460,21 @@
     work01 = take(3)
     g3, total3 = take(2)
     work3 = take(4)
-    index, table, send, recv, local_sems, in_sems = take(6)
+    cols, load, moved, index, table, send, recv, local_sems, in_sems = take(9)
     n, w = u0.shape[2:]
     net = Net(send, recv)
     c = net.c
+    barrier = pltpu.get_barrier_semaphore()
+    greeted = [net.device(partner=True)] + [net.device(dx=k) for k in (2, 1, 3)]
+    greeted += [net.device(dy=k) for k in (2, 1, 3)] + [net.device(dz=k) for k in (2, 1, 3)]
+    for d in greeted:
+        pl.semaphore_signal(barrier, inc=1, device_id=d, device_id_type=MESH)
+    small = [
+        pltpu.make_async_copy(a, b, in_sems.at[6 + i])
+        for i, (a, b) in enumerate(((cols_in, cols), (load_in, load), (moved_in, moved)))
+    ]
+    for d in small:
+        d.start()
     loads = [
         pltpu.make_async_copy(rhs.at[:, pl.ds(j * n, n)], u0.at[j], in_sems.at[j]) for j in range(2)
     ] + [
@@ -472,13 +483,10 @@
     ]
     for d in loads:
         d.start()
-    barrier = pltpu.get_barrier_semaphore()
-    greeted = [net.device(partner=True)] + [net.device(dx=k) for k in (2, 1, 3)]
-    greeted += [net.device(dy=k % RING, dz=k // RING) for k in FAR_FIRST]
-    for d in greeted:
-        pl.semaphore_signal(barrier, inc=1, device_id=d, device_id_type=MESH)
     first = (net.g * 32 + lax.axis_index("bulk")) * ROW_COUNT
 
+    for d in small:
+        d.wait()
     lane = lax.broadcasted_iota(jnp.int32, (1, PART_ROWS), 1)
     lane = bits(lane, 6, 1) * 4 + bits(lane, 2, 15) * 8 + bits(lane, 0, 3)
     tops = [jnp.full((1, PART_ROWS), -1, jnp.int32)] * 2
@@ -564,26 +572,24 @@
     fill(stage0, 1 - c, 0, 2)
     scatters = [scatter_steps(net, j, owed0, stage0, r0, *parts0) for j in range(2)]
     advance(scatters, 2)
+    fill(r0, c, 0, 2)
+    advance(scatters)
+    advance(gathers, 3)
+    advance(scatters, 3)
+    advance(gathers)
+    advance(scatters, 4)
     advance(gathers, 2)
-    fill(r0, c, 0, 2)
-    advance(gathers)
-    advance(scatters)
-    advance(gathers)
-    advance(scatters, 3)
-    run(borders)
     loads[3].wait()
     loads[4].wait()
+    set_rest(u0)
+    run(borders)
+    add_crossed(border0)
+    advance(scatters, 2)
     advance(gathers, 2)
-    advance(scatters, 4)
-    set_rest(u0)
-    add_crossed(border0)
-    advance(gathers, 2)
-    advance(scatters, 1)
+    advance(scatters, 2)
     run(*gathers)
     for s in range(ROW_COUNT):
         part[s] = part[s] + tiles_of(panel0, s)
-        if s < 3:
-            advance(scatters)
     run(*scatters)
     for s in range(ROW_COUNT):
         for j in range(2):
@@ -676,7 +682,6 @@
     rows, n2, w = rhs.shape
     n = n2 // 2
     vm = pl.BlockSpec(memory_space=pltpu.VMEM)
-    sm = pl.BlockSpec(memory_space=pltpu.SMEM)
     anys = pl.BlockSpec(memory_space=pl.ANY)
     def vmem(*shape):
         return pltpu.VMEM(shape, f32)
@@ -713,9 +718,10 @@
         + scatter
         + axis_reduction(2 * n2, 2 * n2)
         + reduction(n, 2 * n2)
+        + [pltpu.SMEM(a.shape, jnp.int32) for a in (col_index.T, load, new_slot)]
         + [pltpu.VMEM((8, PART_ROWS), jnp.int32), pltpu.SMEM((8, PART_ROWS), jnp.int32)]
         + [pltpu.SemaphoreType.DMA((copies,))] * 2
-        + [pltpu.SemaphoreType.DMA((6,)), pltpu.SemaphoreType.DMA((6,))]
+        + [pltpu.SemaphoreType.DMA((6,)), pltpu.SemaphoreType.DMA((9,))]
     )
     weights, basis = pl.pallas_call(
         fused_kernel,
@@ -723,7 +729,7 @@
             jax.ShapeDtypeStruct((3 * n2, 2 * n2), f32),
             jax.ShapeDtypeStruct((3 * n2, rows * w), f32),
         ],
-        in_specs=[sm] * 3 + [anys] * 4,
+        in_specs=[anys] * 7,
         out_specs=[vm, vm],
         scratch_shapes=scratch,
         compiler_params=pltpu.CompilerParams(

time: 84.6 us -> 82.5 us (0.975)
  Pallas kernels: 83.7 us -> 81.7 us
    pallas_call x1, Pallas kernels: 81.5 us -> 79.5 us  [local(): pl.pallas_call(fused_kernel, out_shape=[jax.ShapeDtypeStruct((3 * n2, 2 *...]
where the time goes in v7:
time: 82.5 us; the launch traced here: 82.3 us
  Pallas kernels  81.7 us (99%)
    pallas_call x1, Pallas kernels, local(): pl.pallas_call(fused_kernel, out_shape=[jax.ShapeDtypeStruct((3 * n2, 2 *...  79.5 us
    pallas_call x1, Pallas kernels, local(): pl.pallas_call(last_kernel, out_shape=[jax.ShapeDtypeStruct(rhs.shape, f3...  2.15 us

profile of v7, /device:TPU:1, one launch (start us, length us, event | category | flops | bytes accessed | tf_op | source)
XLA Modules:
  0.0 82.3 jit_solution(10049136986045358425)
XLA Ops:
  0.6 79.5 %fused.1 = (f32[192,128]{1,0:T(8,128)}, f32[192,512]{1,0:T(8,128)}) custom-call(s32[11,512]{1,0:T(8,128)} %bitcast.1, s32[512]{0:T(512)} %load_in.1, s32[512]{0:T(512)} %moved_in.1, f32[4,64,128]{2,1,0:T(8,128)} %rhs.1, f32[4,128,128]{2,1,0:T(8,128)} %diag_in.1, f32[4,11,128,128]{3,2,1,0:T(8,128)} %off_in.1, f32[2,4,128,128]{3,2,1,0:T(8,128)} %coup_in.1), custom_call_target="tpu_custom_call" | custom-call | tf_op jit(solution)/shard_map/fused/pallas_call | solution.py:726
  80.2 2.2 %last.1 = (f32[4,64,128]{2,1,0:T(8,128)}, f32[4,64,128]{2,1,0:T(8,128)}) custom-call(f32[192,128]{1,0:T(8,128)} %get-tuple-element.4.weights, f32[192,512]{1,0:T(8,128)} %get-tuple-element.5.basis), custom_call_target="tpu_custom_call" | custom-call | tf_op jit(solution)/shard_map/last/pallas_call | solution.py:740

commit v8 on v7

--- a/solution.py
+++ b/solution.py
@@ -24,6 +24,7 @@
         self.z = b // (2 * RING)
         self.send, self.recv = send, recv
         self.count = 0
+        self.arrivals = 0
         self.pending = []
 
     def device(self, dx=0, dy=0, dz=0, partner=False):
@@ -32,35 +33,41 @@
         z = lax.rem(self.z + dz, RING)
         return (lax.rem(self.g + dx, RING), (z * RING + y) * 2 + c)
 
-    def copy(self, src, dst, device):
-        i = self.count
+    def slot(self):
         self.count += 1
+        return self.count - 1
+
+    def sent(self, ref):
+        i = self.slot()
+        self.pending.append((i, ref))
+        return i
+
+    def copy(self, src, dst, device, out, into=None):
         d = pltpu.make_async_remote_copy(
             src_ref=src,
             dst_ref=dst,
-            send_sem=self.send.at[i],
-            recv_sem=self.recv.at[i],
+            send_sem=self.send.at[out],
+            recv_sem=self.recv.at[self.arrival() if into is None else into],
             device_id=device,
             device_id_type=MESH,
         )
         d.start()
-        self.pending.append(d)
         return d
 
+    def arrival(self):
+        self.arrivals += 1
+        return self.arrivals - 1
+
+    def arrived(self, ref, into):
+        pltpu.make_async_copy(ref, ref, self.recv.at[into]).wait()
+
     def drain(self):
-        for d in self.pending:
-            d.wait_send()
+        for i, ref in self.pending:
+            pltpu.make_async_copy(ref, ref, self.send.at[i]).wait()
 
 
 def plus(a, k):
     return lax.rem(a + k, RING)
-
-
-def greet(net, devices):
-    barrier = pltpu.get_barrier_semaphore()
-    for d in devices:
-        pl.semaphore_signal(barrier, inc=1, device_id=d, device_id_type=MESH)
-    pl.semaphore_wait(barrier, len(devices))
 
 
 def gather_steps(net, j, u, panel, local_sem):
@@ -80,29 +87,32 @@
     mine = unit(f0, s0)
     own = pltpu.make_async_copy(u.at[j], mine, local_sem)
     own.start()
-    near = [net.copy(u.at[j], mine, to(k, 0)) for k in (1, 3)]
-    ups = [net.copy(u.at[j], mine, to(0, 1))]
-    downs = [net.copy(u.at[j], mine, to(0, 3))]
-    far = net.copy(u.at[j], mine, to(2, 0))
+    out = net.sent(panel.at[0, 0, pl.ds(0, 3)])
+    out_half = net.sent(panel.at[0, 0, 0, pl.ds(0, 3)])
+    out_swap = net.sent(panel.at[0, 0])
+    into_half, into_swap = net.arrival(), net.arrival()
+    near = [net.copy(u.at[j], mine, to(k, 0), out) for k in (1, 3)]
+    ups = [net.copy(u.at[j], mine, to(0, 1), out)]
+    downs = [net.copy(u.at[j], mine, to(0, 3), out)]
+    far = net.copy(u.at[j], mine, to(2, 0), out)
     lo, hi = pl.ds(0, 2), pl.ds(2, 2)
     order = [f0, plus(f0, 3), plus(f0, 1), plus(f0, 2)]
-    halves = []
 
     def pass_on(p):
         piece = unit(order[p], s0)
-        ups.append(net.copy(piece, piece, to(0, 1)))
-        downs.append(net.copy(piece, piece, to(0, 3)))
+        ups.append(net.copy(piece, piece, to(0, 1), out))
+        downs.append(net.copy(piece, piece, to(0, 3), out))
 
     def forward(p):
         ups[p].wait_recv()
         piece = unit(order[p], plus(s0, 3)).at[lo]
-        halves.append(net.copy(piece, piece, to(0, 1)))
+        net.copy(piece, piece, to(0, 1), out_half, into_half)
         downs[p].wait_recv()
         piece = unit(order[p], plus(s0, 1)).at[hi]
-        halves.append(net.copy(piece, piece, to(0, 3)))
+        net.copy(piece, piece, to(0, 3), out_half, into_half)
 
     def swap(k):
-        return net.copy(column(plus(s0, k)), column(plus(s0, k)), partner)
+        net.copy(column(plus(s0, k)), column(plus(s0, k)), partner, out_swap, into_swap)
 
     for p in (1, 2):
         yield
@@ -114,26 +124,24 @@
     far.wait_recv()
     pass_on(3)
     piece = unit(order[3], s0)
-    last = net.copy(piece, piece, to(0, 2))
+    last = net.copy(piece, piece, to(0, 2), out)
     own.wait()
-    swapped = [swap(0)]
+    swap(0)
     for p in (1, 2):
         yield
         forward(p)
     yield
     ups[3].wait_recv()
-    swapped.append(swap(3))
+    swap(3)
     yield
     downs[3].wait_recv()
-    swapped.append(swap(1))
-    yield
-    for d in halves:
-        d.wait_recv()
+    swap(1)
+    yield
+    net.arrived(panel.at[c, j, 0, pl.ds(0, 3)], into_half)
     last.wait_recv()
-    swapped.append(swap(2))
-    for d in swapped:
-        yield
-        d.wait_recv()
+    swap(2)
+    yield
+    net.arrived(panel.at[1 - c, j], into_swap)
 
 
 def scatter_steps(net, j, owed, stage, r, t0, t1, t2, t3):
@@ -152,8 +160,14 @@
     order = [2, 1, 3, 0]
     rows = {k: plus(f0, k) for k in range(RING)}
     first = {}
+    out_first = net.sent(stage.at[0])
+    out = net.sent(stage.at[0, pl.ds(0, 3)])
+    out_last = net.sent(t3.at[0])
+    into = {i: net.arrival() for i in order}
+    into2 = {i: net.arrival() for i in order}
+    into3 = net.arrival()
     for k in order:
-        first[k] = net.copy(column(stage, k), column(t0, k), partner)
+        first[k] = net.copy(column(stage, k), column(t0, k), partner, out_first)
         if k == 2:
             yield
     cols = {k: column(r, k) for k in range(RING)}
@@ -166,8 +180,10 @@
     yield
     first[2].wait_recv()
     start(2)
-    ups = {i: net.copy(cols[2].at[rows[i], lo], t1.at[j, 0, rows[i]], to(0, 1)) for i in order}
-    downs = {i: net.copy(cols[2].at[rows[i], hi], t1.at[j, 1, rows[i]], to(0, 3)) for i in order}
+    for i in order:
+        q = rows[i]
+        net.copy(cols[2].at[q, lo], t1.at[j, 0, q], to(0, 1), out, into[i])
+        net.copy(cols[2].at[q, hi], t1.at[j, 1, q], to(0, 3), out, into[i])
     yield
     first[1].wait_recv()
     start(1)
@@ -177,28 +193,23 @@
     yield
     first[0].wait_recv()
     start(0)
-    ups2, downs2 = {}, {}
     for i in order:
         q = rows[i]
         yield
-        ups[i].wait_recv()
+        net.arrived(t1.at[j, :, q], into[i])
         cols[1][q, lo] = cols[1][q, lo] + t1[j, 0, q]
-        ups2[i] = net.copy(cols[1].at[q], t2.at[j, 0, q], to(0, 1))
-        downs[i].wait_recv()
+        net.copy(cols[1].at[q], t2.at[j, 0, q], to(0, 1), out, into2[i])
         cols[3][q, hi] = cols[3][q, hi] + t1[j, 1, q]
-        downs2[i] = net.copy(cols[3].at[q], t2.at[j, 1, q], to(0, 3))
-    sent = []
+        net.copy(cols[3].at[q], t2.at[j, 1, q], to(0, 3), out, into2[i])
     for i in order:
         q = rows[i]
         yield
-        ups2[i].wait_recv()
-        downs2[i].wait_recv()
+        net.arrived(t2.at[j, :, q], into2[i])
         cols[0][q] = cols[0][q] + (t2[j, 0, q] + t2[j, 1, q])
         if i:
-            sent.append(net.copy(cols[0].at[q], t3.at[j, i - 1], to(i, 0)))
-    for d in sent:
-        yield
-        d.wait_recv()
+            net.copy(cols[0].at[q], t3.at[j, i - 1], to(i, 0), out_last, into3)
+    yield
+    net.arrived(t3.at[j], into3)
     owed[j] = (cols[0][rows[0]] + t3[j, 0]) + (t3[j, 1] + t3[j, 2])
 
 
@@ -206,36 +217,37 @@
     src = u.at[:, pl.ds(0, 2)]
     own = pltpu.make_async_copy(src, border.at[net.g], local_sem)
     own.start()
-    sent = [net.copy(src, border.at[net.g], net.device(dx=k)) for k in (1, 3, 2)]
+    others = border.at[pl.ds(0, RING - 1)]
+    out, into = net.sent(others), net.arrival()
+    for k in (1, 3, 2):
+        net.copy(src, border.at[net.g], net.device(dx=k), out, into)
     yield
     own.wait()
-    for d in sent:
-        d.wait_recv()
+    net.arrived(others, into)
 
 
 def axis_reduce_steps(net, m, out, acc, slots, halves):
     c = net.c
     rows = acc.shape[1]
     partner = net.device(partner=True)
-    d = net.copy(m.at[pl.ds((1 - c) * rows, rows)], halves, partner)
+    out_pair, out_axis = net.sent(acc.at[pl.ds(0, 2)]), net.sent(slots)
+    d = net.copy(m.at[pl.ds((1 - c) * rows, rows)], halves, partner, out_pair)
     yield
     d.wait_recv()
     acc[0] = m[pl.ds(c * rows, rows)] + halves[...]
     for t in range(3):
-        sent = []
+        into = net.arrival()
         for k in (1, 3, 2):
             step = [0, 0, 0]
             step[t] = k * (1 - c)
             step[(t + 1) % 3] = step[(t + 1) % 3] + k * c
-            sent.append(
-                net.copy(acc.at[t], slots.at[t, k - 1], net.device(step[0], step[1], step[2]))
-            )
+            to = net.device(step[0], step[1], step[2])
+            net.copy(acc.at[t], slots.at[t, k - 1], to, out_axis, into)
         yield
-        for d in sent:
-            d.wait_recv()
+        net.arrived(slots.at[t], into)
         acc[t + 1] = (acc[t] + slots[t, 0]) + (slots[t, 1] + slots[t, 2])
     out[pl.ds(c * rows, rows)] = acc[3]
-    d = net.copy(acc.at[3], out.at[pl.ds(c * rows, rows)], partner)
+    d = net.copy(acc.at[3], out.at[pl.ds(c * rows, rows)], partner, out_pair)
     yield
     d.wait_recv()
 
@@ -244,28 +256,29 @@
     c = net.c
     rows = acc.shape[1]
     partner = net.device(partner=True)
-    d = net.copy(m.at[pl.ds((1 - c) * rows, rows)], halves, partner)
+    out_pair = net.sent(acc.at[pl.ds(0, 2)])
+    out_x, out_plane = net.sent(slots), net.sent(plane_slots)
+    into_x, into_plane = net.arrival(), net.arrival()
+    d = net.copy(m.at[pl.ds((1 - c) * rows, rows)], halves, partner, out_pair)
     yield
     d.wait_recv()
     acc[0] = m[pl.ds(c * rows, rows)] + halves[...]
-    sent = [net.copy(acc.at[0], slots.at[k - 1], net.device(dx=k)) for k in (1, 3, 2)]
-    yield
-    for d in sent:
-        d.wait_recv()
+    for k in (1, 3, 2):
+        net.copy(acc.at[0], slots.at[k - 1], net.device(dx=k), out_x, into_x)
+    yield
+    net.arrived(slots, into_x)
     acc[1] = (acc[0] + slots[0]) + (slots[1] + slots[2])
-    sent = [
-        net.copy(acc.at[1], plane_slots.at[k - 1], net.device(dy=k % RING, dz=k // RING))
-        for k in FAR_FIRST
-    ]
-    yield
-    for d in sent:
-        d.wait_recv()
+    for k in FAR_FIRST:
+        to = net.device(dy=k % RING, dz=k // RING)
+        net.copy(acc.at[1], plane_slots.at[k - 1], to, out_plane, into_plane)
+    yield
+    net.arrived(plane_slots, into_plane)
     terms = [acc[1]] + [plane_slots[k] for k in range(RING * RING - 1)]
     while len(terms) > 1:
         terms = [a + b for a, b in zip(terms[::2], terms[1::2])]
     acc[2] = terms[0]
     out[pl.ds(c * rows, rows)] = terms[0]
-    d = net.copy(acc.at[2], out.at[pl.ds(c * rows, rows)], partner)
+    d = net.copy(acc.at[2], out.at[pl.ds(c * rows, rows)], partner, out_pair)
     yield
     d.wait_recv()
 
@@ -666,6 +679,7 @@
     run(*scatters)
     for s in range(ROW_COUNT):
         basis[4 * n :, s * w : (s + 1) * w] = whole(owed1, s)
+    assert net.count == send.shape[0] and net.arrivals == recv.shape[0]
     net.drain()
 
 
@@ -708,7 +722,7 @@
             vmem(half, k),
         ]
 
-    copies = 2 * (2 * 22 + 3 + 2 * 23 + 20)
+    sends, arrivals = 2 * (2 * 3 + 1 + 2 * 3) + 5, 2 * (2 * 14 + 1 + 2 * 13) + 9
     scratch = (
         [vmem(2, rows, n, w), vmem(2, rows, n, w), vmem(*diag.shape), vmem(*off.shape), vmem(*coup.shape)]
         + [vmem(OWN + rows, 2, n, w), vmem(rows, n2, w)]
@@ -720,7 +734,7 @@
         + reduction(n, 2 * n2)
         + [pltpu.SMEM(a.shape, jnp.int32) for a in (col_index.T, load, new_slot)]
         + [pltpu.VMEM((8, PART_ROWS), jnp.int32), pltpu.SMEM((8, PART_ROWS), jnp.int32)]
-        + [pltpu.SemaphoreType.DMA((copies,))] * 2
+        + [pltpu.SemaphoreType.DMA((sends,)), pltpu.SemaphoreType.DMA((arrivals,))]
         + [pltpu.SemaphoreType.DMA((6,)), pltpu.SemaphoreType.DMA((9,))]
     )
     weights, basis = pl.pallas_call(

time: 82.5 us -> 79.4 us (0.962)
  Pallas kernels: 81.7 us -> 78.7 us
    pallas_call x1, Pallas kernels: 79.5 us -> 76.5 us  [local(): pl.pallas_call(fused_kernel, out_shape=[jax.ShapeDtypeStruct((3 * n2, 2 *...]
where the time goes in v8:
time: 79.4 us; the launch traced here: 79.3 us
  Pallas kernels  78.7 us (99%)
    pallas_call x1, Pallas kernels, local(): pl.pallas_call(fused_kernel, out_shape=[jax.ShapeDtypeStruct((3 * n2, 2 *...  76.5 us
    pallas_call x1, Pallas kernels, local(): pl.pallas_call(last_kernel, out_shape=[jax.ShapeDtypeStruct(rhs.shape, f3...  2.15 us

profile of v8, /device:TPU:1, one launch (start us, length us, event | category | flops | bytes accessed | tf_op | source)
XLA Modules:
  0.0 79.3 jit_solution(3231845013658283129)
XLA Ops:
  0.6 76.5 %fused.1 = (f32[192,128]{1,0:T(8,128)}, f32[192,512]{1,0:T(8,128)}) custom-call(s32[11,512]{1,0:T(8,128)} %bitcast.1, s32[512]{0:T(512)} %load_in.1, s32[512]{0:T(512)} %moved_in.1, f32[4,64,128]{2,1,0:T(8,128)} %rhs.1, f32[4,128,128]{2,1,0:T(8,128)} %diag_in.1, f32[4,11,128,128]{3,2,1,0:T(8,128)} %off_in.1, f32[2,4,128,128]{3,2,1,0:T(8,128)} %coup_in.1), custom_call_target="tpu_custom_call" | custom-call | tf_op jit(solution)/shard_map/fused/pallas_call | solution.py:740
  77.1 2.2 %last.1 = (f32[4,64,128]{2,1,0:T(8,128)}, f32[4,64,128]{2,1,0:T(8,128)}) custom-call(f32[192,128]{1,0:T(8,128)} %get-tuple-element.4.weights, f32[192,512]{1,0:T(8,128)} %get-tuple-element.5.basis), custom_call_target="tpu_custom_call" | custom-call | tf_op jit(solution)/shard_map/last/pallas_call | solution.py:754

commit v9 on v8

--- a/solution.py
+++ b/solution.py
@@ -665,8 +665,9 @@
     advance(scatters, 4)
     for s in range(ROW_COUNT):
         basis[2 * n : 4 * n, s * w : (s + 1) * w] = panel_row(panel1, mine[s])
+    advance([sums])
     known = finish(solving)[0]
-    advance(scatters, 1)
+    advance(scatters, 2)
     run(sums)
     n3 = jnp.concatenate([total3[:, : 2 * n], total3[:, 2 * n :]], axis=0)
     solving = both(last_coefficients(known, n3))

time: 79.4 us -> 78.6 us (0.990)
  Pallas kernels: 78.7 us -> 77.8 us
    pallas_call x1, Pallas kernels: 76.5 us -> 75.7 us  [local(): pl.pallas_call(fused_kernel, out_shape=[jax.ShapeDtypeStruct((3 * n2, 2 *...]
where the time goes in v9:
time: 78.6 us; the launch traced here: 78.5 us
  Pallas kernels  77.8 us (99%)
    pallas_call x1, Pallas kernels, local(): pl.pallas_call(fused_kernel, out_shape=[jax.ShapeDtypeStruct((3 * n2, 2 *...  75.7 us
    pallas_call x1, Pallas kernels, local(): pl.pallas_call(last_kernel, out_shape=[jax.ShapeDtypeStruct(rhs.shape, f3...  2.16 us

profile of v9, /device:TPU:1, one launch (start us, length us, event | category | flops | bytes accessed | tf_op | source)
XLA Modules:
  0.0 78.5 jit_solution(13562918863786207287)
XLA Ops:
  0.6 75.7 %fused.1 = (f32[192,128]{1,0:T(8,128)}, f32[192,512]{1,0:T(8,128)}) custom-call(s32[11,512]{1,0:T(8,128)} %bitcast.1, s32[512]{0:T(512)} %load_in.1, s32[512]{0:T(512)} %moved_in.1, f32[4,64,128]{2,1,0:T(8,128)} %rhs.1, f32[4,128,128]{2,1,0:T(8,128)} %diag_in.1, f32[4,11,128,128]{3,2,1,0:T(8,128)} %off_in.1, f32[2,4,128,128]{3,2,1,0:T(8,128)} %coup_in.1), custom_call_target="tpu_custom_call" | custom-call | tf_op jit(solution)/shard_map/fused/pallas_call | solution.py:741
  76.3 2.2 %last.1 = (f32[4,64,128]{2,1,0:T(8,128)}, f32[4,64,128]{2,1,0:T(8,128)}) custom-call(f32[192,128]{1,0:T(8,128)} %get-tuple-element.4.weights, f32[192,512]{1,0:T(8,128)} %get-tuple-element.5.basis), custom_call_target="tpu_custom_call" | custom-call | tf_op jit(solution)/shard_map/last/pallas_call | solution.py:755
